TPU v7x, 32 devices: a whole 2x2x4 slice. The times are simulated.
32 devices in a mesh: dp: 4 (over y, x), fsdp: 8 (over z, core).
Axes of the slice: x: 2, y: 2, z: 4, core: 2. Of those that a mesh axis runs over, the one named last changes fastest.
Arguments:
- tokens_in: bfloat16 [32, 1024, 768], P(('dp', 'fsdp')), may hold values from -6 to 6
- ln1_gain: bfloat16 [768], P('fsdp'), may hold values from 0.5 to 1.5
- ln1_bias: bfloat16 [768], P('fsdp'), may hold values from -3 to 3
- ln2_gain: bfloat16 [768], P('fsdp'), may hold values from 0.5 to 1.5
- ln2_bias: bfloat16 [768], P('fsdp'), may hold values from -3 to 3
- qkv_weight: bfloat16 [768, 2304], P('fsdp'), may hold values from -0.21875 to 0.21875
- qkv_bias: bfloat16 [2304], P('fsdp'), may hold values from -2 to 2
- out_weight: bfloat16 [768, 768], P('fsdp'), may hold values from -0.625 to 0.625
- out_bias: bfloat16 [768], P('fsdp'), may hold values from -2 to 2
- up_weight: bfloat16 [768, 3072], P('fsdp'), may hold values from -0.21875 to 0.21875
- up_bias: bfloat16 [3072], P('fsdp'), may hold values from -2 to 2
- down_weight: bfloat16 [3072, 768], P('fsdp'), may hold values from -0.15625 to 0.15625
- down_bias: bfloat16 [768], P('fsdp'), may hold values from -2 to 2
- cotangent: bfloat16 [32, 1024, 768], P(('dp', 'fsdp')), may hold values from -6 to 6
- lengths: int32 [32], P(('dp', 'fsdp')), may hold values from 128 to 1024, as said below
- assignment: int32 [32], P(('dp', 'fsdp')), may hold values from 0 to 31, each once
- clip_bound: int32 [1], replicated, may hold values from 6 to 10
Outputs:
- mixed: bfloat16 [32, 1024, 768], P(('dp', 'fsdp'))
- tokens_grad: bfloat16 [32, 1024, 768], P(('dp', 'fsdp'))
- clip_scale: float32 [32], replicated
- ln1_gain_grad: float32 [768], P('fsdp')
- ln1_bias_grad: float32 [768], P('fsdp')
- ln2_gain_grad: float32 [768], P('fsdp')
- ln2_bias_grad: float32 [768], P('fsdp')
- qkv_weight_grad: float32 [768, 2304], P('fsdp')
- qkv_bias_grad: float32 [2304], P('fsdp')
- out_weight_grad: float32 [768, 768], P('fsdp')
- out_bias_grad: float32 [768], P('fsdp')
- up_weight_grad: float32 [768, 3072], P('fsdp')
- up_bias_grad: float32 [3072], P('fsdp')
- down_weight_grad: float32 [3072, 768], P('fsdp')
- down_bias_grad: float32 [768], P('fsdp')
Inputs may be any that keep to these rules, and one draw needn't show every extreme that they name: `lengths`: every slot's length lies between 128 and 1024; both ends occur in every draw. `assignment`: each example number occurs once.
All inputs are finite; a program needn't handle non-finite values.
Results may differ from a plain program's by a relative error of at most 0.0095.
Values may be sent and summed in bfloat16 or wider, within the bound.
No kernel may reach another device: no remote copies, remote signals or barrier semaphores. Data moves between devices by JAX's collectives and lax.ppermute only.
A program may use at most 256 MiB of HBM per device.

v0:
```python
import functools
import math

import jax
import jax.numpy as jnp
from jax import lax
from jax.experimental import pallas as pl
from jax.experimental.pallas import tpu as pltpu
from jax.sharding import PartitionSpec as P


HEAD_DIM = 64
ROT_DIM = 16
LANES = 128
f32 = jnp.float32
bf16 = jnp.bfloat16


def nn(left, right):
    return lax.dot_general(left, right, (((1,), (0,)), ((), ())), preferred_element_type=f32)


def nt(left, right):
    return lax.dot_general(left, right, (((1,), (1,)), ((), ())), preferred_element_type=f32)


def tn(left, right):
    return lax.dot_general(left, right, (((0,), (0,)), ((), ())), preferred_element_type=f32)


def fold(row):
    total = row[:, 0:LANES]
    for start in range(LANES, row.shape[1], LANES):
        total = total + row[:, start : start + LANES]
    return total


def fixed(shape):
    return pl.BlockSpec(shape, lambda *_: (0,) * len(shape), pipeline_mode=pl.Buffered(1))


def params(mib=60):
    return pltpu.CompilerParams(vmem_limit_bytes=mib * 2**20)


def z_of(at, coords):
    return ((at % 2) * 2 + at // 2) ^ coords[3]


def z_at(z, coords):
    rel = z ^ coords[3]
    return (rel % 2) * 2 + rel // 2


def put_rows(scr, x, row, coords, refs, extra=(), tiles=None):
    half = scr.shape[0] // 16
    x_rel = x ^ coords[1]

    def put(c, near, pair):
        def one(z):
            shard = z_of(z, coords) * 2 + (c ^ coords[0])
            for y in range(2):
                start = pl.multiple_of((2 * shard + (y ^ coords[2])) * half, half)
                ref, s2 = (pair[0], y) if near else (pair[y], x_rel)
                for t, tile in enumerate(tiles or range(scr.shape[1] // LANES)):
                    to = pl.ds(pl.multiple_of(row + t * half, half), half)
                    ref[(s2, z) + extra + (to, slice(None))] = scr[
                        pl.ds(start, half), tile * LANES : (tile + 1) * LANES
                    ]

        if extra:
            for z in range(4):
                one(z)
        else:
            pl.loop(0, 4)(one)

    for c in range(2):
        kept, sent = refs[2 * c : 2 * c + 2]
        near = coords[0] == c
        pl.when(near & (x_rel == 0))(functools.partial(put, c, True, (kept,)))
        pl.when(near & (x_rel == 1))(functools.partial(put, c, True, (sent,)))
        pl.when(jnp.logical_not(near))(functools.partial(put, c, False, (kept, sent)))


def prepare_kernel(
    len_ref, x_ref, cot_ref, ln_ref, h1_ref, h2_ref, h1t_ref, h2t_ref, cotm_ref, cott_ref
):
    x = x_ref[...].astype(f32)
    centred = x - jnp.mean(x, -1, keepdims=True)
    normed = centred * lax.rsqrt(jnp.mean(centred * centred, -1, keepdims=True) + 1e-05)
    h1 = (normed * ln_ref[0:1, :] + ln_ref[1:2, :]).astype(bf16)
    h2 = (normed * ln_ref[2:3, :] + ln_ref[3:4, :]).astype(bf16)
    row = pl.program_id(0) * x.shape[0] + lax.broadcasted_iota(jnp.int32, (x.shape[0], 1), 0)
    cot = jnp.where(row < len_ref[0], cot_ref[...], jnp.zeros_like(cot_ref[...]))
    h1_ref[...] = h1
    h2_ref[...] = h2
    cotm_ref[...] = cot
    h1t_ref[...] = h1.T
    h2t_ref[...] = h2.T
    cott_ref[...] = cot.T


def prepare(lengths, x, cot, ln, rows=256):
    count, width = x.shape
    block = pl.BlockSpec((rows, width), lambda i, n: (i, 0))
    turned = pl.BlockSpec((width, rows), lambda i, n: (0, i))
    straight = jax.ShapeDtypeStruct((count, width), bf16)
    across = jax.ShapeDtypeStruct((width, count), bf16)
    return pl.pallas_call(
        prepare_kernel,
        grid_spec=pltpu.PrefetchScalarGridSpec(
            num_scalar_prefetch=1,
            grid=(count // rows,),
            in_specs=[block, block, fixed(ln.shape)],
            out_specs=[block, block, turned, turned, block, turned],
        ),
        out_shape=[straight, straight, across, across, straight, across],
        compiler_params=params(),
        cost_estimate=pl.CostEstimate(
            flops=20 * count * width, bytes_accessed=12 * 2**20, transcendentals=0
        ),
        name="prepare",
    )(lengths, x, cot, ln)


def cut_kernel(co_ref, qkv_ref, out_ref, up_ref, down_ref, in_ref, in0_ref, ff_ref, ff0_ref):
    half = qkv_ref.shape[0] // 2
    unit = LANES // 2
    for y in range(2):
        for x in range(2):
            at = (y ^ co_ref[2]) * 2 + (x ^ co_ref[1])

            def fill(inner, feeds):
                row = 0
                for ref in (qkv_ref, out_ref):
                    tiles = ref.shape[1] // 2 // LANES
                    for t in range(tiles):
                        lanes = slice((x * tiles + t) * LANES, (x * tiles + t + 1) * LANES)
                        inner[row : row + half, :] = ref[y * half : (y + 1) * half, lanes]
                        row += half
                for sub in range(3):
                    for z in range(2):
                        for c in range(2):
                            tile = (2 * (2 * x + z) + c) * 3 + sub
                            row = ((3 * z + sub) * 2 + c) * half
                            feeds[0, row : row + half, :] = up_ref[
                                y * half : (y + 1) * half, tile * LANES : (tile + 1) * LANES
                            ]
                    for t in range(3):
                        row = (3 * sub + t) * unit
                        start = sub * LANES + y * unit
                        lanes = slice((3 * x + t) * LANES, (3 * x + t + 1) * LANES)
                        feeds[1, row : row + unit, :] = down_ref[start : start + unit, lanes]

            fill(in_ref.at[at], ff_ref.at[at])
            pl.when(at == 0)(lambda: fill(in0_ref, ff0_ref))


def cut(coords, qkv, out, up, down):
    whole = lambda s: pl.BlockSpec(s, lambda i, co: (0,) * len(s))
    rows = qkv.shape[0] // 2 * ((qkv.shape[1] + out.shape[1]) // 2 // LANES)
    shapes = [(4, rows, LANES), (rows, LANES), (4, 2, rows, LANES), (2, rows, LANES)]
    return pl.pallas_call(
        cut_kernel,
        grid_spec=pltpu.PrefetchScalarGridSpec(
            num_scalar_prefetch=1,
            grid=(1,),
            in_specs=[whole(entry.shape) for entry in (qkv, out, up, down)],
            out_specs=[whole(shape) for shape in shapes],
        ),
        out_shape=[jax.ShapeDtypeStruct(shape, bf16) for shape in shapes],
        compiler_params=params(),
        name="cut",
    )(coords, qkv, out, up, down)


def piece_of(parts, q, k):
    own, line, side, up, diagonal = parts
    if isinstance(k, int) and k == 0:
        return own.at[q]
    return (line, side, up, diagonal)[q].at[k - 1]


def qkv_kernel(
    co_ref, h1_ref, b_ref, c_ref, sa_ref, sb_ref,
    p0, p1, p2, p3, p4, r0, r1, r2, r3, r4, o_ref, w_ref, wo_ref,
):
    width = h1_ref.shape[1]
    half = width // 16

    @pl.when(pl.program_id(0) == 0)
    def _():
        for other, parts in enumerate(((p0, p1, p2, p3, p4), (r0, r1, r2, r3, r4))):


            def fill(k, other=other, parts=parts):
                for q in range(4):
                    ref = piece_of(parts, q, k)
                    shard = (k ^ co_ref[3]) * 2 + (other ^ co_ref[0])
                    row = pl.multiple_of(shard * 2 * half + ((q // 2) ^ co_ref[2]) * half, half)
                    x = (q % 2) ^ co_ref[1]
                    start = 0
                    for target in (w_ref, wo_ref):
                        tiles = target.shape[1] // 2 // LANES
                        for t in range(tiles):
                            lane = pl.multiple_of((x * tiles + t) * LANES, LANES)
                            target[pl.ds(row, half), pl.ds(lane, LANES)] = ref[start : start + half, :]
                            start += half

            fill(0)
            pl.loop(1, 4)(fill)

    h1 = h1_ref[...]
    cosine, ahead, behind = c_ref[...], sa_ref[...], sb_ref[...]
    low = lax.broadcasted_iota(jnp.int32, (1, LANES), 1) < HEAD_DIM

    def turn(y):
        return y * cosine - pltpu.roll(y * ahead, LANES - 8, 1) - pltpu.roll(y * behind, 8, 1)

    for part in range(3):
        cols = slice(part * width, (part + 1) * width)
        y = nn(h1, w_ref[:, cols]) + b_ref[:, cols]
        for pair in range(2):
            base = pair * 3 * LANES
            t0 = y[:, base : base + LANES]
            t1 = y[:, base + LANES : base + 2 * LANES]
            t2 = y[:, base + 2 * LANES : base + 3 * LANES]
            queries = turn(jnp.where(low, t0, t1)) * (HEAD_DIM**-0.5)
            keys = turn(pltpu.roll(jnp.where(low, t2, t0), HEAD_DIM, 1))
            at = (2 * part + pair) * LANES
            o_ref[:, at : at + LANES] = queries.astype(bf16)
            o_ref[:, width + at : width + at + LANES] = keys.astype(bf16)
            o_ref[:, 2 * width + at : 2 * width + at + LANES] = jnp.where(low, t1, t2).astype(bf16)


def qkv_forward(coords, h1, bias, tables, pieces, rows=256):
    count, width = h1.shape
    block = lambda n: pl.BlockSpec((rows, n), lambda i, co: (i, 0))
    whole = lambda s: pl.BlockSpec(s, lambda i, co: (0,) * len(s))
    arrays = [entry for part in pieces for entry in part]
    return pl.pallas_call(
        qkv_kernel,
        grid_spec=pltpu.PrefetchScalarGridSpec(
            num_scalar_prefetch=1,
            grid=(count // rows,),
            in_specs=[block(width), fixed(bias.shape)]
            + [block(LANES)] * 3
            + [fixed(entry.shape) for entry in arrays],
            out_specs=[block(3 * width), whole((width, 3 * width)), whole((width, width))],
        ),
        out_shape=[
            jax.ShapeDtypeStruct((count, 3 * width), bf16),
            jax.ShapeDtypeStruct((width, 3 * width), bf16),
            jax.ShapeDtypeStruct((width, width), bf16),
        ],
        compiler_params=params(),
        cost_estimate=pl.CostEstimate(
            flops=6 * count * width * width, bytes_accessed=18 * 2**20, transcendentals=0
        ),
        name="qkv_forward",
    )(coords, h1, bias, *tables[:3], *arrays)


def rotary_tables(count):
    half = ROT_DIM // 2
    lane = lax.broadcasted_iota(jnp.int32, (1, LANES), 1) % HEAD_DIM
    row = lax.broadcasted_iota(jnp.int32, (half, 1), 0)
    inverse = lambda at: 10000.0 ** (-(2 * (at % half)).astype(f32) / ROT_DIM)
    angles = lax.broadcasted_iota(jnp.int32, (count, 1), 0).astype(f32) * inverse(lane)
    turned = lax.broadcasted_iota(jnp.int32, (1, count), 1).astype(f32) * inverse(row)
    cosine, sine = jnp.cos(angles), jnp.sin(angles)
    return (
        jnp.where(lane < ROT_DIM, cosine, 1.0),
        jnp.where((lane >= half) & (lane < ROT_DIM), sine, 0.0),
        jnp.where(lane < half, -sine, 0.0),
        jnp.cos(turned),
        jnp.sin(turned),
    )


def attention_kernel(
    q_ref, k_ref, v_ref, cot_ref, w_ref, c_ref, sa_ref, sb_ref, ct_ref, st_ref,
    a_ref, dqkv_ref, da_ref, qt_ref, dat_ref, dq, dkt, dvt, *, rows,
):
    count = q_ref.shape[0]
    blocks = count // rows
    low = lax.broadcasted_iota(jnp.int32, (1, LANES), 1) < HEAD_DIM
    causal = lax.broadcasted_iota(jnp.int32, (rows, rows), 1) <= lax.broadcasted_iota(
        jnp.int32, (rows, rows), 0
    )
    da_ref[...] = nt(cot_ref[...], w_ref[...]).astype(bf16)
    qt_ref[...] = q_ref[...].T
    dat_ref[...] = da_ref[...].T

    def products(i, h):
        here, past = slice(i * rows, (i + 1) * rows), slice(0, i * rows)
        mine = low if h == 0 else jnp.logical_not(low)
        q, da = q_ref[here, :], da_ref[here, :]
        q = jnp.where(mine, q, jnp.zeros_like(q))
        da = jnp.where(mine, da, jnp.zeros_like(da))
        s_here, d_here = nt(q, k_ref[here, :]), nt(da, v_ref[here, :])
        if not i:
            return [s_here], [d_here]
        return [s_here, nt(q, k_ref[past, :])], [d_here, nt(da, v_ref[past, :])]

    def rest(i, h, scores, grads):
        here, past = slice(i * rows, (i + 1) * rows), slice(0, i * rows)
        head = slice(HEAD_DIM * h, HEAD_DIM * (h + 1))
        spans = (here, past)[: len(scores)]
        scores = [jnp.where(causal, scores[0], -1e30)] + scores[1:]
        highest = jnp.max(scores[0], -1, keepdims=True)
        for s in scores[1:]:
            highest = jnp.maximum(highest, jnp.max(s, -1, keepdims=True))
        raised = [jnp.exp(s - highest) for s in scores]
        inverse = 1.0 / sum(jnp.sum(e, -1, keepdims=True) for e in raised)
        probs = [e * inverse for e in raised]
        row_dot = sum(jnp.sum(p * d, -1, keepdims=True) for p, d in zip(probs, grads))
        out, grad = 0.0, 0.0
        for span, p, d in zip(spans, probs, grads):
            weights = p.astype(bf16)
            ds = (p * (d - row_dot)).astype(bf16)
            out = out + nn(weights, v_ref[span, :])
            grad = grad + nn(ds, k_ref[span, :])
            dk, dv = nn(qt_ref[head, here], ds), nn(dat_ref[head, here], weights)
            if i == blocks - 1:
                dkt[head, span], dvt[head, span] = dk, dv
            else:
                dkt[head, span] += dk
                dvt[head, span] += dv
        return out, grad

    units = [(i, h) for i in reversed(range(blocks)) for h in range(2)]
    ready = products(*units[0])
    results = {}
    for at, unit in enumerate(units):
        now = ready
        if at + 1 < len(units):
            ready = products(*units[at + 1])
        results[unit] = rest(*unit, *now)
        i, h = unit
        if h == 1:
            here = slice(i * rows, (i + 1) * rows)
            first, second = results.pop((i, 0)), results.pop((i, 1))
            a_ref[here, :] = jnp.where(low, first[0], second[0]).astype(bf16)
            y = jnp.where(low, first[1], second[1]) * (HEAD_DIM**-0.5)
            dq[here, :] = (
                y * c_ref[here, :]
                + pltpu.roll(y * sa_ref[here, :], LANES - 8, 1)
                + pltpu.roll(y * sb_ref[here, :], 8, 1)
            )
    cosine, sine = ct_ref[...], st_ref[...]
    for h in range(2):
        one = slice(HEAD_DIM * h, HEAD_DIM * h + 8)
        two = slice(HEAD_DIM * h + 8, HEAD_DIM * h + 16)
        first, second = dkt[one, :], dkt[two, :]
        dkt[one, :] = first * cosine + second * sine
        dkt[two, :] = second * cosine - first * sine
    gk = dkt[...].astype(bf16).T
    gv = dvt[...].astype(bf16).T
    gq = dq[...].astype(bf16)
    gk = jnp.concatenate([gk[:, HEAD_DIM:], gk[:, :HEAD_DIM]], 1)
    dqkv_ref[:, 0:LANES] = jnp.where(low, gq, gk)
    dqkv_ref[:, LANES : 2 * LANES] = jnp.where(low, gv, gq)
    dqkv_ref[:, 2 * LANES : 3 * LANES] = jnp.where(low, gk, gv)


def attention(qkv, cot, out_weight, tables, rows=256):
    count, width = cot.shape
    pairs = width // LANES
    column = lambda offset: pl.BlockSpec((count, LANES), lambda p: (0, offset + p))
    return pl.pallas_call(
        functools.partial(attention_kernel, rows=rows),
        grid=(pairs,),
        in_specs=[column(0), column(pairs), column(2 * pairs), fixed((count, width))]
        + [pl.BlockSpec((LANES, width), lambda p: (p, 0))]
        + [fixed((count, LANES))] * 3
        + [fixed((8, count))] * 2,
        out_specs=[column(0), pl.BlockSpec((count, 3 * LANES), lambda p: (0, p))],
        out_shape=[
            jax.ShapeDtypeStruct((count, width), bf16),
            jax.ShapeDtypeStruct((count, 3 * width), bf16),
        ],
        scratch_shapes=[
            pltpu.VMEM((count, LANES), bf16),
            pltpu.VMEM((LANES, count), bf16),
            pltpu.VMEM((LANES, count), bf16),
            pltpu.VMEM((count, LANES), f32),
            pltpu.VMEM((LANES, count), f32),
            pltpu.VMEM((LANES, count), f32),
        ],
        compiler_params=params(),
        cost_estimate=pl.CostEstimate(
            flops=30 * 10**9, bytes_accessed=20 * 2**20, transcendentals=8 * 10**6
        ),
        name="attention",
    )(qkv, qkv, qkv, cot, out_weight, *tables)


def feed_kernel(
    co_ref, h2_ref, h2t_ref, cot_ref, cott_ref, upb_ref, acc0_ref, before_ref,
    p0, p1, p2, p3, p4, r0, r1, r2, r3, r4, e0, e1, e2, e3, e4, f0, f1, f2, f3, f4,
    mix_ref, k0_ref, s0_ref, k1_ref, s1_ref, ubg_ref, dh2_ref, sq_ref, up_ref, down_ref, us, ds, g_ref, du_ref, *acc,
):
    j = pl.program_id(0)
    side, sub = j % 2, j // 2
    rows = up_ref.shape[0] // 16
    unit = LANES // 2
    x_here = side ^ co_ref[1]
    acc_ref = acc[0] if acc else mix_ref

    @pl.when(j == 0)
    def _():
        acc_ref[...] = acc0_ref[...]
        dh2_ref[...] = jnp.zeros_like(dh2_ref) if before_ref is None else before_ref[...]
        sq_ref[...] = jnp.zeros_like(sq_ref)

    def fill_up(x, k):
        for other, parts in enumerate(((p0, p1, p2, p3, p4), (r0, r1, r2, r3, r4))):
            for y in range(2):
                ref = piece_of(parts, 2 * y + x, k)
                shard = (k ^ co_ref[3]) * 2 + (other ^ co_ref[0])
                row = pl.multiple_of((2 * shard + (y ^ co_ref[2])) * rows, rows)
                for t in range(4):
                    up_ref[pl.ds(row, rows), t * LANES : (t + 1) * LANES] = ref[
                        0, t // 2, 0, (t % 2) * rows : (t % 2 + 1) * rows, :
                    ]

    for x in range(2):

        @pl.when(x_here == x)
        def _(x=x):
            fill_up(x, 0)
            pl.loop(1, 4)(lambda k: fill_up(x, k))


    def fill_down(k):
        z = k ^ co_ref[3]
        for other, parts in enumerate(((e0, e1, e2, e3, e4), (f0, f1, f2, f3, f4))):
            first = (2 * (z % 2) + (other ^ co_ref[0])) * LANES
            for q in range(4):
                ref = piece_of(parts, q, k)
                row = pl.multiple_of(first + ((q // 2) ^ co_ref[2]) * unit, unit)
                for t in range(3):
                    lane = pl.multiple_of((((q % 2) ^ co_ref[1]) * 3 + t) * LANES, LANES)
                    down_ref[pl.ds(row, unit), pl.ds(lane, LANES)] = ref[0, t * unit : (t + 1) * unit, :]

    pl.when(co_ref[3] // 2 == side)(lambda: fill_down(0))

    @pl.loop(1, 4)
    def _(k):
        pl.when((k ^ co_ref[3]) // 2 == side)(lambda: fill_down(k))


    part = g_ref.shape[0] // 2
    ubg_ref[...] = jnp.zeros_like(ubg_ref)

    @pl.loop(0, 2)
    def _(at):
        here = pl.ds(pl.multiple_of(at * part, part), part)
        u = nn(h2_ref[here, :], up_ref[...]) + upb_ref[...]
        act = nt(cot_ref[here, :], down_ref[...])
        cdf = 0.5 * (1.0 + lax.erf(u * math.sqrt(0.5)))
        pdf = jnp.exp(-0.5 * u * u) * (1.0 / math.sqrt(2.0 * math.pi))
        g = (u * cdf).astype(bf16)
        du = (act * (cdf + u * pdf)).astype(bf16)
        g_ref[here, :] = g
        du_ref[here, :] = du
        ubg_ref[...] += jnp.sum(du.astype(f32), 0, keepdims=True)
        acc_ref[here, :] += nn(g, down_ref[...])
        dh2_ref[here, :] += nt(du, up_ref[...])

    bias_grad = ubg_ref[...]
    up_grad = nn(h2t_ref[...], du_ref[...])
    us[...] = up_grad.astype(bf16)
    down_grad = nn(cott_ref[...], g_ref[...])
    ds[...] = down_grad.astype(bf16)
    refs = (k0_ref, s0_ref, k1_ref, s1_ref)
    for x in range(2):
        put_rows(us, x, (2 * sub + side) * 2 * rows, co_ref, refs, tiles=(2 * x, 2 * x + 1))
    first = pl.num_programs(0) * 2 * rows

    def put_down(c, pair):
        for z in range(2):
            tile = 2 * z + c
            for x in range(2):
                for y in range(2):
                    ref, s2 = (pair[x], y) if c == 0 else (pair[y], x)
                    for t in range(3):
                        start = ((x ^ co_ref[1]) * 3 + t) * LANES + (y ^ co_ref[2]) * unit
                        to = pl.ds(pl.multiple_of(first + (3 * sub + t) * unit, unit), unit)
                        ref[s2, z_at(2 * side + z, co_ref), to, :] = ds[
                            pl.ds(pl.multiple_of(start, unit), unit), tile * LANES : (tile + 1) * LANES
                        ]

    for c in range(2):
        pl.when(co_ref[0] == c)(functools.partial(put_down, c, refs[:2]))
        pl.when(co_ref[0] != c)(functools.partial(put_down, c, refs[2:]))
    sq_ref[0:1, :] += fold(
        jnp.sum(up_grad * up_grad + down_grad * down_grad, 0, keepdims=True)
        + bias_grad * bias_grad
    )
    if not acc:
        return

    @pl.when(j == pl.num_programs(0) - 1)
    def _():
        row = lax.broadcasted_iota(jnp.int32, (mix_ref.shape[0], 1), 0)
        mix_ref[...] = jnp.where(row < co_ref[4], acc_ref[...], 0.0).astype(bf16)


def feed(coords, h2, h2t, cot, cott, up_bias, acc, before, pieces, first, subs):
    count, width = h2.shape
    tile = 4 * LANES
    hidden = 2 * subs * tile
    rows = width // 16
    last = before is not None
    piece = jax.ShapeDtypeStruct((2, 4, subs * (4 * rows + 3 * LANES // 2), LANES), bf16)
    up_pieces = [
        [entry.reshape(*entry.shape[:2], 2, 3, 2 * rows, LANES) for entry in part] for part in pieces
    ]
    up_spec = lambda n: pl.BlockSpec(
        (n, 1, 2, 1, 2 * rows, LANES), lambda j, co: (0, 0, 0, first + j // 2, 0, 0)
    )
    down_spec = lambda n: pl.BlockSpec(
        (n, 1, 3 * LANES // 2, LANES), lambda j, co: (0, 1, first + j // 2, 0)
    )
    up_parts = [up_spec(4)] + [up_spec(3)] * 4
    down_parts = [down_spec(4)] + [down_spec(3)] * 4
    up_arrays = [entry for part in up_pieces for entry in part]
    arrays = [entry for part in pieces for entry in part]
    whole = lambda s: pl.BlockSpec(s, lambda j, co: (0,) * len(s))
    start = [before] if last else []
    kernel = feed_kernel
    if not last:
        kernel = lambda *refs: feed_kernel(*refs[:7], None, *refs[7:])
    return pl.pallas_call(
        kernel,
        grid_spec=pltpu.PrefetchScalarGridSpec(
            num_scalar_prefetch=1,
            grid=(2 * subs,),
            in_specs=[
                fixed((count, width)),
                fixed((width, count)),
                fixed((count, width)),
                fixed((width, count)),
                pl.BlockSpec((1, tile), lambda j, co: (0, 2 * first + j)),
                fixed((count, width)),
            ]
            + [fixed((count, width))] * len(start)
            + up_parts * 2
            + down_parts * 2,
            out_specs=[whole((count, width))]
            + [whole(piece.shape)] * 4
            + [
                pl.BlockSpec((1, tile), lambda j, co: (0, j)),
                whole((count, width)),
                whole((8, LANES)),
            ],
            scratch_shapes=[
                pltpu.VMEM((width, tile), bf16),
                pltpu.VMEM((tile, width), bf16),
                pltpu.VMEM((width, tile), bf16),
                pltpu.VMEM((width, tile), bf16),
                pltpu.VMEM((count, tile), bf16),
                pltpu.VMEM((count, tile), bf16),
            ]
            + [pltpu.VMEM((count, width), f32)] * len(start),
        ),
        out_shape=[jax.ShapeDtypeStruct((count, width), bf16 if last else f32)]
        + [piece] * 4
        + [
            jax.ShapeDtypeStruct((1, hidden), f32),
            jax.ShapeDtypeStruct((count, width), f32),
            jax.ShapeDtypeStruct((8, LANES), f32),
        ],
        compiler_params=params(),
        cost_estimate=pl.CostEstimate(
            flops=12 * count * width * hidden,
            bytes_accessed=12 * subs * 2**20,
            transcendentals=2 * count * hidden,
        ),
        name="feed",
    )(coords, h2, h2t, cot, cott, up_bias, acc, *start, *up_arrays, *arrays)


def inner_kernel(
    co_ref, h1t_ref, dqkv_ref, w_ref, heads_ref, cot_ref, x_ref, wo_ref, ob_ref,
    k0_ref, s0_ref, k1_ref, s1_ref, bias_ref, cotsum_ref, dh1_ref, acc_ref, sq_ref, scr,
):
    j = pl.program_id(0)
    inner = j < pl.num_programs(0) - 1

    @pl.when(j == 0)
    def _():
        sq_ref[...] = jnp.zeros_like(sq_ref)

    @pl.when(inner)
    def _():
        right = dqkv_ref[...]
        grad = nn(h1t_ref[...], right)
        scr[...] = grad.astype(bf16)
        bias_grad = jnp.sum(right.astype(f32), 0, keepdims=True)
        bias_ref[...] = bias_grad
        part = nt(right, w_ref[...])

        @pl.when(j == 0)
        def _():
            dh1_ref[...] = part

        @pl.when(j > 0)
        def _():
            dh1_ref[...] += part

        sq_ref[0:1, :] += fold(jnp.sum(grad * grad, 0, keepdims=True) + bias_grad * bias_grad)

    @pl.when(jnp.logical_not(inner))
    def _():
        right = cot_ref[...]
        grad = tn(heads_ref[...], right)
        scr[...] = grad.astype(bf16)
        bias_grad = jnp.sum(right.astype(f32), 0, keepdims=True)
        cotsum_ref[...] = bias_grad
        acc_ref[...] = x_ref[...].astype(f32) + nn(heads_ref[...], wo_ref[...]) + ob_ref[...]
        sq_ref[0:1, :] += fold(jnp.sum(grad * grad, 0, keepdims=True) + 2.0 * bias_grad * bias_grad)

    half = scr.shape[1] // LANES // 2
    for x in range(2):
        tiles = range(x * half, (x + 1) * half)
        put_rows(scr, x, 0, co_ref, (k0_ref, s0_ref, k1_ref, s1_ref), (0,), tiles)


def inner_grads(coords, h1t, dqkv, weight, heads, cot, x, out_weight, out_bias):
    count, width = heads.shape
    cols = dqkv.shape[1]
    tile = width
    steps = cols // tile + 1
    inner = lambda j: jnp.minimum(j, steps - 2)
    piece = jax.ShapeDtypeStruct((2, 4, steps, tile // LANES // 2 * width // 16, LANES), bf16)
    spec = pl.BlockSpec((2, 4, 1) + piece.shape[3:], lambda j, co: (0, 0, j, 0, 0))
    outer_block = lambda r: fixed((r, tile))
    outer_out = lambda r: pl.BlockSpec((r, tile), lambda j, co: (0, 0))
    return pl.pallas_call(
        inner_kernel,
        grid_spec=pltpu.PrefetchScalarGridSpec(
            num_scalar_prefetch=1,
            grid=(steps,),
            in_specs=[
                fixed((width, count)),
                pl.BlockSpec((count, tile), lambda j, co: (0, inner(j))),
                pl.BlockSpec((width, tile), lambda j, co: (0, inner(j))),
                fixed((count, width)),
                outer_block(count),
                outer_block(count),
                outer_block(width),
                outer_block(1),
            ],
            out_specs=[spec] * 4
            + [
                pl.BlockSpec((1, tile), lambda j, co: (0, inner(j))),
                outer_out(1),
                pl.BlockSpec((count, width), lambda j, co: (0, 0)),
                outer_out(count),
                pl.BlockSpec((8, LANES), lambda j, co: (0, 0)),
            ],
            scratch_shapes=[pltpu.VMEM((width, tile), bf16)],
        ),
        out_shape=[piece] * 4
        + [
            jax.ShapeDtypeStruct((1, cols), f32),
            jax.ShapeDtypeStruct((1, width), f32),
            jax.ShapeDtypeStruct((count, width), f32),
            jax.ShapeDtypeStruct((count, width), f32),
            jax.ShapeDtypeStruct((8, LANES), f32),
        ],
        compiler_params=params(),
        cost_estimate=pl.CostEstimate(
            flops=16 * count * width * width, bytes_accessed=24 * 2**20, transcendentals=0
        ),
        name="inner_grads",
    )(coords, h1t, dqkv, weight, heads, cot, x, out_weight, out_bias)


def combine_kernel(scale_ref, co_ref, *refs, vectors):
    pieces, out_ref = refs[:4], refs[-1]
    weigh = lambda parts: sum(scale_ref[at] * part.astype(f32) for at, part in enumerate(parts)).astype(bf16)
    rows = pieces[0].shape[2]
    out_ref[0, :rows] = weigh([ref[0, 0] for ref in pieces])
    if vectors:
        owner = 2 * z_of(pl.program_id(0), co_ref) + co_ref[0]
        out_ref[0, rows:] = weigh([ref[pl.ds(owner, 1)][0] for ref in refs[4:8]])


def combine(scales, coords, s2, arrays, vectors=()):
    rows = arrays[0].shape[2]
    extra = vectors[0].shape[1] if vectors else 0
    return pl.pallas_call(
        functools.partial(combine_kernel, vectors=bool(vectors)),
        grid_spec=pltpu.PrefetchScalarGridSpec(
            num_scalar_prefetch=2,
            grid=(4,),
            in_specs=[pl.BlockSpec((1, 1, rows, LANES), lambda i, s, co: (s2, i, 0, 0))] * 4
            + [fixed(entry.shape) for entry in vectors],
            out_specs=pl.BlockSpec((1, rows + extra, LANES), lambda i, s, co: (i, 0, 0)),
        ),
        out_shape=jax.ShapeDtypeStruct((4, rows + extra, LANES), bf16),
        compiler_params=params(),
        cost_estimate=pl.CostEstimate(
            flops=10**7, bytes_accessed=40 * rows * LANES, transcendentals=0
        ),
        name="combine",
    )(scales, coords, *arrays, *vectors)


def pack_kernel(ln_ref, qkv_ref, cot_ref, ub1_ref, ub2_ref, out_ref, row_ref):
    out_ref[...] = jnp.zeros_like(out_ref)
    for f in range(8):
        to = 0
        sources = [ln_ref.at[i : i + 1] for i in range(4)] + [qkv_ref, cot_ref]
        for ref in sources:
            size = ref.shape[1] // 8
            row_ref[f : f + 1, to : to + size] = ref[:, f * size : (f + 1) * size]
            to += size
        for sub in range(3):
            ref, at = (ub1_ref, 8 * sub + f) if sub < 2 else (ub2_ref, f)
            row_ref[f : f + 1, to : to + LANES] = ref[:, at * LANES : (at + 1) * LANES]
            to += LANES
        for row in range(row_ref.shape[1] // LANES):
            out_ref[f, row : row + 1, :] = row_ref[f : f + 1, row * LANES : (row + 1) * LANES]


def pack(*arrays):
    whole = lambda s: pl.BlockSpec(s, lambda i: (0,) * len(s))
    width = (4 * arrays[0].shape[1] + sum(entry.shape[1] for entry in arrays[1:])) // 8
    rows = -(-width // LANES // 16) * 16
    return pl.pallas_call(
        pack_kernel,
        grid=(1,),
        in_specs=[whole(entry.shape) for entry in arrays],
        out_specs=whole((8, rows, LANES)),
        out_shape=jax.ShapeDtypeStruct((8, rows, LANES), f32),
        scratch_shapes=[pltpu.VMEM((8, width), f32)],
        compiler_params=params(),
        name="pack",
    )(*arrays)


def finish_kernel(co_ref, *refs):
    groups = refs[0:4], refs[4:8], refs[8:12]
    gq_ref, go_ref, gu_ref, gd_ref, gv_ref = refs[12:17]
    half = gq_ref.shape[0] // 2
    unit = LANES // 2
    for group, parts, scr in zip(range(3), groups, refs[17:20]):
        for at, part in enumerate(parts):
            scr[((at // 2) ^ co_ref[2]) * 2 + ((at % 2) ^ co_ref[1])] = part[...]
        for y in range(2):
            rows = slice(y * half, (y + 1) * half)
            for x in range(2):
                owner = 2 * y + x
                if group == 0:
                    for window in range(4):
                        for t in range(3):
                            at = (window * 3 + t) * half
                            value = scr[owner, at : at + half, :].astype(f32)
                            ref, tile = gq_ref, (2 * window + x) * 3 + t
                            if window == 3:
                                ref, tile = go_ref, x * 3 + t
                            ref[rows, tile * LANES : (tile + 1) * LANES] = value
                    continue
                for i in range(2 // group):
                    sub = 2 * (group - 1) + i
                    for z in range(2):
                        for c in range(2):
                            at = ((2 * i + z) * 2 + c) * half
                            tile = (2 * (2 * z + x) + c) * 3 + sub
                            gu_ref[rows, tile * LANES : (tile + 1) * LANES] = scr[
                                owner, at : at + half, :
                            ].astype(f32)
        if group == 0:
            continue
        for i in range(2 // group):
            sub = 2 * (group - 1) + i
            for x in range(2):
                for t in range(3):
                    at = 4 * (2 // group) * half + (3 * i + t) * unit
                    block = jnp.concatenate([scr[2 * y + x, at : at + unit, :] for y in range(2)], 0)
                    lanes = slice((3 * x + t) * LANES, (3 * x + t + 1) * LANES)
                    gd_ref[sub * LANES : (sub + 1) * LANES, lanes] = block.astype(f32).T
    gv_ref[...] = scr[0, scr.shape[1] - gv_ref.shape[0] :, :].astype(f32)


def finish(coords, groups, shapes):
    whole = lambda s: pl.BlockSpec(s, lambda i, co: (0,) * len(s))
    arrays = [entry for group in groups for entry in group]
    return pl.pallas_call(
        finish_kernel,
        grid_spec=pltpu.PrefetchScalarGridSpec(
            num_scalar_prefetch=1,
            grid=(1,),
            in_specs=[whole(entry.shape) for entry in arrays],
            out_specs=[whole(s) for s in shapes],
            scratch_shapes=[pltpu.VMEM((4,) + group[0].shape, bf16) for group in groups],
        ),
        out_shape=[jax.ShapeDtypeStruct(s, f32) for s in shapes],
        compiler_params=params(),
        name="finish",
    )(coords, *arrays)


def norm_back_kernel(x_ref, cot_ref, dh1_ref, dh2_ref, ln_ref, dx_ref, sums_ref):
    x = x_ref[...].astype(f32)
    centred = x - jnp.mean(x, -1, keepdims=True)
    inverse = lax.rsqrt(jnp.mean(centred * centred, -1, keepdims=True) + 1e-05)
    normed = centred * inverse
    dh1, dh2 = dh1_ref[...], dh2_ref[...]
    scaled = dh1 * ln_ref[0:1, :] + dh2 * ln_ref[2:3, :]
    spread = (
        scaled
        - jnp.mean(scaled, -1, keepdims=True)
        - normed * jnp.mean(scaled * normed, -1, keepdims=True)
    )
    dx_ref[...] = cot_ref[...].astype(f32) + inverse * spread

    @pl.when(pl.program_id(0) == 0)
    def _():
        sums_ref[...] = jnp.zeros_like(sums_ref)

    for row, value in enumerate((dh1 * normed, dh1, dh2 * normed, dh2)):
        sums_ref[row : row + 1, :] += jnp.sum(value, 0, keepdims=True)


def norm_back(x, cot, dh1, dh2, ln, rows=256):
    count, width = x.shape
    block = pl.BlockSpec((rows, width), lambda i: (i, 0))
    return pl.pallas_call(
        norm_back_kernel,
        grid=(count // rows,),
        in_specs=[block] * 4 + [fixed(ln.shape)],
        out_specs=[block, pl.BlockSpec((8, width), lambda i: (0, 0))],
        out_shape=[
            jax.ShapeDtypeStruct((count, width), f32),
            jax.ShapeDtypeStruct((8, width), f32),
        ],
        compiler_params=params(),
        cost_estimate=pl.CostEstimate(
            flops=30 * count * width, bytes_accessed=12 * 2**20, transcendentals=0
        ),
        name="norm_back",
    )(x, cot, dh1, dh2, ln)


def body(
    tokens_in, ln1_gain, ln1_bias, ln2_gain, ln2_bias, qkv_weight, qkv_bias, out_weight, out_bias,
    up_weight, up_bias, down_weight, down_bias, cotangent, lengths, assignment, clip_bound,
):
    dp, fsdp = lax.axis_size("dp"), lax.axis_size("fsdp")
    both = ("dp", "fsdp")
    total = dp * fsdp
    fast = (dp, fsdp) == (4, 8)
    me = lax.axis_index("dp") * fsdp + lax.axis_index("fsdp")

    def swap(value, even, odd=None):
        pairs = [(i, i ^ (even if odd is None or i % 2 == 0 else odd)) for i in range(total)]
        return lax.ppermute(value, both, pairs)

    width = tokens_in.shape[2]
    smalls = (ln1_gain, ln1_bias, ln2_gain, ln2_bias, qkv_bias, out_bias, up_bias, down_bias)
    packed = jnp.concatenate(smalls)
    if fast:
        slot = lax.broadcasted_iota(jnp.int32, (fsdp, 1), 0) == lax.axis_index("fsdp")
        rows = jnp.where(slot, packed[None, :], jnp.zeros_like(packed)[None, :])
        for at in range(3):
            rows = rows + swap(rows, 2**at)
    else:
        rows = lax.all_gather(packed, "fsdp", axis=0)
    vectors, start = [], 0
    for entry in smalls:
        stop = start + entry.shape[0]
        vectors.append(rows[:, start:stop].reshape(1, -1).astype(f32))
        start = stop
    ln = jnp.concatenate(vectors[:4] + [jnp.zeros((4, vectors[0].shape[1]), f32)], 0)
    qkv_b, out_b, up_b, down_b = vectors[4:]

    spot = [me & 1, (me >> 3) & 1, (me >> 4) & 1, (me >> 1) & 3] if fast else [0 * me] * 4
    coords = jnp.stack(spot + [lengths[0]]).astype(jnp.int32)
    if fast:
        in_own, in_mine, ff_own, ff_mine = cut(coords, qkv_weight, out_weight, up_weight, down_weight)
        lines = []
        for piece in (in_mine, ff_mine):
            lines.append([swap(piece, 2 * k) for k in (1, 2, 3)])
        gathered = []
        for own, line in ((in_own, lines[0]), (ff_own, lines[1])):
            line = lax.optimization_barrier(jnp.stack(line))
            mine = [own, line] + [swap(line, 8 * way) for way in (1, 2, 3)]
            theirs = [swap(entry, 1) for entry in mine]
            gathered.append((mine, theirs))
    else:
        whole = [
            lax.all_gather(w, "fsdp", axis=0, tiled=True)
            for w in (qkv_weight, out_weight, up_weight, down_weight)
        ]
        flat = lambda w: w.reshape(4, 2, 2, w.shape[0] // 16, 2, -1, LANES).transpose(
            0, 1, 2, 4, 5, 3, 6
        ).reshape(4, 2, 4, -1, LANES)
        qkv_p, out_p, up_p = (flat(w) for w in whole[:3])
        down_p = whole[3].reshape(4, 2, 3, 2, LANES // 2, 2, 3, LANES).transpose(0, 1, 3, 5, 2, 6, 4, 7)
        down_p = down_p.reshape(up_p.shape)
        up_p = up_p.reshape(4, 2, 4, 2, 2, 3, width // 16, LANES).swapaxes(4, 5).reshape(up_p.shape)
        gathered = []
        for entry in (jnp.concatenate([qkv_p, out_p], 3), jnp.stack([up_p, down_p], 3)):
            gathered.append(
                tuple([entry[0, c]] + [entry[1:, c, q] for q in range(4)] for c in range(2))
            )

    tokens = tokens_in[0]
    count, width = tokens.shape
    tables = rotary_tables(count)
    h1, h2, h1t, h2t, cot, cott = prepare(lengths, tokens, cotangent[0], ln)
    qkv, w_qkv, w_out = qkv_forward(coords, h1, qkv_b, tables, gathered[0])
    heads, dqkv = attention(qkv, cot, w_out, tables)
    *in_pieces, qkv_bias_grad, cot_sum, dh1, acc, in_sq = inner_grads(
        coords, h1t, dqkv, w_qkv, heads, cot, tokens, w_out, out_b + down_b
    )
    up_b = up_b.reshape(8, 3, LANES).swapaxes(0, 1).reshape(1, -1)
    ff = (coords, h2, h2t, cot, cott, up_b)
    acc, *f1_pieces, ub_grad1, dh2, f1_sq = feed(*ff, acc, None, gathered[1], 0, 2)
    mixed, *f2_pieces, ub_grad2, dh2, f2_sq = feed(*ff, acc, dh2, gathered[1], 2, 1)
    groups = []
    for pieces in (in_pieces, f1_pieces, f2_pieces):
        kept, sent, kept_other, sent_other = (entry.reshape(2, 4, -1, LANES) for entry in pieces)
        if fast:
            sent, sent_other = swap(sent, 8, 16), swap(sent_other, 16, 8)
            kept_other, sent_other = swap(kept_other, 1), swap(sent_other, 1)
        groups.append((kept, sent, kept_other, sent_other))
    dx, ln_sums = norm_back(tokens, cot, dh1, dh2, ln)
    ln_grads = ln_sums[:4]

    squares = jnp.sum(in_sq + f1_sq + f2_sq) + jnp.sum(ln_grads * ln_grads)
    slots = jnp.arange(total, dtype=jnp.int32)
    facts = jnp.stack([squares, assignment[0].astype(f32)])[:, None]
    facts = jnp.where(slots[None, :] == me, facts, 0.0)
    if fast:
        facts = facts + swap(facts, 1)
        packed = pack(ln_sums, qkv_bias_grad, cot_sum, ub_grad1, ub_grad2)
        vectors = [packed, swap(packed, 8, 16)]
        facts = facts + swap(facts, 8) + swap(facts, 16) + swap(facts, 24)
        vectors += [swap(packed, 1), swap(packed, 17, 9)]
        facts = facts + swap(facts, 2) + swap(facts, 4) + swap(facts, 6)
    else:
        facts = lax.psum(facts, both)
    norms, numbers = jnp.sqrt(facts[0]), facts[1].astype(jnp.int32)
    ahead = (norms[None, :] < norms[:, None]) | (
        (norms[None, :] == norms[:, None]) & (slots[None, :] < slots[:, None])
    )
    rank = jnp.sum(ahead.astype(jnp.int32), 1)
    median = jnp.sum(jnp.where(rank == total // 2, norms, 0.0))
    bound = median * clip_bound[0].astype(f32) / 8.0
    slot_scale = jnp.minimum(1.0, bound / (norms + 1e-06))
    clip_scale = jnp.sum(jnp.where(numbers[None, :] == slots[:, None], slot_scale[None, :], 0.0), 1)
    if fast:
        next_slot = me ^ jnp.where(me % 2 == 0, 8, 16)
        sources = jnp.stack([me, next_slot, me ^ 1, next_slot ^ 1])
    else:
        sources = jnp.stack([me] * 4)
    own_scales = jnp.sum(jnp.where(slots[None, :] == sources[:, None], slot_scale[None, :], 0.0), 1)
    own = own_scales[0]
    scales = own_scales / total
    share = scales[0]

    if fast:
        finals, kepts = [], []
        for arrays, more in zip(groups, ((), (), vectors)):
            sent = combine(scales, coords, 1, arrays, more)
            kepts.append(swap(sent, 16, 8))
        for name, arrays, came, more in zip("abc", groups, kepts, ((), (), vectors)):
            kept = combine(scales, coords, 0, arrays, more)
            add = lambda at, *more: sum((e.astype(f32) for e in more), kept[at].astype(f32) + came[at])
            near = swap(add(slice(2, 4)).astype(bf16), 2)
            last = swap(add(1, near[1]).astype(bf16), 4)
            line = add(0, near[0], last).astype(bf16)
            along_x, along_y = swap(line, 8), swap(line, 16)
            turn = (along_y, 8) if name == "b" else (along_x, 16)
            finals.append((line, along_x, along_y, swap(*turn)))
        own_rows = width // fsdp
        hidden = up_b.shape[1]
        shapes = [(own_rows, 3 * width), (own_rows, width), (own_rows, hidden)]
        shapes += [(hidden // fsdp, width), vectors[0].shape[1:]]
        gq, go, gu, gd, own_row = finish(coords, finals, shapes)
        own_row = own_row.reshape(-1)
    else:
        up_bias_grad = jnp.concatenate([ub_grad1, ub_grad2], 1).reshape(3, 8, LANES).swapaxes(0, 1)
        vector_grads = [ln_grads[i] for i in range(4)] + [qkv_bias_grad, cot_sum, up_bias_grad]
        vector_grads = jnp.concatenate([entry.reshape(fsdp, -1) for entry in vector_grads], 1)
        vector_grads = lax.psum(vector_grads * share, both)
        own_row = lax.dynamic_index_in_dim(vector_grads, lax.axis_index("fsdp"), 0, keepdims=False)

        def plain(arrays):
            kept, sent, kept_other, sent_other = (
                entry.reshape(2, 2, 2, -1, LANES).swapaxes(1, 2).reshape(entry.shape)
                for entry in arrays
            )
            return jnp.stack([jnp.stack([kept, sent]), jnp.stack([kept_other, sent_other], 1)])

        half = width // 16
        inner = plain(groups[0]).reshape(2, 2, 2, 4, 4, 3, half, LANES)
        flat = lambda e: e.transpose(3, 0, 2, 6, 4, 1, 5, 7).reshape(width, -1)
        outs = [flat(inner[:, :, :, :, :3]), flat(inner[:, :, :, :, 3:])]
        ups, downs = [], []
        for entry in groups[1:]:
            up, down = jnp.split(plain(entry), 2, 4)
            ups.append(up.reshape(2, 2, 2, 4, -1, 2, 2, half, LANES))
            downs.append(down.reshape(2, 2, 2, 4, -1, 3, LANES // 2, LANES))
        up, down = jnp.concatenate(ups, 4), jnp.concatenate(downs, 4)
        outs.append(up.transpose(3, 0, 2, 7, 5, 1, 6, 4, 8).reshape(width, -1))
        outs.append(down.transpose(3, 0, 4, 7, 1, 5, 2, 6).reshape(-1, width))
        outs = [(entry.astype(f32) * share).astype(bf16) for entry in outs]
        gq, go, gu, gd = (
            lax.psum(
                lax.psum_scatter(w, "fsdp", scatter_dimension=0, tiled=True).astype(f32), "dp"
            )
            for w in outs
        )

    tokens_grad = (own * dx).astype(bf16)[None]
    sizes = [ln1_gain.shape[0]] * 4 + [qkv_bias.shape[0], out_bias.shape[0], up_bias.shape[0]]
    parts, start = [], 0
    for size in sizes:
        parts.append(own_row[start : start + size])
        start += size
    g1, b1, g2, b2, gqb, gob, gub = parts
    return (mixed[None], tokens_grad, clip_scale, g1, b1, g2, b2, gq, gqb, go, gob, gu, gub, gd, gob)


def solution(mesh):
    step = mapped(mesh)
    if dict(mesh.shape) != {"dp": 4, "fsdp": 8}:
        return step
    return step


def mapped(mesh):
    rows, cols, flat = P("fsdp", None), P("fsdp"), P(("dp", "fsdp"))
    slots = P(("dp", "fsdp"), None, None)
    return jax.shard_map(
        body,
        mesh=mesh,
        in_specs=(slots, cols, cols, cols, cols, rows, cols, rows, cols, rows, cols, rows, cols)
        + (slots, flat, flat, P()),
        out_specs=(slots, slots, P(), cols, cols, cols, cols, rows, cols, rows, cols, rows, cols)
        + (rows, cols),
        check_vma=False,
    )
```

profile of v0, /device:TPU:0, one launch (start us, length us, event | category | flops | bytes accessed | tf_op | source)
XLA Modules:
  0.0 395.2 jit_solution(12031396878646368522)
XLA Ops:
  2.0 3.9 cut.1
  5.9 3.1 collective-permute-start.3
  9.0 2.6 collective-permute-start.4
  12.8 3.2 fusion.3
  18.1 8.0 %collective-permute-done.1 = bf16[8,1248]{1,0:T(8,128)(2,1)S(1)} collective-permute-done((bf16[8,1248]{1,0:T(8,128)(2,1)S(1)}, bf16[8,1248]{1,0:T(8,128)(2,1)S(1)}, u32[]{:S(2)}, u32[]{:S(2)}) %collective-permute-start.1) | collective-permute-done | bytes 20000 | tf_op jit(solution)/shard_map/ppermute | solution.py:863
  26.2 2.8 collective-permute-start.2
  30.9 2.8 collective-permute-start.15
  35.2 1.6 collective-permute-start.6
  36.7 1.5 collective-permute-start.7
  38.8 14.7 %collective-permute-done.15 = bf16[2,576,128]{2,1,0:T(8,128)(2,1)S(1)} collective-permute-done((bf16[2,576,128]{2,1,0:T(8,128)(2,1)S(1)}, bf16[2,576,128]{2,1,0:T(8,128)(2,1)S(1)}, u32[]{:S(2)}, u32[]{:S(2)}) %collective-permute-start.15) | collective-permute-done | bytes 294944 | tf_op jit(solution)/shard_map/ppermute | solution.py:863
  54.1 2.4 collective-permute-done.7.p3
  59.4 6.6 %prepare.1 = (bf16[1024,768]{1,0:T(8,128)(2,1)}, bf16[1024,768]{1,0:T(8,128)(2,1)}, bf16[768,1024]{1,0:T(8,128)(2,1)}, bf16[768,1024]{1,0:T(8,128)(2,1)}, bf16[1...) custom-call(s32[1]{0:T(128)S(6)} %copy.33.len_ref, bf16[1024,768]{1,0:T(8,128)(2,1)} %bitcast.74, ...), custom_call_target="tpu_custom_call" | custom-call | flops 15728640 | bytes 12582912 | tf_op jit(solution)/shard_map/prepare/pallas_call | solution.py:109
  70.4 12.3 %qkv_forward.1 = (bf16[1024,2304]{1,0:T(8,128)(2,1)}, bf16[768,2304]{1,0:T(8,128)(2,1)}, bf16[768,768]{1,0:T(8,128)(2,1)}) custom-call(s32[5]{0:T(128)} %stack.65.co_ref.refs_0_, bf16[1024,768]{1,0:T(8,128)(2,1)} %get-tuple-element.67.h1_ref, f32[1,2304]{1,0:T(1,128)} %reshape.373.b_ref, f32[1024,128]{1,0:T(8,128)} %get-tuple-element.122.c_ref, ...), custom_call_target="tpu_custom_call" | custom-call | flops 3623878656 | bytes 18874368 | tf_op jit(solution)/shard_map/qkv_forward/pallas_call | solution.py:241
  82.7 41.5 %attention.1 = (bf16[1024,768]{1,0:T(8,128)(2,1)}, bf16[1024,2304]{1,0:T(8,128)(2,1)}) custom-call(bf16[1024,2304]{1,0:T(8,128)(2,1)} %get-tuple-element.70.q_ref.k_ref.v_ref, bf16[1024,2304]{1,0:T(8,128)(2,1)} %get-tuple-element.70.q_ref.k_ref.v_ref, bf16[1024,2304]{1,0:T(8,128)(2,1)} %get-tuple-element.70.q_ref.k_ref.v_ref, ...), custom_call_target="tpu_custom_call" | custom-call | flops 30000001024 | bytes 20971520 | tf_op jit(solution)/shard_map/attention/pallas_call | solution.py:371
  125.3 21.5 %inner_grads.1 = (bf16[2,4,4,144,128]{4,3,2,1,0:T(8,128)(2,1)}, bf16[2,4,4,144,128]{4,3,2,1,0:T(8,128)(2,1)}, bf16[2,4,4,144,128]{4,3,2,1,0:T(8,128)(2,1)}, bf16...) custom-call(s32[5]{0:T(128)} %stack.65.co_ref.refs_0_, ...), custom_call_target="tpu_custom_call" | custom-call | flops 9663676416 | bytes 25165824 | tf_op jit(solution)/shard_map/inner_grads/pallas_call | solution.py:642
  146.8 1.6 collective-permute-start.34
  149.4 39.2 %feed.2 = (f32[1024,768]{1,0:T(8,128)}, bf16[2,4,768,128]{3,2,1,0:T(8,128)(2,1)}, bf16[2,4,768,128]{3,2,1,0:T(8,128)(2,1)}, bf16[2,4,768,128]{3,2,1,0:T(8,128)(2...) custom-call(s32[5]{0:T(128)} %stack.65.co_ref.refs_0_, ...), custom_call_target="tpu_custom_call" | custom-call | flops 19327352832 | bytes 25165824 | tf_op jit(solution)/shard_map/feed/pallas_call | solution.py:536
  188.7 24.7 %feed.3 = (bf16[1024,768]{1,0:T(8,128)(2,1)}, bf16[2,4,384,128]{3,2,1,0:T(8,128)(2,1)}, bf16[2,4,384,128]{3,2,1,0:T(8,128)(2,1)}, bf16[2,4,384,128]{3,2,1,0:T(8,...) custom-call(s32[5]{0:T(128)} %stack.65.co_ref.refs_0_, ...), custom_call_target="tpu_custom_call" | custom-call | flops 9663676416 | bytes 12582912 | tf_op jit(solution)/shard_map/feed/pallas_call | solution.py:536
  213.4 6.9 %norm_back.1 = (f32[1024,768]{1,0:T(8,128)}, f32[8,768]{1,0:T(8,128)}) custom-call(bf16[1024,768]{1,0:T(8,128)(2,1)} %bitcast.76, bf16[1024,768]{1,0:T(8,128)(2,1)} %get-tuple-element.64.cot_ref.refs_3_, f32[1024,768]{1,0:T(8,128)} %get-tuple-element.84.dh1_ref, f32[1024,768]{1,0:T(8,128)} %get-tuple-element.85.dh2_ref, f32[8,768]{1,0:T(8,128)} %concatenate.7.ln_ref), custom_call_target="tpu_custom_call" | custom-call | flops 23592960 | bytes 12582912 | tf_op jit(solution)/shard_map/norm_back/pallas_call | solution.py:834
  226.8 2.4 collective-permute-done.26
  230.5 11.8 %collective-permute-done.27 = f32[2,32]{1,0:T(2,128)S(1)} collective-permute-done((f32[2,32]{1,0:T(2,128)S(1)}, f32[2,32]{1,0:T(2,128)S(1)}, u32[]{:S(2)}, u32[]{:S(2)}) %collective-permute-start.27) | collective-permute-done | bytes 288 | tf_op jit(solution)/shard_map/ppermute | solution.py:863
  243.6 3.1 collective-permute-done.28
  246.8 3.7 collective-permute-start.29
  250.5 1.6 collective-permute-done.29
  252.0 3.5 collective-permute-start.30
  255.5 1.6 collective-permute-done.30
  257.1 2.4 collective-permute-start.31
  259.4 1.5 pack.1.refs_4_
  261.0 1.5 collective-permute-done.31
  263.3 3.6 collective-permute-done.56.refs_5_
  266.9 1.5 collective-permute-done.57.refs_6_
  273.9 18.3 %collective-permute-done.54 = bf16[2,4,384,128]{3,2,1,0:T(8,128)(2,1)} collective-permute-done((bf16[2,4,384,128]{3,2,1,0:T(8,128)(2,1)}, bf16[2,4,384,128]{3,2,1,0:T(8,128)(2,1)}, u32[]{:S(2)}, u32[]{:S(2)}) %collective-permute-start.54) | collective-permute-done | bytes 786464 | tf_op jit(solution)/shard_map/ppermute | solution.py:863
  293.4 4.0 %collective-permute-done.42.refs_1_ = bf16[2,4,768,128]{3,2,1,0:T(8,128)(2,1)S(1)} collective-permute-done((bf16[2,4,768,128]{3,2,1,0:T(8,128)(2,1)}, bf16[2,4,768,128]{3,2,1,0:T(8,128)(2,1)S(1)}, u32[]{:S(2)}, u32[]{:S(2)}) %collective-permute-start.42) | collective-permute-done | bytes 1572896 | tf_op jit(solution)/shard_map/ppermute | solution.py:863
  298.3 4.6 %combine.7 = bf16[4,576,128]{2,1,0:T(8,128)(2,1)} custom-call(f32[4]{0:T(128)} %broadcast_multiply_fusion.scale_ref, s32[5]{0:T(128)} %stack.65.co_ref.refs_0_, bf16[2,4,576,128]{3,2,1,0:T(8,128)(2,1)} %bitcast.77, bf16[2,4,576,128]{3,2,1,0:T(8,128)(2,1)} %copy-done.2, bf16[2,4,576,128]{3,2,1,0:T(8,128)(2,1)} %collective-permute-done.33.refs_2_, ...), custom_call_target="tpu_custom_call" | custom-call | flops 10000000 | bytes 2949120 | tf_op jit(solution)/shard_map/combine/pallas_call | solution.py:696
  304.1 5.0 %combine.9 = bf16[4,768,128]{2,1,0:T(8,128)(2,1)} custom-call(f32[4]{0:T(128)} %broadcast_multiply_fusion.scale_ref, s32[5]{0:T(128)} %stack.65.co_ref.refs_0_, bf16[2,4,768,128]{3,2,1,0:T(8,128)(2,1)} %get-tuple-element.92.refs_0_, bf16[2,4,768,128]{3,2,1,0:T(8,128)(2,1)} %copy-done, bf16[2,4,768,128]{3,2,1,0:T(8,128)(2,1)} %copy-done.1, ...), custom_call_target="tpu_custom_call" | custom-call | flops 10000000 | bytes 3932160 | tf_op jit(solution)/shard_map/combine/pallas_call | solution.py:696
  309.1 4.1 %collective-permute-done.58.refs_7_ = f32[8,16,128]{2,1,0:T(8,128)S(1)} collective-permute-done((f32[8,16,128]{2,1,0:T(8,128)S(1)}, f32[8,16,128]{2,1,0:T(8,128)S(1)}, u32[]{:S(2)}, u32[]{:S(2)}) %collective-permute-start.58) | collective-permute-done | bytes 65568 | tf_op jit(solution)/shard_map/ppermute | solution.py:863
  314.0 4.3 %combine.11 = bf16[4,400,128]{2,1,0:T(8,128)(2,1)} custom-call(f32[4]{0:T(128)} %broadcast_multiply_fusion.scale_ref, s32[5]{0:T(128)} %stack.65.co_ref.refs_0_, bf16[2,4,384,128]{3,2,1,0:T(8,128)(2,1)} %get-tuple-element.96.refs_0_, bf16[2,4,384,128]{3,2,1,0:T(8,128)(2,1)} %collective-permute-done.52.refs_1_, ...), custom_call_target="tpu_custom_call" | custom-call | flops 10000000 | bytes 1966080 | tf_op jit(solution)/shard_map/combine/pallas_call | solution.py:696
  319.6 4.4 %combine.6 = bf16[4,576,128]{2,1,0:T(8,128)(2,1)} custom-call(f32[4]{0:T(128)} %broadcast_multiply_fusion.scale_ref, s32[5]{0:T(128)} %stack.65.co_ref.refs_0_, bf16[2,4,576,128]{3,2,1,0:T(8,128)(2,1)} %bitcast.78, bf16[2,4,576,128]{3,2,1,0:T(8,128)(2,1)} %copy-done.2, bf16[2,4,576,128]{3,2,1,0:T(8,128)(2,1)} %collective-permute-done.33.refs_2_, ...), custom_call_target="tpu_custom_call" | custom-call | flops 10000000 | bytes 2949120 | tf_op jit(solution)/shard_map/combine/pallas_call | solution.py:696
  324.0 4.5 %combine.10 = bf16[4,400,128]{2,1,0:T(8,128)(2,1)} custom-call(f32[4]{0:T(128)} %broadcast_multiply_fusion.scale_ref, s32[5]{0:T(128)} %stack.65.co_ref.refs_0_, bf16[2,4,384,128]{3,2,1,0:T(8,128)(2,1)} %get-tuple-element.96.refs_0_, bf16[2,4,384,128]{3,2,1,0:T(8,128)(2,1)} %collective-permute-done.52.refs_1_, ...), custom_call_target="tpu_custom_call" | custom-call | flops 10000000 | bytes 1966080 | tf_op jit(solution)/shard_map/combine/pallas_call | solution.py:696
  330.8 1.9 collective-permute-start.60
  332.7 4.7 %combine.8 = bf16[4,768,128]{2,1,0:T(8,128)(2,1)} custom-call(f32[4]{0:T(128)} %broadcast_multiply_fusion.scale_ref, s32[5]{0:T(128)} %stack.65.co_ref.refs_0_, bf16[2,4,768,128]{3,2,1,0:T(8,128)(2,1)} %get-tuple-element.92.refs_0_, bf16[2,4,768,128]{3,2,1,0:T(8,128)(2,1)} %copy-done, bf16[2,4,768,128]{3,2,1,0:T(8,128)(2,1)} %copy-done.1, ...), custom_call_target="tpu_custom_call" | custom-call | flops 10000000 | bytes 3932160 | tf_op jit(solution)/shard_map/combine/pallas_call | solution.py:696
  338.8 5.0 %collective-permute-done.60 = bf16[2,400,128]{2,1,0:T(8,128)(2,1)S(1)} collective-permute-done((bf16[2,400,128]{2,1,0:T(8,128)(2,1)S(1)}, bf16[2,400,128]{2,1,0:T(8,128)(2,1)S(1)}, u32[]{:S(2)}, u32[]{:S(2)}) %collective-permute-start.60) | collective-permute-done | bytes 204832 | tf_op jit(solution)/shard_map/ppermute | solution.py:863
  346.2 1.9 collective-permute-start.38
  348.1 8.1 %collective-permute-done.47 = bf16[2,768,128]{2,1,0:T(8,128)(2,1)S(1)} collective-permute-done((bf16[2,768,128]{2,1,0:T(8,128)(2,1)S(1)}, bf16[2,768,128]{2,1,0:T(8,128)(2,1)S(1)}, u32[]{:S(2)}, u32[]{:S(2)}) %collective-permute-start.47) | collective-permute-done | bytes 393248 | tf_op jit(solution)/shard_map/ppermute | solution.py:863
  359.6 7.5 %collective-permute-done.48 = bf16[768,128]{1,0:T(8,128)(2,1)S(1)} collective-permute-done((bf16[768,128]{1,0:T(8,128)(2,1)S(1)}, bf16[768,128]{1,0:T(8,128)(2,1)S(1)}, u32[]{:S(2)}, u32[]{:S(2)}) %collective-permute-start.48) | collective-permute-done | bytes 196640 | tf_op jit(solution)/shard_map/ppermute | solution.py:863
  379.1 5.8 %collective-permute-done.64.refs_11_ = bf16[400,128]{1,0:T(8,128)(2,1)S(1)} collective-permute-done((bf16[400,128]{1,0:T(8,128)(2,1)S(1)}, bf16[400,128]{1,0:T(8,128)(2,1)S(1)}, u32[]{:S(2)}, u32[]{:S(2)}) %collective-permute-start.64) | collective-permute-done | bytes 102432 | tf_op jit(solution)/shard_map/ppermute | solution.py:863
  386.4 4.3 %finish.1 = (f32[96,2304]{1,0:T(8,128)}, f32[96,768]{1,0:T(8,128)}, f32[96,3072]{1,0:T(8,128)}, f32[384,768]{1,0:T(8,128)}, f32[16,128]{1,0:T(8,128)}) custom-call(s32[5]{0:T(128)} %stack.65.co_ref.refs_0_, bf16[576,128]{1,0:T(8,128)(2,1)} %copy-done.10, bf16[576,128]{1,0:T(8,128)(2,1)} %copy-done.19, bf16[576,128]{1,0:T(8,128)(2,1)} %copy-done.20, ...), custom_call_target="tpu_custom_call" | custom-call | tf_op jit(solution)/shard_map/finish/pallas_call | solution.py:794
  390.7 1.5 fusion.29
  (240 shorter events, 61.4 us)
Async XLA Ops:
  5.9 27.8 %collective-permute-start.3 = (bf16[576,128]{1,0:T(8,128)(2,1)}, bf16[576,128]{1,0:T(8,128)(2,1)S(1)}, u32[]{:S(2)}, u32[]{:S(2)}) collective-permute-start(bf16[576,128]{1,0:T(8,128)(2,1)} %get-tuple-element.69), channel_id=1, source_target_pairs={{0,2},{1,3},{2,0},{3,1},{4,6},{5,7},{6,4},{7,5},{8,10},{9,11},{10,... | collective-permute-start | bytes 442376 | tf_op jit(solution)/shard_map/ppermute | solution.py:863
  9.0 26.1 %collective-permute-start.4 = (bf16[576,128]{1,0:T(8,128)(2,1)}, bf16[576,128]{1,0:T(8,128)(2,1)S(1)}, u32[]{:S(2)}, u32[]{:S(2)}) collective-permute-start(bf16[576,128]{1,0:T(8,128)(2,1)} %get-tuple-element.69), channel_id=1, source_target_pairs={{0,4},{1,5},{2,6},{3,7},{4,0},{5,1},{6,2},{7,3},{8,12},{9,13},{10,... | collective-permute-start | bytes 442376 | tf_op jit(solution)/shard_map/ppermute | solution.py:863
  11.6 23.5 %collective-permute-start.5 = (bf16[576,128]{1,0:T(8,128)(2,1)}, bf16[576,128]{1,0:T(8,128)(2,1)S(1)}, u32[]{:S(2)}, u32[]{:S(2)}) collective-permute-start(bf16[576,128]{1,0:T(8,128)(2,1)} %get-tuple-element.69), channel_id=1, source_target_pairs={{0,6},{1,7},{2,4},{3,5},{4,2},{5,3},{6,0},{7,1},{8,14},{9,15},{10,... | collective-permute-start | bytes 442376 | tf_op jit(solution)/shard_map/ppermute | solution.py:863
  11.8 26.4 %collective-permute-start.14 = (bf16[2,576,128]{2,1,0:T(8,128)(2,1)}, bf16[2,576,128]{2,1,0:T(8,128)(2,1)S(1)}, u32[]{:S(2)}, u32[]{:S(2)}) collective-permute-start(bf16[2,576,128]{2,1,0:T(8,128)(2,1)} %get-tuple-element.77), channel_id=1, source_target_pairs={{0,2},{1,3},{2,0},{3,1},{4,6},{5,7},{6,4},{7,5},{8,10},{9,11},{10,... | collective-permute-start | bytes 884744 | tf_op jit(solution)/shard_map/ppermute | solution.py:863
  30.9 22.6 %collective-permute-start.15 = (bf16[2,576,128]{2,1,0:T(8,128)(2,1)S(1)}, bf16[2,576,128]{2,1,0:T(8,128)(2,1)S(1)}, u32[]{:S(2)}, u32[]{:S(2)}) collective-permute-start(bf16[2,576,128]{2,1,0:T(8,128)(2,1)S(1)} %copy-done.41), channel_id=1, source_target_pairs={{0,4},{1,5},{2,6},{3,7},{4,0},{5,1},{6,2},{7,3},{8,12},{9,13},{10,... | collective-permute-start | bytes 884744 | tf_op jit(solution)/shard_map/ppermute | solution.py:863
  33.7 19.8 %collective-permute-start.16 = (bf16[2,576,128]{2,1,0:T(8,128)(2,1)S(1)}, bf16[2,576,128]{2,1,0:T(8,128)(2,1)S(1)}, u32[]{:S(2)}, u32[]{:S(2)}) collective-permute-start(bf16[2,576,128]{2,1,0:T(8,128)(2,1)S(1)} %copy-done.41), channel_id=1, source_target_pairs={{0,6},{1,7},{2,4},{3,5},{4,2},{5,3},{6,0},{7,1},{8,14},{9,15},{10,... | collective-permute-start | bytes 884744 | tf_op jit(solution)/shard_map/ppermute | solution.py:863
  35.2 18.8 %collective-permute-start.6 = (bf16[3,576,128]{2,1,0:T(8,128)(2,1)S(1)}, bf16[3,576,128]{2,1,0:T(8,128)(2,1)}, u32[]{:S(2)}, u32[]{:S(2)}) collective-permute-start(bf16[3,576,128]{2,1,0:T(8,128)(2,1)S(1)} %pad_maximum_fusion.1.p1), channel_id=1, source_target_pairs={{0,8},{1,9},{2,10},{3,11},{4,12},{5,13},{6,14},{7,15},{8,0},{9,1},... | collective-permute-start | bytes 1327112 | tf_op jit(solution)/shard_map/ppermute | solution.py:863
  36.7 19.7 %collective-permute-start.7 = (bf16[3,576,128]{2,1,0:T(8,128)(2,1)S(1)}, bf16[3,576,128]{2,1,0:T(8,128)(2,1)}, u32[]{:S(2)}, u32[]{:S(2)}) collective-permute-start(bf16[3,576,128]{2,1,0:T(8,128)(2,1)S(1)} %pad_maximum_fusion.1.p1), channel_id=1, source_target_pairs={{0,16},{1,17},{2,18},{3,19},{4,20},{5,21},{6,22},{7,23},{8,24},{9,... | collective-permute-start | bytes 1327112 | tf_op jit(solution)/shard_map/ppermute | solution.py:863
  38.2 18.2 %collective-permute-start.8 = (bf16[3,576,128]{2,1,0:T(8,128)(2,1)S(1)}, bf16[3,576,128]{2,1,0:T(8,128)(2,1)}, u32[]{:S(2)}, u32[]{:S(2)}) collective-permute-start(bf16[3,576,128]{2,1,0:T(8,128)(2,1)S(1)} %pad_maximum_fusion.1.p1), channel_id=1, source_target_pairs={{0,24},{1,25},{2,26},{3,27},{4,28},{5,29},{6,30},{7,31},{8,16},{9,... | collective-permute-start | bytes 1327112 | tf_op jit(solution)/shard_map/ppermute | solution.py:863
  53.5 13.3 %collective-permute-start.9 = (bf16[4,576,128]{2,1,0:T(8,128)(2,1)S(1)}, bf16[4,576,128]{2,1,0:T(8,128)(2,1)S(1)}, u32[]{:S(2)}, u32[]{:S(2)}) collective-permute-start(bf16[4,576,128]{2,1,0:T(8,128)(2,1)S(1)} %copy-done.39), channel_id=1, source_target_pairs={{0,1},{1,0},{2,3},{3,2},{4,5},{5,4},{6,7},{7,6},{8,9},{9,8},{10,11... | collective-permute-start | bytes 1769480 | tf_op jit(solution)/shard_map/ppermute | solution.py:863
  53.5 13.2 %collective-permute-start.10 = (bf16[3,576,128]{2,1,0:T(8,128)(2,1)S(1)}, bf16[3,576,128]{2,1,0:T(8,128)(2,1)}, u32[]{:S(2)}, u32[]{:S(2)}) collective-permute-start(bf16[3,576,128]{2,1,0:T(8,128)(2,1)S(1)} %pad_maximum_fusion.1.p1), channel_id=1, source_target_pairs={{0,1},{1,0},{2,3},{3,2},{4,5},{5,4},{6,7},{7,6},{8,9},{9,8},{10,11... | collective-permute-start | bytes 1327112 | tf_op jit(solution)/shard_map/ppermute | solution.py:863
  54.0 14.0 %collective-permute-start.11 = (bf16[3,576,128]{2,1,0:T(8,128)(2,1)}, bf16[3,576,128]{2,1,0:T(8,128)(2,1)}, u32[]{:S(2)}, u32[]{:S(2)}) collective-permute-start(bf16[3,576,128]{2,1,0:T(8,128)(2,1)} %collective-permute-done.6.p2), channel_id=1, source_target_pairs={{0,1},{1,0},{2,3},{3,2},{4,5},{5,4},{6,7},{7,6},{8,9},{9,8},{10,11... | collective-permute-start | bytes 1327112 | tf_op jit(solution)/shard_map/ppermute | solution.py:863
  56.5 12.5 %collective-permute-start.12 = (bf16[3,576,128]{2,1,0:T(8,128)(2,1)}, bf16[3,576,128]{2,1,0:T(8,128)(2,1)}, u32[]{:S(2)}, u32[]{:S(2)}) collective-permute-start(bf16[3,576,128]{2,1,0:T(8,128)(2,1)} %collective-permute-done.7.p3), channel_id=1, source_target_pairs={{0,1},{1,0},{2,3},{3,2},{4,5},{5,4},{6,7},{7,6},{8,9},{9,8},{10,11... | collective-permute-start | bytes 1327112 | tf_op jit(solution)/shard_map/ppermute | solution.py:863
  56.5 13.9 %collective-permute-start.13 = (bf16[3,576,128]{2,1,0:T(8,128)(2,1)}, bf16[3,576,128]{2,1,0:T(8,128)(2,1)}, u32[]{:S(2)}, u32[]{:S(2)}) collective-permute-start(bf16[3,576,128]{2,1,0:T(8,128)(2,1)} %collective-permute-done.8.p4), channel_id=1, source_target_pairs={{0,1},{1,0},{2,3},{3,2},{4,5},{5,4},{6,7},{7,6},{8,9},{9,8},{10,11... | collective-permute-start | bytes 1327112 | tf_op jit(solution)/shard_map/ppermute | solution.py:863
  66.7 81.7 %collective-permute-start.20 = (bf16[4,2,576,128]{3,2,1,0:T(8,128)(2,1)}, bf16[4,2,576,128]{3,2,1,0:T(8,128)(2,1)S(1)}, u32[]{:S(2)}, u32[]{:S(2)}) collective-permute-start(bf16[4,2,576,128]{3,2,1,0:T(8,128)(2,1)} %get-tuple-element.76.refs_17_.e0), channel_id=1, source_target_pairs={{0,1},{1,0},{2,3},{3,2},{4,5},{5,4},{6,7},{7,6},{8,9},{9,8},{10,11... | collective-permute-start | bytes 3538952 | tf_op jit(solution)/shard_map/ppermute | solution.py:863
  66.8 57.5 %collective-permute-start.17 = (bf16[3,2,576,128]{3,2,1,0:T(8,128)(2,1)S(1)}, bf16[3,2,576,128]{3,2,1,0:T(8,128)(2,1)}, u32[]{:S(2)}, u32[]{:S(2)}) collective-permute-start(bf16[3,2,576,128]{3,2,1,0:T(8,128)(2,1)S(1)} %pad_maximum_fusion.refs_18_.e1), channel_id=1, source_target_pairs={{0,8},{1,9},{2,10},{3,11},{4,12},{5,13},{6,14},{7,15},{8,0},{9,1},... | collective-permute-start | bytes 2654216 | tf_op jit(solution)/shard_map/ppermute | solution.py:863
  68.0 56.8 %collective-permute-start.18 = (bf16[3,2,576,128]{3,2,1,0:T(8,128)(2,1)S(1)}, bf16[3,2,576,128]{3,2,1,0:T(8,128)(2,1)}, u32[]{:S(2)}, u32[]{:S(2)}) collective-permute-start(bf16[3,2,576,128]{3,2,1,0:T(8,128)(2,1)S(1)} %pad_maximum_fusion.refs_18_.e1), channel_id=1, source_target_pairs={{0,16},{1,17},{2,18},{3,19},{4,20},{5,21},{6,22},{7,23},{8,24},{9,... | collective-permute-start | bytes 2654216 | tf_op jit(solution)/shard_map/ppermute | solution.py:863
  68.9 56.0 %collective-permute-start.19 = (bf16[3,2,576,128]{3,2,1,0:T(8,128)(2,1)S(1)}, bf16[3,2,576,128]{3,2,1,0:T(8,128)(2,1)}, u32[]{:S(2)}, u32[]{:S(2)}) collective-permute-start(bf16[3,2,576,128]{3,2,1,0:T(8,128)(2,1)S(1)} %pad_maximum_fusion.refs_18_.e1), channel_id=1, source_target_pairs={{0,24},{1,25},{2,26},{3,27},{4,28},{5,29},{6,30},{7,31},{8,16},{9,... | collective-permute-start | bytes 2654216 | tf_op jit(solution)/shard_map/ppermute | solution.py:863
  70.4 76.5 %collective-permute-start.21 = (bf16[3,2,576,128]{3,2,1,0:T(8,128)(2,1)S(1)}, bf16[3,2,576,128]{3,2,1,0:T(8,128)(2,1)S(1)}, u32[]{:S(2)}, u32[]{:S(2)}) collective-permute-start(bf16[3,2,576,128]{3,2,1,0:T(8,128)(2,1)S(1)} %pad_maximum_fusion.refs_18_.e1), channel_id=1, source_target_pairs={{0,1},{1,0},{2,3},{3,2},{4,5},{5,4},{6,7},{7,6},{8,9},{9,8},{10,11... | collective-permute-start | bytes 2654216 | tf_op jit(solution)/shard_map/ppermute | solution.py:863
  124.2 24.8 %collective-permute-start.22 = (bf16[3,2,576,128]{3,2,1,0:T(8,128)(2,1)}, bf16[3,2,576,128]{3,2,1,0:T(8,128)(2,1)}, u32[]{:S(2)}, u32[]{:S(2)}) collective-permute-start(bf16[3,2,576,128]{3,2,1,0:T(8,128)(2,1)} %collective-permute-done.17.refs_19_.e2), channel_id=1, source_target_pairs={{0,1},{1,0},{2,3},{3,2},{4,5},{5,4},{6,7},{7,6},{8,9},{9,8},{10,11... | collective-permute-start | bytes 2654216 | tf_op jit(solution)/shard_map/ppermute | solution.py:863
  124.8 24.2 %collective-permute-start.23 = (bf16[3,2,576,128]{3,2,1,0:T(8,128)(2,1)}, bf16[3,2,576,128]{3,2,1,0:T(8,128)(2,1)}, u32[]{:S(2)}, u32[]{:S(2)}) collective-permute-start(bf16[3,2,576,128]{3,2,1,0:T(8,128)(2,1)} %collective-permute-done.18.refs_20_.e3), channel_id=1, source_target_pairs={{0,1},{1,0},{2,3},{3,2},{4,5},{5,4},{6,7},{7,6},{8,9},{9,8},{10,11... | collective-permute-start | bytes 2654216 | tf_op jit(solution)/shard_map/ppermute | solution.py:863
  124.9 24.2 %collective-permute-start.24 = (bf16[3,2,576,128]{3,2,1,0:T(8,128)(2,1)}, bf16[3,2,576,128]{3,2,1,0:T(8,128)(2,1)}, u32[]{:S(2)}, u32[]{:S(2)}) collective-permute-start(bf16[3,2,576,128]{3,2,1,0:T(8,128)(2,1)} %collective-permute-done.19.refs_21_.e4), channel_id=1, source_target_pairs={{0,1},{1,0},{2,3},{3,2},{4,5},{5,4},{6,7},{7,6},{8,9},{9,8},{10,11... | collective-permute-start | bytes 2654216 | tf_op jit(solution)/shard_map/ppermute | solution.py:863
  146.8 122.4 %collective-permute-start.34 = (bf16[2,4,576,128]{3,2,1,0:T(8,128)(2,1)}, bf16[2,4,576,128]{3,2,1,0:T(8,128)(2,1)}, u32[]{:S(2)}, u32[]{:S(2)}) collective-permute-start(bf16[2,4,576,128]{3,2,1,0:T(8,128)(2,1)} %bitcast.94), channel_id=1, source_target_pairs={{0,16},{1,9},{2,18},{3,11},{4,20},{5,13},{6,22},{7,15},{8,24},{9,1... | collective-permute-start | bytes 3538952 | tf_op jit(solution)/shard_map/ppermute | solution.py:863
  148.4 120.8 %collective-permute-start.32 = (bf16[2,4,576,128]{3,2,1,0:T(8,128)(2,1)}, bf16[2,4,576,128]{3,2,1,0:T(8,128)(2,1)S(1)}, u32[]{:S(2)}, u32[]{:S(2)}) collective-permute-start(bf16[2,4,576,128]{3,2,1,0:T(8,128)(2,1)} %bitcast.93), channel_id=1, source_target_pairs={{0,8},{1,17},{2,10},{3,19},{4,12},{5,21},{6,14},{7,23},{8,0},{9,25... | collective-permute-start | bytes 3538952 | tf_op jit(solution)/shard_map/ppermute | solution.py:863
  221.6 50.5 %collective-permute-start.44 = (bf16[2,4,768,128]{3,2,1,0:T(8,128)(2,1)}, bf16[2,4,768,128]{3,2,1,0:T(8,128)(2,1)}, u32[]{:S(2)}, u32[]{:S(2)}) collective-permute-start(bf16[2,4,768,128]{3,2,1,0:T(8,128)(2,1)} %get-tuple-element.95), channel_id=1, source_target_pairs={{0,16},{1,9},{2,18},{3,11},{4,20},{5,13},{6,22},{7,15},{8,24},{9,1... | collective-permute-start | bytes 4718600 | tf_op jit(solution)/shard_map/ppermute | solution.py:863
  224.4 47.1 %collective-permute-start.33 = (bf16[2,4,576,128]{3,2,1,0:T(8,128)(2,1)}, bf16[2,4,576,128]{3,2,1,0:T(8,128)(2,1)}, u32[]{:S(2)}, u32[]{:S(2)}) collective-permute-start(bf16[2,4,576,128]{3,2,1,0:T(8,128)(2,1)} %bitcast.41), channel_id=1, source_target_pairs={{0,1},{1,0},{2,3},{3,2},{4,5},{5,4},{6,7},{7,6},{8,9},{9,8},{10,11... | collective-permute-start | bytes 3538952 | tf_op jit(solution)/shard_map/ppermute | solution.py:863
  229.2 13.1 %collective-permute-start.27 = (f32[2,32]{1,0:T(2,128)S(1)}, f32[2,32]{1,0:T(2,128)S(1)}, u32[]{:S(2)}, u32[]{:S(2)}) collective-permute-start(f32[2,32]{1,0:T(2,128)S(1)} %fusion.28), channel_id=1, source_target_pairs={{0,16},{1,17},{2,18},{3,19},{4,20},{5,21},{6,22},{7,23},{8,24},{9,... | collective-permute-start | bytes 776 | tf_op jit(solution)/shard_map/ppermute | solution.py:863
  268.4 29.1 %collective-permute-start.42 = (bf16[2,4,768,128]{3,2,1,0:T(8,128)(2,1)}, bf16[2,4,768,128]{3,2,1,0:T(8,128)(2,1)S(1)}, u32[]{:S(2)}, u32[]{:S(2)}) collective-permute-start(bf16[2,4,768,128]{3,2,1,0:T(8,128)(2,1)} %get-tuple-element.93), channel_id=1, source_target_pairs={{0,8},{1,17},{2,10},{3,19},{4,12},{5,21},{6,14},{7,23},{8,0},{9,25... | collective-permute-start | bytes 4718600 | tf_op jit(solution)/shard_map/ppermute | solution.py:863
  269.2 24.2 %collective-permute-start.35 = (bf16[2,4,576,128]{3,2,1,0:T(8,128)(2,1)}, bf16[2,4,576,128]{3,2,1,0:T(8,128)(2,1)}, u32[]{:S(2)}, u32[]{:S(2)}) collective-permute-start(bf16[2,4,576,128]{3,2,1,0:T(8,128)(2,1)} %collective-permute-done.34), channel_id=1, source_target_pairs={{0,1},{1,0},{2,3},{3,2},{4,5},{5,4},{6,7},{7,6},{8,9},{9,8},{10,11... | collective-permute-start | bytes 3538952 | tf_op jit(solution)/shard_map/ppermute | solution.py:863
  270.3 32.7 %collective-permute-start.43 = (bf16[2,4,768,128]{3,2,1,0:T(8,128)(2,1)}, bf16[2,4,768,128]{3,2,1,0:T(8,128)(2,1)S(1)}, u32[]{:S(2)}, u32[]{:S(2)}) collective-permute-start(bf16[2,4,768,128]{3,2,1,0:T(8,128)(2,1)} %get-tuple-element.94), channel_id=1, source_target_pairs={{0,1},{1,0},{2,3},{3,2},{4,5},{5,4},{6,7},{7,6},{8,9},{9,8},{10,11... | collective-permute-start | bytes 4718600 | tf_op jit(solution)/shard_map/ppermute | solution.py:863
  271.4 20.8 %collective-permute-start.54 = (bf16[2,4,384,128]{3,2,1,0:T(8,128)(2,1)}, bf16[2,4,384,128]{3,2,1,0:T(8,128)(2,1)}, u32[]{:S(2)}, u32[]{:S(2)}) collective-permute-start(bf16[2,4,384,128]{3,2,1,0:T(8,128)(2,1)} %get-tuple-element.99), channel_id=1, source_target_pairs={{0,16},{1,9},{2,18},{3,11},{4,20},{5,13},{6,22},{7,15},{8,24},{9,1... | collective-permute-start | bytes 2359304 | tf_op jit(solution)/shard_map/ppermute | solution.py:863
  272.0 31.7 %collective-permute-start.45 = (bf16[2,4,768,128]{3,2,1,0:T(8,128)(2,1)}, bf16[2,4,768,128]{3,2,1,0:T(8,128)(2,1)}, u32[]{:S(2)}, u32[]{:S(2)}) collective-permute-start(bf16[2,4,768,128]{3,2,1,0:T(8,128)(2,1)} %collective-permute-done.44), channel_id=1, source_target_pairs={{0,1},{1,0},{2,3},{3,2},{4,5},{5,4},{6,7},{7,6},{8,9},{9,8},{10,11... | collective-permute-start | bytes 4718600 | tf_op jit(solution)/shard_map/ppermute | solution.py:863
  292.2 21.7 %collective-permute-start.52 = (bf16[2,4,384,128]{3,2,1,0:T(8,128)(2,1)}, bf16[2,4,384,128]{3,2,1,0:T(8,128)(2,1)}, u32[]{:S(2)}, u32[]{:S(2)}) collective-permute-start(bf16[2,4,384,128]{3,2,1,0:T(8,128)(2,1)} %get-tuple-element.97), channel_id=1, source_target_pairs={{0,8},{1,17},{2,10},{3,19},{4,12},{5,21},{6,14},{7,23},{8,0},{9,25... | collective-permute-start | bytes 2359304 | tf_op jit(solution)/shard_map/ppermute | solution.py:863
  293.4 20.5 %collective-permute-start.53 = (bf16[2,4,384,128]{3,2,1,0:T(8,128)(2,1)}, bf16[2,4,384,128]{3,2,1,0:T(8,128)(2,1)}, u32[]{:S(2)}, u32[]{:S(2)}) collective-permute-start(bf16[2,4,384,128]{3,2,1,0:T(8,128)(2,1)} %get-tuple-element.98), channel_id=1, source_target_pairs={{0,1},{1,0},{2,3},{3,2},{4,5},{5,4},{6,7},{7,6},{8,9},{9,8},{10,11... | collective-permute-start | bytes 2359304 | tf_op jit(solution)/shard_map/ppermute | solution.py:863
  297.4 16.5 %collective-permute-start.55 = (bf16[2,4,384,128]{3,2,1,0:T(8,128)(2,1)}, bf16[2,4,384,128]{3,2,1,0:T(8,128)(2,1)}, u32[]{:S(2)}, u32[]{:S(2)}) collective-permute-start(bf16[2,4,384,128]{3,2,1,0:T(8,128)(2,1)} %collective-permute-done.54), channel_id=1, source_target_pairs={{0,1},{1,0},{2,3},{3,2},{4,5},{5,4},{6,7},{7,6},{8,9},{9,8},{10,11... | collective-permute-start | bytes 2359304 | tf_op jit(solution)/shard_map/ppermute | solution.py:863
  302.9 25.5 %collective-permute-start.36 = (bf16[4,576,128]{2,1,0:T(8,128)(2,1)}, bf16[4,576,128]{2,1,0:T(8,128)(2,1)}, u32[]{:S(2)}, u32[]{:S(2)}) collective-permute-start(bf16[4,576,128]{2,1,0:T(8,128)(2,1)} %combine.7), channel_id=1, source_target_pairs={{0,16},{1,9},{2,18},{3,11},{4,20},{5,13},{6,22},{7,15},{8,24},{9,1... | collective-permute-start | bytes 1769480 | tf_op jit(solution)/shard_map/ppermute | solution.py:863
  313.2 24.3 %collective-permute-start.46 = (bf16[4,768,128]{2,1,0:T(8,128)(2,1)}, bf16[4,768,128]{2,1,0:T(8,128)(2,1)S(1)}, u32[]{:S(2)}, u32[]{:S(2)}) collective-permute-start(bf16[4,768,128]{2,1,0:T(8,128)(2,1)} %combine.9), channel_id=1, source_target_pairs={{0,16},{1,9},{2,18},{3,11},{4,20},{5,13},{6,22},{7,15},{8,24},{9,1... | collective-permute-start | bytes 2359304 | tf_op jit(solution)/shard_map/ppermute | solution.py:863
  318.3 11.4 %collective-permute-start.59 = (bf16[4,400,128]{2,1,0:T(8,128)(2,1)}, bf16[4,400,128]{2,1,0:T(8,128)(2,1)S(1)}, u32[]{:S(2)}, u32[]{:S(2)}) collective-permute-start(bf16[4,400,128]{2,1,0:T(8,128)(2,1)} %combine.11), channel_id=1, source_target_pairs={{0,16},{1,9},{2,18},{3,11},{4,20},{5,13},{6,22},{7,15},{8,24},{9,1... | collective-permute-start | bytes 1228808 | tf_op jit(solution)/shard_map/ppermute | solution.py:863
  329.5 15.6 %collective-permute-start.37 = (bf16[2,576,128]{2,1,0:T(8,128)(2,1)S(1)}, bf16[2,576,128]{2,1,0:T(8,128)(2,1)S(1)}, u32[]{:S(2)}, u32[]{:S(2)}) collective-permute-start(bf16[2,576,128]{2,1,0:T(8,128)(2,1)S(1)} %add_convert_fusion.1), channel_id=1, source_target_pairs={{0,2},{1,3},{2,0},{3,1},{4,6},{5,7},{6,4},{7,5},{8,10},{9,11},{10,... | collective-permute-start | bytes 884744 | tf_op jit(solution)/shard_map/ppermute | solution.py:863
  330.8 13.1 %collective-permute-start.60 = (bf16[2,400,128]{2,1,0:T(8,128)(2,1)S(1)}, bf16[2,400,128]{2,1,0:T(8,128)(2,1)S(1)}, u32[]{:S(2)}, u32[]{:S(2)}) collective-permute-start(bf16[2,400,128]{2,1,0:T(8,128)(2,1)S(1)} %add_convert_fusion.2), channel_id=1, source_target_pairs={{0,2},{1,3},{2,0},{3,1},{4,6},{5,7},{6,4},{7,5},{8,10},{9,11},{10,... | collective-permute-start | bytes 614408 | tf_op jit(solution)/shard_map/ppermute | solution.py:863
  338.6 17.6 %collective-permute-start.47 = (bf16[2,768,128]{2,1,0:T(8,128)(2,1)S(1)}, bf16[2,768,128]{2,1,0:T(8,128)(2,1)S(1)}, u32[]{:S(2)}, u32[]{:S(2)}) collective-permute-start(bf16[2,768,128]{2,1,0:T(8,128)(2,1)S(1)} %add_convert_fusion), channel_id=1, source_target_pairs={{0,2},{1,3},{2,0},{3,1},{4,6},{5,7},{6,4},{7,5},{8,10},{9,11},{10,... | collective-permute-start | bytes 1179656 | tf_op jit(solution)/shard_map/ppermute | solution.py:863
  343.9 24.2 %collective-permute-start.61 = (bf16[400,128]{1,0:T(8,128)(2,1)S(1)}, bf16[400,128]{1,0:T(8,128)(2,1)S(1)}, u32[]{:S(2)}, u32[]{:S(2)}) collective-permute-start(bf16[400,128]{1,0:T(8,128)(2,1)S(1)} %fusion.10), channel_id=1, source_target_pairs={{0,4},{1,5},{2,6},{3,7},{4,0},{5,1},{6,2},{7,3},{8,12},{9,13},{10,... | collective-permute-start | bytes 307208 | tf_op jit(solution)/shard_map/ppermute | solution.py:863
  346.2 11.5 %collective-permute-start.38 = (bf16[576,128]{1,0:T(8,128)(2,1)S(1)}, bf16[576,128]{1,0:T(8,128)(2,1)S(1)}, u32[]{:S(2)}, u32[]{:S(2)}) collective-permute-start(bf16[576,128]{1,0:T(8,128)(2,1)S(1)} %fusion.9), channel_id=1, source_target_pairs={{0,4},{1,5},{2,6},{3,7},{4,0},{5,1},{6,2},{7,3},{8,12},{9,13},{10,... | collective-permute-start | bytes 442376 | tf_op jit(solution)/shard_map/ppermute | solution.py:863
  356.2 10.9 %collective-permute-start.48 = (bf16[768,128]{1,0:T(8,128)(2,1)S(1)}, bf16[768,128]{1,0:T(8,128)(2,1)S(1)}, u32[]{:S(2)}, u32[]{:S(2)}) collective-permute-start(bf16[768,128]{1,0:T(8,128)(2,1)S(1)} %fusion.8), channel_id=1, source_target_pairs={{0,4},{1,5},{2,6},{3,7},{4,0},{5,1},{6,2},{7,3},{8,12},{9,13},{10,... | collective-permute-start | bytes 589832 | tf_op jit(solution)/shard_map/ppermute | solution.py:863
  358.7 12.6 %collective-permute-start.39 = (bf16[576,128]{1,0:T(8,128)(2,1)S(1)}, bf16[576,128]{1,0:T(8,128)(2,1)S(1)}, u32[]{:S(2)}, u32[]{:S(2)}) collective-permute-start(bf16[576,128]{1,0:T(8,128)(2,1)S(1)} %fusion.6.refs_0_), channel_id=1, source_target_pairs={{0,8},{1,9},{2,10},{3,11},{4,12},{5,13},{6,14},{7,15},{8,0},{9,1},... | collective-permute-start | bytes 442376 | tf_op jit(solution)/shard_map/ppermute | solution.py:863
  370.5 14.4 %collective-permute-start.40 = (bf16[576,128]{1,0:T(8,128)(2,1)S(1)}, bf16[576,128]{1,0:T(8,128)(2,1)S(1)}, u32[]{:S(2)}, u32[]{:S(2)}) collective-permute-start(bf16[576,128]{1,0:T(8,128)(2,1)S(1)} %fusion.6.refs_0_), channel_id=1, source_target_pairs={{0,16},{1,17},{2,18},{3,19},{4,20},{5,21},{6,22},{7,23},{8,24},{9,... | collective-permute-start | bytes 442376 | tf_op jit(solution)/shard_map/ppermute | solution.py:863
  371.3 13.6 %collective-permute-start.41 = (bf16[576,128]{1,0:T(8,128)(2,1)S(1)}, bf16[576,128]{1,0:T(8,128)(2,1)S(1)}, u32[]{:S(2)}, u32[]{:S(2)}) collective-permute-start(bf16[576,128]{1,0:T(8,128)(2,1)S(1)} %collective-permute-done.39.refs_1_), channel_id=1, source_target_pairs={{0,16},{1,17},{2,18},{3,19},{4,20},{5,21},{6,22},{7,23},{8,24},{9,... | collective-permute-start | bytes 442376 | tf_op jit(solution)/shard_map/ppermute | solution.py:863
  372.9 12.0 %collective-permute-start.49 = (bf16[768,128]{1,0:T(8,128)(2,1)S(1)}, bf16[768,128]{1,0:T(8,128)(2,1)S(1)}, u32[]{:S(2)}, u32[]{:S(2)}) collective-permute-start(bf16[768,128]{1,0:T(8,128)(2,1)S(1)} %fusion.5.refs_4_), channel_id=1, source_target_pairs={{0,8},{1,9},{2,10},{3,11},{4,12},{5,13},{6,14},{7,15},{8,0},{9,1},... | collective-permute-start | bytes 589832 | tf_op jit(solution)/shard_map/ppermute | solution.py:863
  (59 other events, 566.8 us)
where the time goes:
time: 397 us; the launch traced here: 395 us
  Pallas kernels  190 us (48%)
  waiting for transfers between devices  109 us (27%)
  starting transfers between devices  63 us (16%)
  other arithmetic  16.9 us (4%)
  local copies, waits for them, and re-layouts  10.6 us (3%)
  between operations  5.22 us (1%)
    ppermute x65, waiting for transfers between devices, swap(): return lax.ppermute(value, both, pairs)  109 us
    pallas_call x2, Pallas kernels, feed(): pl.pallas_call(kernel, grid_spec=pltpu.PrefetchScalarGridSpec(num_scalar_...  63.9 us
    ppermute x65, starting transfers between devices, swap(): return lax.ppermute(value, both, pairs)  63 us
    pallas_call x1, Pallas kernels, attention(): pl.pallas_call(functools.partial(attention_kernel, rows=rows), grid=(pair...  41.5 us
    pallas_call x6, Pallas kernels, combine(): pl.pallas_call(functools.partial(combine_kernel, vectors=bool(vectors)),...  27.5 us
    pallas_call x1, Pallas kernels, inner_grads(): pl.pallas_call(inner_kernel, grid_spec=pltpu.PrefetchScalarGridSpec(num_s...  21.5 us
    pallas_call x1, Pallas kernels, qkv_forward(): pl.pallas_call(qkv_kernel, grid_spec=pltpu.PrefetchScalarGridSpec(num_sca...  12.3 us
  transfers between devices with their start and end apart: 65, of which 24 were waited for; matrix products, arithmetic and copies ran while one was open for 5% of the time, Pallas kernels for 46%

commit v1 on v0

--- a/solution.py
+++ b/solution.py
@@ -703,7 +703,7 @@
             out_specs=pl.BlockSpec((1, rows + extra, LANES), lambda i, s, co: (i, 0, 0)),
         ),
         out_shape=jax.ShapeDtypeStruct((4, rows + extra, LANES), bf16),
-        compiler_params=params(),
+        compiler_params=params(12),
         cost_estimate=pl.CostEstimate(
             flops=10**7, bytes_accessed=40 * rows * LANES, transcendentals=0
         ),
@@ -746,10 +746,11 @@
 
 def finish_kernel(co_ref, *refs):
     groups = refs[0:4], refs[4:8], refs[8:12]
-    gq_ref, go_ref, gu_ref, gd_ref, gv_ref = refs[12:17]
+    gq_ref, go_ref, gu_ref, gd_ref = refs[12:16]
+    vector_refs, row_ref = refs[16:-4], refs[-1]
     half = gq_ref.shape[0] // 2
     unit = LANES // 2
-    for group, parts, scr in zip(range(3), groups, refs[17:20]):
+    for group, parts, scr in zip(range(3), groups, refs[-4:-1]):
         for at, part in enumerate(parts):
             scr[((at // 2) ^ co_ref[2]) * 2 + ((at % 2) ^ co_ref[1])] = part[...]
         for y in range(2):
@@ -785,7 +786,15 @@
                     block = jnp.concatenate([scr[2 * y + x, at : at + unit, :] for y in range(2)], 0)
                     lanes = slice((3 * x + t) * LANES, (3 * x + t + 1) * LANES)
                     gd_ref[sub * LANES : (sub + 1) * LANES, lanes] = block.astype(f32).T
-    gv_ref[...] = scr[0, scr.shape[1] - gv_ref.shape[0] :, :].astype(f32)
+    rows = -(-row_ref.shape[1] // LANES // 16) * 16
+    sums = scr[0, scr.shape[1] - rows :, :].astype(f32)
+    for at in range(row_ref.shape[1] // LANES):
+        row_ref[:, at * LANES : (at + 1) * LANES] = sums[at : at + 1]
+    start = 0
+    for ref in vector_refs[:-1]:
+        ref[...] = row_ref[:, start : start + ref.shape[1]]
+        start += ref.shape[1]
+    vector_refs[-1][...] = vector_refs[-3][...]
 
 
 def finish(coords, groups, shapes):
@@ -798,10 +807,11 @@
             grid=(1,),
             in_specs=[whole(entry.shape) for entry in arrays],
             out_specs=[whole(s) for s in shapes],
-            scratch_shapes=[pltpu.VMEM((4,) + group[0].shape, bf16) for group in groups],
+            scratch_shapes=[pltpu.VMEM((4,) + group[0].shape, bf16) for group in groups]
+            + [pltpu.VMEM((1, sum(s[1] for s in shapes[4:-1])), f32)],
         ),
         out_shape=[jax.ShapeDtypeStruct(s, f32) for s in shapes],
-        compiler_params=params(),
+        compiler_params=params(24),
         name="finish",
     )(coords, *arrays)
 
@@ -965,6 +975,7 @@
     own = own_scales[0]
     scales = own_scales / total
     share = scales[0]
+    sizes = [ln1_gain.shape[0]] * 4 + [qkv_bias.shape[0], out_bias.shape[0], up_bias.shape[0]]
 
     if fast:
         finals, kepts = [], []
@@ -975,7 +986,8 @@
             kept = combine(scales, coords, 0, arrays, more)
             add = lambda at, *more: sum((e.astype(f32) for e in more), kept[at].astype(f32) + came[at])
             near = swap(add(slice(2, 4)).astype(bf16), 2)
-            last = swap(add(1, near[1]).astype(bf16), 4)
+            sent = add(1, near[1]).astype(bf16)
+            last = swap(sent, 4)
             line = add(0, near[0], last).astype(bf16)
             along_x, along_y = swap(line, 8), swap(line, 16)
             turn = (along_y, 8) if name == "b" else (along_x, 16)
@@ -983,15 +995,21 @@
         own_rows = width // fsdp
         hidden = up_b.shape[1]
         shapes = [(own_rows, 3 * width), (own_rows, width), (own_rows, hidden)]
-        shapes += [(hidden // fsdp, width), vectors[0].shape[1:]]
-        gq, go, gu, gd, own_row = finish(coords, finals, shapes)
-        own_row = own_row.reshape(-1)
+        shapes.append((hidden // fsdp, width))
+        shapes += [(1, size) for size in sizes + sizes[5:6]]
+        gq, go, gu, gd, *parts = finish(coords, finals, shapes)
+        parts = [entry.reshape(-1) for entry in parts]
     else:
         up_bias_grad = jnp.concatenate([ub_grad1, ub_grad2], 1).reshape(3, 8, LANES).swapaxes(0, 1)
         vector_grads = [ln_grads[i] for i in range(4)] + [qkv_bias_grad, cot_sum, up_bias_grad]
         vector_grads = jnp.concatenate([entry.reshape(fsdp, -1) for entry in vector_grads], 1)
         vector_grads = lax.psum(vector_grads * share, both)
         own_row = lax.dynamic_index_in_dim(vector_grads, lax.axis_index("fsdp"), 0, keepdims=False)
+        parts, start = [], 0
+        for size in sizes:
+            parts.append(own_row[start : start + size])
+            start += size
+        parts.append(parts[5])
 
         def plain(arrays):
             kept, sent, kept_other, sent_other = (
@@ -1021,13 +1039,8 @@
         )
 
     tokens_grad = (own * dx).astype(bf16)[None]
-    sizes = [ln1_gain.shape[0]] * 4 + [qkv_bias.shape[0], out_bias.shape[0], up_bias.shape[0]]
-    parts, start = [], 0
-    for size in sizes:
-        parts.append(own_row[start : start + size])
-        start += size
-    g1, b1, g2, b2, gqb, gob, gub = parts
-    return (mixed[None], tokens_grad, clip_scale, g1, b1, g2, b2, gq, gqb, go, gob, gu, gub, gd, gob)
+    g1, b1, g2, b2, gqb, gob, gub, gdb = parts
+    return (mixed[None], tokens_grad, clip_scale, g1, b1, g2, b2, gq, gqb, go, gob, gu, gub, gd, gdb)
 
 
 def solution(mesh):

time: 397 us -> 383 us (0.965)
  Pallas kernels: 190 us -> 174 us
  waiting for transfers between devices: 109 us -> 121 us
  other arithmetic: 16.9 us -> 12.5 us
    pallas_call x6, Pallas kernels: 27.5 us -> 13.6 us  [combine(): pl.pallas_call(functools.partial(combine_kernel, vectors=bool(vectors)),...]
    ppermute x65, waiting for transfers between devices: 109 us -> 121 us  [swap(): return lax.ppermute(value, both, pairs)]
    slice x3 -> x0, local copies, waits for them, and re-layouts: 3.99 us -> none  [body(): parts.append(own_row[start:start + size])]
  transfers between devices with their start and end apart: 65 -> 65, of which waited for: 24 -> 23; matrix products, arithmetic and copies ran while one was open for 5% -> 4% of each run, Pallas kernels for 46% -> 44%
where the time goes in v1:
time: 383 us; the launch traced here: 382 us
  Pallas kernels  174 us (45%)
  waiting for transfers between devices  121 us (32%)
  starting transfers between devices  62 us (16%)
  other arithmetic  12.5 us (3%)
  local copies, waits for them, and re-layouts  7.66 us (2%)
  between operations  5.18 us (1%)
    ppermute x65, waiting for transfers between devices, swap(): return lax.ppermute(value, both, pairs)  121 us
    pallas_call x2, Pallas kernels, feed(): pl.pallas_call(kernel, grid_spec=pltpu.PrefetchScalarGridSpec(num_scalar_...  63.8 us
    ppermute x65, starting transfers between devices, swap(): return lax.ppermute(value, both, pairs)  62 us
    pallas_call x1, Pallas kernels, attention(): pl.pallas_call(functools.partial(attention_kernel, rows=rows), grid=(pair...  41.5 us
    pallas_call x1, Pallas kernels, inner_grads(): pl.pallas_call(inner_kernel, grid_spec=pltpu.PrefetchScalarGridSpec(num_s...  21.6 us
    pallas_call x6, Pallas kernels, combine(): pl.pallas_call(functools.partial(combine_kernel, vectors=bool(vectors)),...  13.6 us
    pallas_call x1, Pallas kernels, qkv_forward(): pl.pallas_call(qkv_kernel, grid_spec=pltpu.PrefetchScalarGridSpec(num_sca...  12.3 us
  transfers between devices with their start and end apart: 65, of which 23 were waited for; matrix products, arithmetic and copies ran while one was open for 4% of the time, Pallas kernels for 44%

profile of v1, /device:TPU:0, one launch (start us, length us, event | category | flops | bytes accessed | tf_op | source)
XLA Modules:
  0.0 382.5 jit_solution(9416759562677014203)
XLA Ops:
  2.0 3.9 %cut.1 = (bf16[4,576,128]{2,1,0:T(8,128)(2,1)}, bf16[576,128]{1,0:T(8,128)(2,1)}, bf16[4,2,576,128]{3,2,1,0:T(8,128)(2,1)}, bf16[2,576,128]{2,1,0:T(8,128)(2,1)}) custom-call(s32[5]{0:T(128)} %stack.65.co_ref.refs_0_, bf16[96,2304]{1,0:T(8,128)(2,1)} %qkv_ref.1, bf16[96,768]{1,0:T(8,128)(2,1)} %out_ref.1, bf16[96,3072]{1,0:T(8,128)(2,1)} %up_ref.1, ...), custom_call_target="tpu_custom_call" | custom-call | tf_op jit(solution)/shard_map/cut/pallas_call | solution.py:163
  5.9 3.1 collective-permute-start.3
  8.9 2.6 collective-permute-start.4
  12.8 3.2 fusion.3
  18.1 8.0 %collective-permute-done.1 = bf16[8,1248]{1,0:T(8,128)(2,1)S(1)} collective-permute-done((bf16[8,1248]{1,0:T(8,128)(2,1)S(1)}, bf16[8,1248]{1,0:T(8,128)(2,1)S(1)}, u32[]{:S(2)}, u32[]{:S(2)}) %collective-permute-start.1) | collective-permute-done | bytes 20000 | tf_op jit(solution)/shard_map/ppermute | solution.py:873
  26.2 2.8 collective-permute-start.2
  30.9 2.8 collective-permute-start.15
  35.1 1.6 collective-permute-start.6
  36.7 1.5 collective-permute-start.7
  38.8 14.7 %collective-permute-done.15 = bf16[2,576,128]{2,1,0:T(8,128)(2,1)S(1)} collective-permute-done((bf16[2,576,128]{2,1,0:T(8,128)(2,1)S(1)}, bf16[2,576,128]{2,1,0:T(8,128)(2,1)S(1)}, u32[]{:S(2)}, u32[]{:S(2)}) %collective-permute-start.15) | collective-permute-done | bytes 294944 | tf_op jit(solution)/shard_map/ppermute | solution.py:873
  54.1 2.4 collective-permute-done.7.p3
  59.3 6.6 %prepare.1 = (bf16[1024,768]{1,0:T(8,128)(2,1)}, bf16[1024,768]{1,0:T(8,128)(2,1)}, bf16[768,1024]{1,0:T(8,128)(2,1)}, bf16[768,1024]{1,0:T(8,128)(2,1)}, bf16[1...) custom-call(s32[1]{0:T(128)S(6)} %copy.32.len_ref, bf16[1024,768]{1,0:T(8,128)(2,1)} %bitcast.79, ...), custom_call_target="tpu_custom_call" | custom-call | flops 15728640 | bytes 12582912 | tf_op jit(solution)/shard_map/prepare/pallas_call | solution.py:109
  70.7 12.3 %qkv_forward.1 = (bf16[1024,2304]{1,0:T(8,128)(2,1)}, bf16[768,2304]{1,0:T(8,128)(2,1)}, bf16[768,768]{1,0:T(8,128)(2,1)}) custom-call(s32[5]{0:T(128)} %stack.65.co_ref.refs_0_, bf16[1024,768]{1,0:T(8,128)(2,1)} %get-tuple-element.74.h1_ref, f32[1,2304]{1,0:T(1,128)} %reshape.400.b_ref, f32[1024,128]{1,0:T(8,128)} %get-tuple-element.131.c_ref, ...), custom_call_target="tpu_custom_call" | custom-call | flops 3623878656 | bytes 18874368 | tf_op jit(solution)/shard_map/qkv_forward/pallas_call | solution.py:241
  83.0 41.5 %attention.1 = (bf16[1024,768]{1,0:T(8,128)(2,1)}, bf16[1024,2304]{1,0:T(8,128)(2,1)}) custom-call(bf16[1024,2304]{1,0:T(8,128)(2,1)} %get-tuple-element.77.q_ref.k_ref.v_ref, bf16[1024,2304]{1,0:T(8,128)(2,1)} %get-tuple-element.77.q_ref.k_ref.v_ref, bf16[1024,2304]{1,0:T(8,128)(2,1)} %get-tuple-element.77.q_ref.k_ref.v_ref, ...), custom_call_target="tpu_custom_call" | custom-call | flops 30000001024 | bytes 20971520 | tf_op jit(solution)/shard_map/attention/pallas_call | solution.py:371
  125.6 21.6 %inner_grads.1 = (bf16[2,4,4,144,128]{4,3,2,1,0:T(8,128)(2,1)}, bf16[2,4,4,144,128]{4,3,2,1,0:T(8,128)(2,1)}, bf16[2,4,4,144,128]{4,3,2,1,0:T(8,128)(2,1)}, bf16...) custom-call(s32[5]{0:T(128)} %stack.65.co_ref.refs_0_, ...), custom_call_target="tpu_custom_call" | custom-call | flops 9663676416 | bytes 25165824 | tf_op jit(solution)/shard_map/inner_grads/pallas_call | solution.py:642
  147.2 1.6 collective-permute-start.34
  149.8 39.1 %feed.2 = (f32[1024,768]{1,0:T(8,128)}, bf16[2,4,768,128]{3,2,1,0:T(8,128)(2,1)}, bf16[2,4,768,128]{3,2,1,0:T(8,128)(2,1)}, bf16[2,4,768,128]{3,2,1,0:T(8,128)(2...) custom-call(s32[5]{0:T(128)} %stack.65.co_ref.refs_0_, ...), custom_call_target="tpu_custom_call" | custom-call | flops 19327352832 | bytes 25165824 | tf_op jit(solution)/shard_map/feed/pallas_call | solution.py:536
  188.9 24.6 %feed.3 = (bf16[1024,768]{1,0:T(8,128)(2,1)}, bf16[2,4,384,128]{3,2,1,0:T(8,128)(2,1)}, bf16[2,4,384,128]{3,2,1,0:T(8,128)(2,1)}, bf16[2,4,384,128]{3,2,1,0:T(8,...) custom-call(s32[5]{0:T(128)} %stack.65.co_ref.refs_0_, ...), custom_call_target="tpu_custom_call" | custom-call | flops 9663676416 | bytes 12582912 | tf_op jit(solution)/shard_map/feed/pallas_call | solution.py:536
  213.6 6.9 %norm_back.1 = (f32[1024,768]{1,0:T(8,128)}, f32[8,768]{1,0:T(8,128)}) custom-call(bf16[1024,768]{1,0:T(8,128)(2,1)} %bitcast.81, bf16[1024,768]{1,0:T(8,128)(2,1)} %get-tuple-element.71.cot_ref.refs_3_, f32[1024,768]{1,0:T(8,128)} %get-tuple-element.91.dh1_ref, f32[1024,768]{1,0:T(8,128)} %get-tuple-element.92.dh2_ref, f32[8,768]{1,0:T(8,128)} %concatenate.7.ln_ref), custom_call_target="tpu_custom_call" | custom-call | flops 23592960 | bytes 12582912 | tf_op jit(solution)/shard_map/norm_back/pallas_call | solution.py:844
  226.8 2.7 collective-permute-done.26
  230.7 11.8 %collective-permute-done.27 = f32[2,32]{1,0:T(2,128)S(1)} collective-permute-done((f32[2,32]{1,0:T(2,128)S(1)}, f32[2,32]{1,0:T(2,128)S(1)}, u32[]{:S(2)}, u32[]{:S(2)}) %collective-permute-start.27) | collective-permute-done | bytes 288 | tf_op jit(solution)/shard_map/ppermute | solution.py:873
  243.7 3.3 collective-permute-done.28
  247.1 3.7 collective-permute-start.29
  250.7 1.6 collective-permute-done.29
  252.3 3.4 collective-permute-start.30
  255.7 1.6 collective-permute-done.30
  257.3 2.4 collective-permute-start.31
  259.7 1.5 pack.1.refs_4_
  263.6 3.6 collective-permute-done.56.refs_5_
  274.2 18.3 %collective-permute-done.54 = bf16[2,4,384,128]{3,2,1,0:T(8,128)(2,1)} collective-permute-done((bf16[2,4,384,128]{3,2,1,0:T(8,128)(2,1)}, bf16[2,4,384,128]{3,2,1,0:T(8,128)(2,1)}, u32[]{:S(2)}, u32[]{:S(2)}) %collective-permute-start.54) | collective-permute-done | bytes 786464 | tf_op jit(solution)/shard_map/ppermute | solution.py:873
  293.6 4.0 %collective-permute-done.42.refs_1_ = bf16[2,4,768,128]{3,2,1,0:T(8,128)(2,1)S(1)} collective-permute-done((bf16[2,4,768,128]{3,2,1,0:T(8,128)(2,1)}, bf16[2,4,768,128]{3,2,1,0:T(8,128)(2,1)S(1)}, u32[]{:S(2)}, u32[]{:S(2)}) %collective-permute-start.42) | collective-permute-done | bytes 1572896 | tf_op jit(solution)/shard_map/ppermute | solution.py:873
  300.4 2.9 combine.7
  304.7 2.9 combine.9
  307.7 5.9 %collective-permute-done.58.refs_7_ = f32[8,16,128]{2,1,0:T(8,128)S(1)} collective-permute-done((f32[8,16,128]{2,1,0:T(8,128)S(1)}, f32[8,16,128]{2,1,0:T(8,128)S(1)}, u32[]{:S(2)}, u32[]{:S(2)}) %collective-permute-start.58) | collective-permute-done | bytes 65568 | tf_op jit(solution)/shard_map/ppermute | solution.py:873
  315.1 1.6 collective-permute-start.59
  316.7 2.9 combine.6
  320.7 9.2 %collective-permute-done.59 = bf16[4,400,128]{2,1,0:T(8,128)(2,1)S(1)} collective-permute-done((bf16[4,400,128]{2,1,0:T(8,128)(2,1)S(1)}, bf16[4,400,128]{2,1,0:T(8,128)(2,1)S(1)}, u32[]{:S(2)}, u32[]{:S(2)}) %collective-permute-start.59) | collective-permute-done | bytes 409632 | tf_op jit(solution)/shard_map/ppermute | solution.py:873
  330.1 2.9 combine.8
  333.2 2.1 collective-permute-start.47
  335.2 2.5 collective-permute-done.60
  338.4 2.5 collective-permute-start.38
  340.9 9.3 %collective-permute-done.47 = bf16[2,768,128]{2,1,0:T(8,128)(2,1)S(1)} collective-permute-done((bf16[2,768,128]{2,1,0:T(8,128)(2,1)S(1)}, bf16[2,768,128]{2,1,0:T(8,128)(2,1)S(1)}, u32[]{:S(2)}, u32[]{:S(2)}) %collective-permute-start.47) | collective-permute-done | bytes 393248 | tf_op jit(solution)/shard_map/ppermute | solution.py:873
  351.9 9.0 %collective-permute-done.48 = bf16[768,128]{1,0:T(8,128)(2,1)S(1)} collective-permute-done((bf16[768,128]{1,0:T(8,128)(2,1)S(1)}, bf16[768,128]{1,0:T(8,128)(2,1)S(1)}, u32[]{:S(2)}, u32[]{:S(2)}) %collective-permute-start.48) | collective-permute-done | bytes 196640 | tf_op jit(solution)/shard_map/ppermute | solution.py:873
  362.6 1.5 collective-permute-start.63
  364.6 1.5 collective-permute-start.41
  367.2 1.6 collective-permute-done.50.refs_6_
  372.3 6.3 %collective-permute-done.64.refs_11_ = bf16[400,128]{1,0:T(8,128)(2,1)S(1)} collective-permute-done((bf16[400,128]{1,0:T(8,128)(2,1)S(1)}, bf16[400,128]{1,0:T(8,128)(2,1)S(1)}, u32[]{:S(2)}, u32[]{:S(2)}) %collective-permute-start.64) | collective-permute-done | bytes 102432 | tf_op jit(solution)/shard_map/ppermute | solution.py:873
  378.6 2.7 finish.1
  (206 shorter events, 51.4 us)
Async XLA Ops:
  5.9 27.8 %collective-permute-start.3 = (bf16[576,128]{1,0:T(8,128)(2,1)}, bf16[576,128]{1,0:T(8,128)(2,1)S(1)}, u32[]{:S(2)}, u32[]{:S(2)}) collective-permute-start(bf16[576,128]{1,0:T(8,128)(2,1)} %get-tuple-element.76), channel_id=1, source_target_pairs={{0,2},{1,3},{2,0},{3,1},{4,6},{5,7},{6,4},{7,5},{8,10},{9,11},{10,... | collective-permute-start | bytes 442376 | tf_op jit(solution)/shard_map/ppermute | solution.py:873
  8.9 26.1 %collective-permute-start.4 = (bf16[576,128]{1,0:T(8,128)(2,1)}, bf16[576,128]{1,0:T(8,128)(2,1)S(1)}, u32[]{:S(2)}, u32[]{:S(2)}) collective-permute-start(bf16[576,128]{1,0:T(8,128)(2,1)} %get-tuple-element.76), channel_id=1, source_target_pairs={{0,4},{1,5},{2,6},{3,7},{4,0},{5,1},{6,2},{7,3},{8,12},{9,13},{10,... | collective-permute-start | bytes 442376 | tf_op jit(solution)/shard_map/ppermute | solution.py:873
  11.5 23.5 %collective-permute-start.5 = (bf16[576,128]{1,0:T(8,128)(2,1)}, bf16[576,128]{1,0:T(8,128)(2,1)S(1)}, u32[]{:S(2)}, u32[]{:S(2)}) collective-permute-start(bf16[576,128]{1,0:T(8,128)(2,1)} %get-tuple-element.76), channel_id=1, source_target_pairs={{0,6},{1,7},{2,4},{3,5},{4,2},{5,3},{6,0},{7,1},{8,14},{9,15},{10,... | collective-permute-start | bytes 442376 | tf_op jit(solution)/shard_map/ppermute | solution.py:873
  11.8 26.4 %collective-permute-start.14 = (bf16[2,576,128]{2,1,0:T(8,128)(2,1)}, bf16[2,576,128]{2,1,0:T(8,128)(2,1)S(1)}, u32[]{:S(2)}, u32[]{:S(2)}) collective-permute-start(bf16[2,576,128]{2,1,0:T(8,128)(2,1)} %get-tuple-element.84), channel_id=1, source_target_pairs={{0,2},{1,3},{2,0},{3,1},{4,6},{5,7},{6,4},{7,5},{8,10},{9,11},{10,... | collective-permute-start | bytes 884744 | tf_op jit(solution)/shard_map/ppermute | solution.py:873
  16.1 10.0 %collective-permute-start.1 = (bf16[8,1248]{1,0:T(8,128)(2,1)S(1)}, bf16[8,1248]{1,0:T(8,128)(2,1)S(1)}, u32[]{:S(2)}, u32[]{:S(2)}) collective-permute-start(bf16[8,1248]{1,0:T(8,128)(2,1)S(1)} %fusion.14), channel_id=1, source_target_pairs={{0,2},{1,3},{2,0},{3,1},{4,6},{5,7},{6,4},{7,5},{8,10},{9,11},{10,... | collective-permute-start | bytes 59912 | tf_op jit(solution)/shard_map/ppermute | solution.py:873
  30.9 22.6 %collective-permute-start.15 = (bf16[2,576,128]{2,1,0:T(8,128)(2,1)S(1)}, bf16[2,576,128]{2,1,0:T(8,128)(2,1)S(1)}, u32[]{:S(2)}, u32[]{:S(2)}) collective-permute-start(bf16[2,576,128]{2,1,0:T(8,128)(2,1)S(1)} %copy-done.25), channel_id=1, source_target_pairs={{0,4},{1,5},{2,6},{3,7},{4,0},{5,1},{6,2},{7,3},{8,12},{9,13},{10,... | collective-permute-start | bytes 884744 | tf_op jit(solution)/shard_map/ppermute | solution.py:873
  33.7 19.8 %collective-permute-start.16 = (bf16[2,576,128]{2,1,0:T(8,128)(2,1)S(1)}, bf16[2,576,128]{2,1,0:T(8,128)(2,1)S(1)}, u32[]{:S(2)}, u32[]{:S(2)}) collective-permute-start(bf16[2,576,128]{2,1,0:T(8,128)(2,1)S(1)} %copy-done.25), channel_id=1, source_target_pairs={{0,6},{1,7},{2,4},{3,5},{4,2},{5,3},{6,0},{7,1},{8,14},{9,15},{10,... | collective-permute-start | bytes 884744 | tf_op jit(solution)/shard_map/ppermute | solution.py:873
  35.1 18.8 %collective-permute-start.6 = (bf16[3,576,128]{2,1,0:T(8,128)(2,1)S(1)}, bf16[3,576,128]{2,1,0:T(8,128)(2,1)}, u32[]{:S(2)}, u32[]{:S(2)}) collective-permute-start(bf16[3,576,128]{2,1,0:T(8,128)(2,1)S(1)} %pad_maximum_fusion.1.p1), channel_id=1, source_target_pairs={{0,8},{1,9},{2,10},{3,11},{4,12},{5,13},{6,14},{7,15},{8,0},{9,1},... | collective-permute-start | bytes 1327112 | tf_op jit(solution)/shard_map/ppermute | solution.py:873
  36.7 19.7 %collective-permute-start.7 = (bf16[3,576,128]{2,1,0:T(8,128)(2,1)S(1)}, bf16[3,576,128]{2,1,0:T(8,128)(2,1)}, u32[]{:S(2)}, u32[]{:S(2)}) collective-permute-start(bf16[3,576,128]{2,1,0:T(8,128)(2,1)S(1)} %pad_maximum_fusion.1.p1), channel_id=1, source_target_pairs={{0,16},{1,17},{2,18},{3,19},{4,20},{5,21},{6,22},{7,23},{8,24},{9,... | collective-permute-start | bytes 1327112 | tf_op jit(solution)/shard_map/ppermute | solution.py:873
  38.2 18.2 %collective-permute-start.8 = (bf16[3,576,128]{2,1,0:T(8,128)(2,1)S(1)}, bf16[3,576,128]{2,1,0:T(8,128)(2,1)}, u32[]{:S(2)}, u32[]{:S(2)}) collective-permute-start(bf16[3,576,128]{2,1,0:T(8,128)(2,1)S(1)} %pad_maximum_fusion.1.p1), channel_id=1, source_target_pairs={{0,24},{1,25},{2,26},{3,27},{4,28},{5,29},{6,30},{7,31},{8,16},{9,... | collective-permute-start | bytes 1327112 | tf_op jit(solution)/shard_map/ppermute | solution.py:873
  53.5 13.8 %collective-permute-start.9 = (bf16[4,576,128]{2,1,0:T(8,128)(2,1)}, bf16[4,576,128]{2,1,0:T(8,128)(2,1)}, u32[]{:S(2)}, u32[]{:S(2)}) collective-permute-start(bf16[4,576,128]{2,1,0:T(8,128)(2,1)} %get-tuple-element.75.p0), channel_id=1, source_target_pairs={{0,1},{1,0},{2,3},{3,2},{4,5},{5,4},{6,7},{7,6},{8,9},{9,8},{10,11... | collective-permute-start | bytes 1769480 | tf_op jit(solution)/shard_map/ppermute | solution.py:873
  53.5 13.2 %collective-permute-start.10 = (bf16[3,576,128]{2,1,0:T(8,128)(2,1)S(1)}, bf16[3,576,128]{2,1,0:T(8,128)(2,1)}, u32[]{:S(2)}, u32[]{:S(2)}) collective-permute-start(bf16[3,576,128]{2,1,0:T(8,128)(2,1)S(1)} %pad_maximum_fusion.1.p1), channel_id=1, source_target_pairs={{0,1},{1,0},{2,3},{3,2},{4,5},{5,4},{6,7},{7,6},{8,9},{9,8},{10,11... | collective-permute-start | bytes 1327112 | tf_op jit(solution)/shard_map/ppermute | solution.py:873
  54.0 14.5 %collective-permute-start.11 = (bf16[3,576,128]{2,1,0:T(8,128)(2,1)}, bf16[3,576,128]{2,1,0:T(8,128)(2,1)}, u32[]{:S(2)}, u32[]{:S(2)}) collective-permute-start(bf16[3,576,128]{2,1,0:T(8,128)(2,1)} %collective-permute-done.6.p2), channel_id=1, source_target_pairs={{0,1},{1,0},{2,3},{3,2},{4,5},{5,4},{6,7},{7,6},{8,9},{9,8},{10,11... | collective-permute-start | bytes 1327112 | tf_op jit(solution)/shard_map/ppermute | solution.py:873
  56.4 12.9 %collective-permute-start.12 = (bf16[3,576,128]{2,1,0:T(8,128)(2,1)}, bf16[3,576,128]{2,1,0:T(8,128)(2,1)}, u32[]{:S(2)}, u32[]{:S(2)}) collective-permute-start(bf16[3,576,128]{2,1,0:T(8,128)(2,1)} %collective-permute-done.7.p3), channel_id=1, source_target_pairs={{0,1},{1,0},{2,3},{3,2},{4,5},{5,4},{6,7},{7,6},{8,9},{9,8},{10,11... | collective-permute-start | bytes 1327112 | tf_op jit(solution)/shard_map/ppermute | solution.py:873
  56.4 14.3 %collective-permute-start.13 = (bf16[3,576,128]{2,1,0:T(8,128)(2,1)}, bf16[3,576,128]{2,1,0:T(8,128)(2,1)}, u32[]{:S(2)}, u32[]{:S(2)}) collective-permute-start(bf16[3,576,128]{2,1,0:T(8,128)(2,1)} %collective-permute-done.8.p4), channel_id=1, source_target_pairs={{0,1},{1,0},{2,3},{3,2},{4,5},{5,4},{6,7},{7,6},{8,9},{9,8},{10,11... | collective-permute-start | bytes 1327112 | tf_op jit(solution)/shard_map/ppermute | solution.py:873
  67.2 81.5 %collective-permute-start.20 = (bf16[4,2,576,128]{3,2,1,0:T(8,128)(2,1)S(1)}, bf16[4,2,576,128]{3,2,1,0:T(8,128)(2,1)S(1)}, u32[]{:S(2)}, u32[]{:S(2)}) collective-permute-start(bf16[4,2,576,128]{3,2,1,0:T(8,128)(2,1)S(1)} %copy-done.23), channel_id=1, source_target_pairs={{0,1},{1,0},{2,3},{3,2},{4,5},{5,4},{6,7},{7,6},{8,9},{9,8},{10,11... | collective-permute-start | bytes 3538952 | tf_op jit(solution)/shard_map/ppermute | solution.py:873
  67.2 57.2 %collective-permute-start.17 = (bf16[3,2,576,128]{3,2,1,0:T(8,128)(2,1)S(1)}, bf16[3,2,576,128]{3,2,1,0:T(8,128)(2,1)}, u32[]{:S(2)}, u32[]{:S(2)}) collective-permute-start(bf16[3,2,576,128]{3,2,1,0:T(8,128)(2,1)S(1)} %pad_maximum_fusion.refs_18_.e1), channel_id=1, source_target_pairs={{0,8},{1,9},{2,10},{3,11},{4,12},{5,13},{6,14},{7,15},{8,0},{9,1},... | collective-permute-start | bytes 2654216 | tf_op jit(solution)/shard_map/ppermute | solution.py:873
  68.5 56.6 %collective-permute-start.18 = (bf16[3,2,576,128]{3,2,1,0:T(8,128)(2,1)S(1)}, bf16[3,2,576,128]{3,2,1,0:T(8,128)(2,1)}, u32[]{:S(2)}, u32[]{:S(2)}) collective-permute-start(bf16[3,2,576,128]{3,2,1,0:T(8,128)(2,1)S(1)} %pad_maximum_fusion.refs_18_.e1), channel_id=1, source_target_pairs={{0,16},{1,17},{2,18},{3,19},{4,20},{5,21},{6,22},{7,23},{8,24},{9,... | collective-permute-start | bytes 2654216 | tf_op jit(solution)/shard_map/ppermute | solution.py:873
  69.3 55.8 %collective-permute-start.19 = (bf16[3,2,576,128]{3,2,1,0:T(8,128)(2,1)S(1)}, bf16[3,2,576,128]{3,2,1,0:T(8,128)(2,1)}, u32[]{:S(2)}, u32[]{:S(2)}) collective-permute-start(bf16[3,2,576,128]{3,2,1,0:T(8,128)(2,1)S(1)} %pad_maximum_fusion.refs_18_.e1), channel_id=1, source_target_pairs={{0,24},{1,25},{2,26},{3,27},{4,28},{5,29},{6,30},{7,31},{8,16},{9,... | collective-permute-start | bytes 2654216 | tf_op jit(solution)/shard_map/ppermute | solution.py:873
  70.7 76.4 %collective-permute-start.21 = (bf16[3,2,576,128]{3,2,1,0:T(8,128)(2,1)S(1)}, bf16[3,2,576,128]{3,2,1,0:T(8,128)(2,1)}, u32[]{:S(2)}, u32[]{:S(2)}) collective-permute-start(bf16[3,2,576,128]{3,2,1,0:T(8,128)(2,1)S(1)} %pad_maximum_fusion.refs_18_.e1), channel_id=1, source_target_pairs={{0,1},{1,0},{2,3},{3,2},{4,5},{5,4},{6,7},{7,6},{8,9},{9,8},{10,11... | collective-permute-start | bytes 2654216 | tf_op jit(solution)/shard_map/ppermute | solution.py:873
  124.5 24.8 %collective-permute-start.22 = (bf16[3,2,576,128]{3,2,1,0:T(8,128)(2,1)}, bf16[3,2,576,128]{3,2,1,0:T(8,128)(2,1)}, u32[]{:S(2)}, u32[]{:S(2)}) collective-permute-start(bf16[3,2,576,128]{3,2,1,0:T(8,128)(2,1)} %collective-permute-done.17.refs_19_.e2), channel_id=1, source_target_pairs={{0,1},{1,0},{2,3},{3,2},{4,5},{5,4},{6,7},{7,6},{8,9},{9,8},{10,11... | collective-permute-start | bytes 2654216 | tf_op jit(solution)/shard_map/ppermute | solution.py:873
  125.0 24.3 %collective-permute-start.23 = (bf16[3,2,576,128]{3,2,1,0:T(8,128)(2,1)}, bf16[3,2,576,128]{3,2,1,0:T(8,128)(2,1)}, u32[]{:S(2)}, u32[]{:S(2)}) collective-permute-start(bf16[3,2,576,128]{3,2,1,0:T(8,128)(2,1)} %collective-permute-done.18.refs_20_.e3), channel_id=1, source_target_pairs={{0,1},{1,0},{2,3},{3,2},{4,5},{5,4},{6,7},{7,6},{8,9},{9,8},{10,11... | collective-permute-start | bytes 2654216 | tf_op jit(solution)/shard_map/ppermute | solution.py:873
  125.1 24.2 %collective-permute-start.24 = (bf16[3,2,576,128]{3,2,1,0:T(8,128)(2,1)}, bf16[3,2,576,128]{3,2,1,0:T(8,128)(2,1)}, u32[]{:S(2)}, u32[]{:S(2)}) collective-permute-start(bf16[3,2,576,128]{3,2,1,0:T(8,128)(2,1)} %collective-permute-done.19.refs_21_.e4), channel_id=1, source_target_pairs={{0,1},{1,0},{2,3},{3,2},{4,5},{5,4},{6,7},{7,6},{8,9},{9,8},{10,11... | collective-permute-start | bytes 2654216 | tf_op jit(solution)/shard_map/ppermute | solution.py:873
  147.2 122.4 %collective-permute-start.34 = (bf16[2,4,576,128]{3,2,1,0:T(8,128)(2,1)}, bf16[2,4,576,128]{3,2,1,0:T(8,128)(2,1)}, u32[]{:S(2)}, u32[]{:S(2)}) collective-permute-start(bf16[2,4,576,128]{3,2,1,0:T(8,128)(2,1)} %bitcast.97), channel_id=1, source_target_pairs={{0,16},{1,9},{2,18},{3,11},{4,20},{5,13},{6,22},{7,15},{8,24},{9,1... | collective-permute-start | bytes 3538952 | tf_op jit(solution)/shard_map/ppermute | solution.py:873
  148.8 120.8 %collective-permute-start.32 = (bf16[2,4,576,128]{3,2,1,0:T(8,128)(2,1)}, bf16[2,4,576,128]{3,2,1,0:T(8,128)(2,1)S(1)}, u32[]{:S(2)}, u32[]{:S(2)}) collective-permute-start(bf16[2,4,576,128]{3,2,1,0:T(8,128)(2,1)} %bitcast.96), channel_id=1, source_target_pairs={{0,8},{1,17},{2,10},{3,19},{4,12},{5,21},{6,14},{7,23},{8,0},{9,25... | collective-permute-start | bytes 3538952 | tf_op jit(solution)/shard_map/ppermute | solution.py:873
  221.8 50.5 %collective-permute-start.44 = (bf16[2,4,768,128]{3,2,1,0:T(8,128)(2,1)}, bf16[2,4,768,128]{3,2,1,0:T(8,128)(2,1)}, u32[]{:S(2)}, u32[]{:S(2)}) collective-permute-start(bf16[2,4,768,128]{3,2,1,0:T(8,128)(2,1)} %get-tuple-element.102), channel_id=1, source_target_pairs={{0,16},{1,9},{2,18},{3,11},{4,20},{5,13},{6,22},{7,15},{8,24},{9,1... | collective-permute-start | bytes 4718600 | tf_op jit(solution)/shard_map/ppermute | solution.py:873
  224.7 47.0 %collective-permute-start.33 = (bf16[2,4,576,128]{3,2,1,0:T(8,128)(2,1)}, bf16[2,4,576,128]{3,2,1,0:T(8,128)(2,1)}, u32[]{:S(2)}, u32[]{:S(2)}) collective-permute-start(bf16[2,4,576,128]{3,2,1,0:T(8,128)(2,1)} %bitcast.41), channel_id=1, source_target_pairs={{0,1},{1,0},{2,3},{3,2},{4,5},{5,4},{6,7},{7,6},{8,9},{9,8},{10,11... | collective-permute-start | bytes 3538952 | tf_op jit(solution)/shard_map/ppermute | solution.py:873
  229.5 13.1 %collective-permute-start.27 = (f32[2,32]{1,0:T(2,128)S(1)}, f32[2,32]{1,0:T(2,128)S(1)}, u32[]{:S(2)}, u32[]{:S(2)}) collective-permute-start(f32[2,32]{1,0:T(2,128)S(1)} %fusion.28), channel_id=1, source_target_pairs={{0,16},{1,17},{2,18},{3,19},{4,20},{5,21},{6,22},{7,23},{8,24},{9,... | collective-permute-start | bytes 776 | tf_op jit(solution)/shard_map/ppermute | solution.py:873
  268.6 29.1 %collective-permute-start.42 = (bf16[2,4,768,128]{3,2,1,0:T(8,128)(2,1)}, bf16[2,4,768,128]{3,2,1,0:T(8,128)(2,1)S(1)}, u32[]{:S(2)}, u32[]{:S(2)}) collective-permute-start(bf16[2,4,768,128]{3,2,1,0:T(8,128)(2,1)} %get-tuple-element.100), channel_id=1, source_target_pairs={{0,8},{1,17},{2,10},{3,19},{4,12},{5,21},{6,14},{7,23},{8,0},{9,25... | collective-permute-start | bytes 4718600 | tf_op jit(solution)/shard_map/ppermute | solution.py:873
  269.5 24.1 %collective-permute-start.35 = (bf16[2,4,576,128]{3,2,1,0:T(8,128)(2,1)}, bf16[2,4,576,128]{3,2,1,0:T(8,128)(2,1)}, u32[]{:S(2)}, u32[]{:S(2)}) collective-permute-start(bf16[2,4,576,128]{3,2,1,0:T(8,128)(2,1)} %collective-permute-done.34), channel_id=1, source_target_pairs={{0,1},{1,0},{2,3},{3,2},{4,5},{5,4},{6,7},{7,6},{8,9},{9,8},{10,11... | collective-permute-start | bytes 3538952 | tf_op jit(solution)/shard_map/ppermute | solution.py:873
  270.6 32.8 %collective-permute-start.43 = (bf16[2,4,768,128]{3,2,1,0:T(8,128)(2,1)}, bf16[2,4,768,128]{3,2,1,0:T(8,128)(2,1)S(1)}, u32[]{:S(2)}, u32[]{:S(2)}) collective-permute-start(bf16[2,4,768,128]{3,2,1,0:T(8,128)(2,1)} %get-tuple-element.101), channel_id=1, source_target_pairs={{0,1},{1,0},{2,3},{3,2},{4,5},{5,4},{6,7},{7,6},{8,9},{9,8},{10,11... | collective-permute-start | bytes 4718600 | tf_op jit(solution)/shard_map/ppermute | solution.py:873
  271.7 20.8 %collective-permute-start.54 = (bf16[2,4,384,128]{3,2,1,0:T(8,128)(2,1)}, bf16[2,4,384,128]{3,2,1,0:T(8,128)(2,1)}, u32[]{:S(2)}, u32[]{:S(2)}) collective-permute-start(bf16[2,4,384,128]{3,2,1,0:T(8,128)(2,1)} %get-tuple-element.106), channel_id=1, source_target_pairs={{0,16},{1,9},{2,18},{3,11},{4,20},{5,13},{6,22},{7,15},{8,24},{9,1... | collective-permute-start | bytes 2359304 | tf_op jit(solution)/shard_map/ppermute | solution.py:873
  272.3 31.7 %collective-permute-start.45 = (bf16[2,4,768,128]{3,2,1,0:T(8,128)(2,1)}, bf16[2,4,768,128]{3,2,1,0:T(8,128)(2,1)}, u32[]{:S(2)}, u32[]{:S(2)}) collective-permute-start(bf16[2,4,768,128]{3,2,1,0:T(8,128)(2,1)} %collective-permute-done.44), channel_id=1, source_target_pairs={{0,1},{1,0},{2,3},{3,2},{4,5},{5,4},{6,7},{7,6},{8,9},{9,8},{10,11... | collective-permute-start | bytes 4718600 | tf_op jit(solution)/shard_map/ppermute | solution.py:873
  292.5 21.6 %collective-permute-start.52 = (bf16[2,4,384,128]{3,2,1,0:T(8,128)(2,1)}, bf16[2,4,384,128]{3,2,1,0:T(8,128)(2,1)S(1)}, u32[]{:S(2)}, u32[]{:S(2)}) collective-permute-start(bf16[2,4,384,128]{3,2,1,0:T(8,128)(2,1)} %get-tuple-element.104), channel_id=1, source_target_pairs={{0,8},{1,17},{2,10},{3,19},{4,12},{5,21},{6,14},{7,23},{8,0},{9,25... | collective-permute-start | bytes 2359304 | tf_op jit(solution)/shard_map/ppermute | solution.py:873
  293.6 20.5 %collective-permute-start.53 = (bf16[2,4,384,128]{3,2,1,0:T(8,128)(2,1)}, bf16[2,4,384,128]{3,2,1,0:T(8,128)(2,1)S(1)}, u32[]{:S(2)}, u32[]{:S(2)}) collective-permute-start(bf16[2,4,384,128]{3,2,1,0:T(8,128)(2,1)} %get-tuple-element.105), channel_id=1, source_target_pairs={{0,1},{1,0},{2,3},{3,2},{4,5},{5,4},{6,7},{7,6},{8,9},{9,8},{10,11... | collective-permute-start | bytes 2359304 | tf_op jit(solution)/shard_map/ppermute | solution.py:873
  297.7 16.4 %collective-permute-start.55 = (bf16[2,4,384,128]{3,2,1,0:T(8,128)(2,1)}, bf16[2,4,384,128]{3,2,1,0:T(8,128)(2,1)S(1)}, u32[]{:S(2)}, u32[]{:S(2)}) collective-permute-start(bf16[2,4,384,128]{3,2,1,0:T(8,128)(2,1)} %collective-permute-done.54), channel_id=1, source_target_pairs={{0,1},{1,0},{2,3},{3,2},{4,5},{5,4},{6,7},{7,6},{8,9},{9,8},{10,11... | collective-permute-start | bytes 2359304 | tf_op jit(solution)/shard_map/ppermute | solution.py:873
  303.4 17.2 %collective-permute-start.36 = (bf16[4,576,128]{2,1,0:T(8,128)(2,1)S(1)}, bf16[4,576,128]{2,1,0:T(8,128)(2,1)S(1)}, u32[]{:S(2)}, u32[]{:S(2)}) collective-permute-start(bf16[4,576,128]{2,1,0:T(8,128)(2,1)S(1)} %combine.7), channel_id=1, source_target_pairs={{0,16},{1,9},{2,18},{3,11},{4,20},{5,13},{6,22},{7,15},{8,24},{9,1... | collective-permute-start | bytes 1769480 | tf_op jit(solution)/shard_map/ppermute | solution.py:873
  313.6 19.4 %collective-permute-start.46 = (bf16[4,768,128]{2,1,0:T(8,128)(2,1)S(1)}, bf16[4,768,128]{2,1,0:T(8,128)(2,1)S(1)}, u32[]{:S(2)}, u32[]{:S(2)}) collective-permute-start(bf16[4,768,128]{2,1,0:T(8,128)(2,1)S(1)} %combine.9), channel_id=1, source_target_pairs={{0,16},{1,9},{2,18},{3,11},{4,20},{5,13},{6,22},{7,15},{8,24},{9,1... | collective-permute-start | bytes 2359304 | tf_op jit(solution)/shard_map/ppermute | solution.py:873
  315.1 14.9 %collective-permute-start.59 = (bf16[4,400,128]{2,1,0:T(8,128)(2,1)S(1)}, bf16[4,400,128]{2,1,0:T(8,128)(2,1)S(1)}, u32[]{:S(2)}, u32[]{:S(2)}) collective-permute-start(bf16[4,400,128]{2,1,0:T(8,128)(2,1)S(1)} %combine.11), channel_id=1, source_target_pairs={{0,16},{1,9},{2,18},{3,11},{4,20},{5,13},{6,22},{7,15},{8,24},{9,1... | collective-permute-start | bytes 1228808 | tf_op jit(solution)/shard_map/ppermute | solution.py:873
  320.7 17.7 %collective-permute-start.37 = (bf16[2,576,128]{2,1,0:T(8,128)(2,1)S(1)}, bf16[2,576,128]{2,1,0:T(8,128)(2,1)S(1)}, u32[]{:S(2)}, u32[]{:S(2)}) collective-permute-start(bf16[2,576,128]{2,1,0:T(8,128)(2,1)S(1)} %add_convert_fusion.1), channel_id=1, source_target_pairs={{0,2},{1,3},{2,0},{3,1},{4,6},{5,7},{6,4},{7,5},{8,10},{9,11},{10,... | collective-permute-start | bytes 884744 | tf_op jit(solution)/shard_map/ppermute | solution.py:873
  333.2 17.1 %collective-permute-start.47 = (bf16[2,768,128]{2,1,0:T(8,128)(2,1)S(1)}, bf16[2,768,128]{2,1,0:T(8,128)(2,1)S(1)}, u32[]{:S(2)}, u32[]{:S(2)}) collective-permute-start(bf16[2,768,128]{2,1,0:T(8,128)(2,1)S(1)} %add_convert_fusion), channel_id=1, source_target_pairs={{0,2},{1,3},{2,0},{3,1},{4,6},{5,7},{6,4},{7,5},{8,10},{9,11},{10,... | collective-permute-start | bytes 1179656 | tf_op jit(solution)/shard_map/ppermute | solution.py:873
  337.8 23.7 %collective-permute-start.61 = (bf16[400,128]{1,0:T(8,128)(2,1)S(1)}, bf16[400,128]{1,0:T(8,128)(2,1)S(1)}, u32[]{:S(2)}, u32[]{:S(2)}) collective-permute-start(bf16[400,128]{1,0:T(8,128)(2,1)S(1)} %fusion.10), channel_id=1, source_target_pairs={{0,4},{1,5},{2,6},{3,7},{4,0},{5,1},{6,2},{7,3},{8,12},{9,13},{10,... | collective-permute-start | bytes 307208 | tf_op jit(solution)/shard_map/ppermute | solution.py:873
  338.4 12.4 %collective-permute-start.38 = (bf16[576,128]{1,0:T(8,128)(2,1)S(1)}, bf16[576,128]{1,0:T(8,128)(2,1)S(1)}, u32[]{:S(2)}, u32[]{:S(2)}) collective-permute-start(bf16[576,128]{1,0:T(8,128)(2,1)S(1)} %fusion.9), channel_id=1, source_target_pairs={{0,4},{1,5},{2,6},{3,7},{4,0},{5,1},{6,2},{7,3},{8,12},{9,13},{10,... | collective-permute-start | bytes 442376 | tf_op jit(solution)/shard_map/ppermute | solution.py:873
  350.4 10.5 %collective-permute-start.48 = (bf16[768,128]{1,0:T(8,128)(2,1)S(1)}, bf16[768,128]{1,0:T(8,128)(2,1)S(1)}, u32[]{:S(2)}, u32[]{:S(2)}) collective-permute-start(bf16[768,128]{1,0:T(8,128)(2,1)S(1)} %fusion.8), channel_id=1, source_target_pairs={{0,4},{1,5},{2,6},{3,7},{4,0},{5,1},{6,2},{7,3},{8,12},{9,13},{10,... | collective-permute-start | bytes 589832 | tf_op jit(solution)/shard_map/ppermute | solution.py:873
  350.9 13.7 %collective-permute-start.39 = (bf16[576,128]{1,0:T(8,128)(2,1)S(1)}, bf16[576,128]{1,0:T(8,128)(2,1)S(1)}, u32[]{:S(2)}, u32[]{:S(2)}) collective-permute-start(bf16[576,128]{1,0:T(8,128)(2,1)S(1)} %fusion.6.refs_0_), channel_id=1, source_target_pairs={{0,8},{1,9},{2,10},{3,11},{4,12},{5,13},{6,14},{7,15},{8,0},{9,1},... | collective-permute-start | bytes 442376 | tf_op jit(solution)/shard_map/ppermute | solution.py:873
  364.1 14.5 %collective-permute-start.40 = (bf16[576,128]{1,0:T(8,128)(2,1)S(1)}, bf16[576,128]{1,0:T(8,128)(2,1)S(1)}, u32[]{:S(2)}, u32[]{:S(2)}) collective-permute-start(bf16[576,128]{1,0:T(8,128)(2,1)S(1)} %fusion.6.refs_0_), channel_id=1, source_target_pairs={{0,16},{1,17},{2,18},{3,19},{4,20},{5,21},{6,22},{7,23},{8,24},{9,... | collective-permute-start | bytes 442376 | tf_op jit(solution)/shard_map/ppermute | solution.py:873
  364.6 14.0 %collective-permute-start.41 = (bf16[576,128]{1,0:T(8,128)(2,1)S(1)}, bf16[576,128]{1,0:T(8,128)(2,1)S(1)}, u32[]{:S(2)}, u32[]{:S(2)}) collective-permute-start(bf16[576,128]{1,0:T(8,128)(2,1)S(1)} %collective-permute-done.39.refs_1_), channel_id=1, source_target_pairs={{0,16},{1,17},{2,18},{3,19},{4,20},{5,21},{6,22},{7,23},{8,24},{9,... | collective-permute-start | bytes 442376 | tf_op jit(solution)/shard_map/ppermute | solution.py:873
  366.3 12.2 %collective-permute-start.49 = (bf16[768,128]{1,0:T(8,128)(2,1)S(1)}, bf16[768,128]{1,0:T(8,128)(2,1)S(1)}, u32[]{:S(2)}, u32[]{:S(2)}) collective-permute-start(bf16[768,128]{1,0:T(8,128)(2,1)S(1)} %fusion.5.refs_4_), channel_id=1, source_target_pairs={{0,8},{1,9},{2,10},{3,11},{4,12},{5,13},{6,14},{7,15},{8,0},{9,1},... | collective-permute-start | bytes 589832 | tf_op jit(solution)/shard_map/ppermute | solution.py:873
  (43 other events, 425.7 us)

commit v2 on v1

--- a/solution.py
+++ b/solution.py
@@ -123,14 +123,13 @@
     )(lengths, x, cot, ln)
 
 
-def cut_kernel(co_ref, qkv_ref, out_ref, up_ref, down_ref, in_ref, in0_ref, ff_ref, ff0_ref):
+def cut_inner_kernel(co_ref, qkv_ref, out_ref, in_ref, in0_ref):
     half = qkv_ref.shape[0] // 2
-    unit = LANES // 2
     for y in range(2):
         for x in range(2):
             at = (y ^ co_ref[2]) * 2 + (x ^ co_ref[1])
 
-            def fill(inner, feeds):
+            def fill(inner):
                 row = 0
                 for ref in (qkv_ref, out_ref):
                     tiles = ref.shape[1] // 2 // LANES
@@ -138,6 +137,19 @@
                         lanes = slice((x * tiles + t) * LANES, (x * tiles + t + 1) * LANES)
                         inner[row : row + half, :] = ref[y * half : (y + 1) * half, lanes]
                         row += half
+
+            fill(in_ref.at[at])
+            pl.when(at == 0)(lambda: fill(in0_ref))
+
+
+def cut_feed_kernel(co_ref, up_ref, down_ref, ff_ref, ff0_ref):
+    half = up_ref.shape[0] // 2
+    unit = LANES // 2
+    for y in range(2):
+        for x in range(2):
+            at = (y ^ co_ref[2]) * 2 + (x ^ co_ref[1])
+
+            def fill(feeds):
                 for sub in range(3):
                     for z in range(2):
                         for c in range(2):
@@ -152,26 +164,25 @@
                         lanes = slice((3 * x + t) * LANES, (3 * x + t + 1) * LANES)
                         feeds[1, row : row + unit, :] = down_ref[start : start + unit, lanes]
 
-            fill(in_ref.at[at], ff_ref.at[at])
-            pl.when(at == 0)(lambda: fill(in0_ref, ff0_ref))
-
-
-def cut(coords, qkv, out, up, down):
+            fill(ff_ref.at[at])
+            pl.when(at == 0)(lambda: fill(ff0_ref))
+
+
+def cut(kernel, coords, arrays, shape):
     whole = lambda s: pl.BlockSpec(s, lambda i, co: (0,) * len(s))
-    rows = qkv.shape[0] // 2 * ((qkv.shape[1] + out.shape[1]) // 2 // LANES)
-    shapes = [(4, rows, LANES), (rows, LANES), (4, 2, rows, LANES), (2, rows, LANES)]
+    shapes = [(4, *shape), shape]
     return pl.pallas_call(
-        cut_kernel,
+        kernel,
         grid_spec=pltpu.PrefetchScalarGridSpec(
             num_scalar_prefetch=1,
             grid=(1,),
-            in_specs=[whole(entry.shape) for entry in (qkv, out, up, down)],
-            out_specs=[whole(shape) for shape in shapes],
-        ),
-        out_shape=[jax.ShapeDtypeStruct(shape, bf16) for shape in shapes],
+            in_specs=[whole(entry.shape) for entry in arrays],
+            out_specs=[whole(entry) for entry in shapes],
+        ),
+        out_shape=[jax.ShapeDtypeStruct(entry, bf16) for entry in shapes],
         compiler_params=params(),
         name="cut",
-    )(coords, qkv, out, up, down)
+    )(coords, *arrays)
 
 
 def piece_of(parts, q, k):
@@ -893,7 +904,9 @@
     spot = [me & 1, (me >> 3) & 1, (me >> 4) & 1, (me >> 1) & 3] if fast else [0 * me] * 4
     coords = jnp.stack(spot + [lengths[0]]).astype(jnp.int32)
     if fast:
-        in_own, in_mine, ff_own, ff_mine = cut(coords, qkv_weight, out_weight, up_weight, down_weight)
+        rows = qkv_weight.shape[0] // 2 * ((qkv_weight.shape[1] + out_weight.shape[1]) // 2 // LANES)
+        in_own, in_mine = cut(cut_inner_kernel, coords, (qkv_weight, out_weight), (rows, LANES))
+        ff_own, ff_mine = cut(cut_feed_kernel, coords, (up_weight, down_weight), (2, rows, LANES))
         lines = []
         for piece in (in_mine, ff_mine):
             lines.append([swap(piece, 2 * k) for k in (1, 2, 3)])
@@ -952,9 +965,9 @@
         facts = facts + swap(facts, 1)
         packed = pack(ln_sums, qkv_bias_grad, cot_sum, ub_grad1, ub_grad2)
         vectors = [packed, swap(packed, 8, 16)]
+        facts = facts + swap(facts, 2) + swap(facts, 4) + swap(facts, 6)
+        vectors += [swap(packed, 1), swap(packed, 17, 9)]
         facts = facts + swap(facts, 8) + swap(facts, 16) + swap(facts, 24)
-        vectors += [swap(packed, 1), swap(packed, 17, 9)]
-        facts = facts + swap(facts, 2) + swap(facts, 4) + swap(facts, 6)
     else:
         facts = lax.psum(facts, both)
     norms, numbers = jnp.sqrt(facts[0]), facts[1].astype(jnp.int32)

time: 383 us -> 378 us (0.987)
  waiting for transfers between devices: 121 us -> 104 us
  local copies, waits for them, and re-layouts: 7.66 us -> 13.1 us
  starting transfers between devices: 62 us -> 66 us
    ppermute x65, waiting for transfers between devices: 121 us -> 104 us  [swap(): return lax.ppermute(value, both, pairs)]
    concatenate x1, local copies, waits for them, and re-layouts: 0.09 us -> 5.46 us  [body(): packed = jnp.concatenate(smalls)]
    ppermute x65, starting transfers between devices: 62 us -> 66 us  [swap(): return lax.ppermute(value, both, pairs)]
  transfers between devices with their start and end apart: 65 -> 65, of which waited for: 23 -> 23; matrix products, arithmetic and copies ran while one was open for 4% -> 5% of each run, Pallas kernels for 44% -> 45%
where the time goes in v2:
time: 378 us; the launch traced here: 377 us
  Pallas kernels  176 us (47%)
  waiting for transfers between devices  104 us (28%)
  starting transfers between devices  66 us (17%)
  local copies, waits for them, and re-layouts  13.1 us (3%)
  other arithmetic  12.5 us (3%)
  between operations  5 us (1%)
    ppermute x65, waiting for transfers between devices, swap(): return lax.ppermute(value, both, pairs)  104 us
    ppermute x65, starting transfers between devices, swap(): return lax.ppermute(value, both, pairs)  66 us
    pallas_call x2, Pallas kernels, feed(): pl.pallas_call(kernel, grid_spec=pltpu.PrefetchScalarGridSpec(num_scalar_...  63.9 us
    pallas_call x1, Pallas kernels, attention(): pl.pallas_call(functools.partial(attention_kernel, rows=rows), grid=(pair...  41.5 us
    pallas_call x1, Pallas kernels, inner_grads(): pl.pallas_call(inner_kernel, grid_spec=pltpu.PrefetchScalarGridSpec(num_s...  21.6 us
    pallas_call x6, Pallas kernels, combine(): pl.pallas_call(functools.partial(combine_kernel, vectors=bool(vectors)),...  13.6 us
    pallas_call x1, Pallas kernels, qkv_forward(): pl.pallas_call(qkv_kernel, grid_spec=pltpu.PrefetchScalarGridSpec(num_sca...  12.2 us
  transfers between devices with their start and end apart: 65, of which 23 were waited for; matrix products, arithmetic and copies ran while one was open for 5% of the time, Pallas kernels for 45%

profile of v2, /device:TPU:0, one launch (start us, length us, event | category | flops | bytes accessed | tf_op | source)
XLA Modules:
  0.0 376.6 jit_solution(15351492964614140024)
XLA Ops:
  1.9 2.7 cut.2
  4.6 3.1 collective-permute-start.3
  7.7 2.6 collective-permute-start.4
  10.3 5.5 %concatenate.6 = bf16[1248]{0:T(1024)(128)(2,1)S(1)} concatenate(bf16[96]{0:T(256)(128)(2,1)} %param.18, bf16[96]{0:T(256)(128)(2,1)} %param.19, bf16[96]{0:T(256)(128)(2,1)} %param.20, bf16[96]{0:T(256)(128)(2,1)} %param.21, bf16[288]{0:T(512)(128)(2,1)} %param.23, bf16[96]{0:T(256)(128)(2,1)} %param.25, bf16[384]{0:T(512)(128)(2,1)} %param.27, bf16[96]{0:T(256)(128)(2,1)} %param.29), dimensions={0} | concatenate | bytes 4992 | tf_op jit(solution)/shard_map/concatenate | solution.py:888
  15.8 3.3 cut.3
  20.0 3.2 fusion.3
  25.3 3.8 %collective-permute-done.1 = bf16[8,1248]{1,0:T(8,128)(2,1)S(1)} collective-permute-done((bf16[8,1248]{1,0:T(8,128)(2,1)S(1)}, bf16[8,1248]{1,0:T(8,128)(2,1)S(1)}, u32[]{:S(2)}, u32[]{:S(2)}) %collective-permute-start.1) | collective-permute-done | bytes 20000 | tf_op jit(solution)/shard_map/ppermute | solution.py:884
  29.2 2.7 collective-permute-start.2
  34.0 2.6 collective-permute-start.15
  37.9 1.6 collective-permute-start.6
  41.5 14.8 %collective-permute-done.15 = bf16[2,576,128]{2,1,0:T(8,128)(2,1)S(1)} collective-permute-done((bf16[2,576,128]{2,1,0:T(8,128)(2,1)S(1)}, bf16[2,576,128]{2,1,0:T(8,128)(2,1)S(1)}, u32[]{:S(2)}, u32[]{:S(2)}) %collective-permute-start.15) | collective-permute-done | bytes 294944 | tf_op jit(solution)/shard_map/ppermute | solution.py:884
  56.9 2.3 collective-permute-done.7.p3
  62.1 6.6 %prepare.1 = (bf16[1024,768]{1,0:T(8,128)(2,1)}, bf16[1024,768]{1,0:T(8,128)(2,1)}, bf16[768,1024]{1,0:T(8,128)(2,1)}, bf16[768,1024]{1,0:T(8,128)(2,1)}, bf16[1...) custom-call(s32[1]{0:T(128)S(6)} %copy.32.len_ref, bf16[1024,768]{1,0:T(8,128)(2,1)} %bitcast.79, ...), custom_call_target="tpu_custom_call" | custom-call | flops 15728640 | bytes 12582912 | tf_op jit(solution)/shard_map/prepare/pallas_call | solution.py:109
  73.5 12.2 %qkv_forward.1 = (bf16[1024,2304]{1,0:T(8,128)(2,1)}, bf16[768,2304]{1,0:T(8,128)(2,1)}, bf16[768,768]{1,0:T(8,128)(2,1)}) custom-call(s32[5]{0:T(128)} %stack.65.co_ref.refs_0_, bf16[1024,768]{1,0:T(8,128)(2,1)} %get-tuple-element.74.h1_ref, f32[1,2304]{1,0:T(1,128)} %reshape.400.b_ref, f32[1024,128]{1,0:T(8,128)} %get-tuple-element.131.c_ref, ...), custom_call_target="tpu_custom_call" | custom-call | flops 3623878656 | bytes 18874368 | tf_op jit(solution)/shard_map/qkv_forward/pallas_call | solution.py:252
  85.7 41.5 %attention.1 = (bf16[1024,768]{1,0:T(8,128)(2,1)}, bf16[1024,2304]{1,0:T(8,128)(2,1)}) custom-call(bf16[1024,2304]{1,0:T(8,128)(2,1)} %get-tuple-element.77.q_ref.k_ref.v_ref, bf16[1024,2304]{1,0:T(8,128)(2,1)} %get-tuple-element.77.q_ref.k_ref.v_ref, bf16[1024,2304]{1,0:T(8,128)(2,1)} %get-tuple-element.77.q_ref.k_ref.v_ref, ...), custom_call_target="tpu_custom_call" | custom-call | flops 30000001024 | bytes 20971520 | tf_op jit(solution)/shard_map/attention/pallas_call | solution.py:382
  128.3 21.6 %inner_grads.1 = (bf16[2,4,4,144,128]{4,3,2,1,0:T(8,128)(2,1)}, bf16[2,4,4,144,128]{4,3,2,1,0:T(8,128)(2,1)}, bf16[2,4,4,144,128]{4,3,2,1,0:T(8,128)(2,1)}, bf16...) custom-call(s32[5]{0:T(128)} %stack.65.co_ref.refs_0_, ...), custom_call_target="tpu_custom_call" | custom-call | flops 9663676416 | bytes 25165824 | tf_op jit(solution)/shard_map/inner_grads/pallas_call | solution.py:653
  149.9 1.6 collective-permute-start.34
  152.5 39.2 %feed.2 = (f32[1024,768]{1,0:T(8,128)}, bf16[2,4,768,128]{3,2,1,0:T(8,128)(2,1)}, bf16[2,4,768,128]{3,2,1,0:T(8,128)(2,1)}, bf16[2,4,768,128]{3,2,1,0:T(8,128)(2...) custom-call(s32[5]{0:T(128)} %stack.65.co_ref.refs_0_, ...), custom_call_target="tpu_custom_call" | custom-call | flops 19327352832 | bytes 25165824 | tf_op jit(solution)/shard_map/feed/pallas_call | solution.py:547
  191.8 24.6 %feed.3 = (bf16[1024,768]{1,0:T(8,128)(2,1)}, bf16[2,4,384,128]{3,2,1,0:T(8,128)(2,1)}, bf16[2,4,384,128]{3,2,1,0:T(8,128)(2,1)}, bf16[2,4,384,128]{3,2,1,0:T(8,...) custom-call(s32[5]{0:T(128)} %stack.65.co_ref.refs_0_, ...), custom_call_target="tpu_custom_call" | custom-call | flops 9663676416 | bytes 12582912 | tf_op jit(solution)/shard_map/feed/pallas_call | solution.py:547
  216.4 6.9 %norm_back.1 = (f32[1024,768]{1,0:T(8,128)}, f32[8,768]{1,0:T(8,128)}) custom-call(bf16[1024,768]{1,0:T(8,128)(2,1)} %bitcast.81, bf16[1024,768]{1,0:T(8,128)(2,1)} %get-tuple-element.71.cot_ref.refs_3_, f32[1024,768]{1,0:T(8,128)} %get-tuple-element.91.dh1_ref, f32[1024,768]{1,0:T(8,128)} %get-tuple-element.92.dh2_ref, f32[8,768]{1,0:T(8,128)} %concatenate.7.ln_ref), custom_call_target="tpu_custom_call" | custom-call | flops 23592960 | bytes 12582912 | tf_op jit(solution)/shard_map/norm_back/pallas_call | solution.py:855
  228.7 3.9 %collective-permute-start.26 = (f32[2,32]{1,0:T(2,128)S(1)}, f32[2,32]{1,0:T(2,128)S(1)}, u32[]{:S(2)}, u32[]{:S(2)}) collective-permute-start(f32[2,32]{1,0:T(2,128)S(1)} %fusion.28), channel_id=1, source_target_pairs={{0,2},{1,3},{2,0},{3,1},{4,6},{5,7},{6,4},{7,5},{8,10},{9,11},{10,... | collective-permute-start | bytes 776 | tf_op jit(solution)/shard_map/ppermute | solution.py:884
  232.7 1.6 collective-permute-done.26
  234.2 4.0 %collective-permute-start.27 = (f32[2,32]{1,0:T(2,128)S(1)}, f32[2,32]{1,0:T(2,128)S(1)}, u32[]{:S(2)}, u32[]{:S(2)}) collective-permute-start(f32[2,32]{1,0:T(2,128)S(1)} %fusion.28), channel_id=1, source_target_pairs={{0,4},{1,5},{2,6},{3,7},{4,0},{5,1},{6,2},{7,3},{8,12},{9,13},{10,... | collective-permute-start | bytes 776 | tf_op jit(solution)/shard_map/ppermute | solution.py:884
  238.2 1.6 collective-permute-done.27
  239.7 2.4 collective-permute-start.28
  242.1 3.0 collective-permute-done.28
  246.1 2.7 collective-permute-done.29
  250.3 2.1 collective-permute-done.30
  252.3 1.9 collective-permute-start.31
  257.7 3.6 collective-permute-done.56.refs_5_
  265.9 1.6 collective-permute-start.54
  269.0 17.7 %collective-permute-done.54 = bf16[2,4,384,128]{3,2,1,0:T(8,128)(2,1)} collective-permute-done((bf16[2,4,384,128]{3,2,1,0:T(8,128)(2,1)}, bf16[2,4,384,128]{3,2,1,0:T(8,128)(2,1)}, u32[]{:S(2)}, u32[]{:S(2)}) %collective-permute-start.54) | collective-permute-done | bytes 786464 | tf_op jit(solution)/shard_map/ppermute | solution.py:884
  287.8 4.0 %collective-permute-done.42.refs_1_ = bf16[2,4,768,128]{3,2,1,0:T(8,128)(2,1)S(1)} collective-permute-done((bf16[2,4,768,128]{3,2,1,0:T(8,128)(2,1)}, bf16[2,4,768,128]{3,2,1,0:T(8,128)(2,1)S(1)}, u32[]{:S(2)}, u32[]{:S(2)}) %collective-permute-start.42) | collective-permute-done | bytes 1572896 | tf_op jit(solution)/shard_map/ppermute | solution.py:884
  294.6 2.9 combine.7
  297.5 1.6 collective-permute-start.36
  299.9 2.9 combine.9
  302.8 4.9 %collective-permute-done.58.refs_7_ = f32[8,16,128]{2,1,0:T(8,128)S(1)} collective-permute-done((f32[8,16,128]{2,1,0:T(8,128)S(1)}, f32[8,16,128]{2,1,0:T(8,128)S(1)}, u32[]{:S(2)}, u32[]{:S(2)}) %collective-permute-start.58) | collective-permute-done | bytes 65568 | tf_op jit(solution)/shard_map/ppermute | solution.py:884
  310.9 2.9 combine.6
  315.0 9.1 %collective-permute-done.59 = bf16[4,400,128]{2,1,0:T(8,128)(2,1)S(1)} collective-permute-done((bf16[4,400,128]{2,1,0:T(8,128)(2,1)S(1)}, bf16[4,400,128]{2,1,0:T(8,128)(2,1)S(1)}, u32[]{:S(2)}, u32[]{:S(2)}) %collective-permute-start.59) | collective-permute-done | bytes 409632 | tf_op jit(solution)/shard_map/ppermute | solution.py:884
  324.2 2.9 combine.8
  327.3 2.1 collective-permute-start.47
  329.4 2.5 collective-permute-done.60
  332.5 2.5 collective-permute-start.38
  335.1 9.3 %collective-permute-done.47 = bf16[2,768,128]{2,1,0:T(8,128)(2,1)S(1)} collective-permute-done((bf16[2,768,128]{2,1,0:T(8,128)(2,1)S(1)}, bf16[2,768,128]{2,1,0:T(8,128)(2,1)S(1)}, u32[]{:S(2)}, u32[]{:S(2)}) %collective-permute-start.47) | collective-permute-done | bytes 393248 | tf_op jit(solution)/shard_map/ppermute | solution.py:884
  346.0 9.0 %collective-permute-done.48 = bf16[768,128]{1,0:T(8,128)(2,1)S(1)} collective-permute-done((bf16[768,128]{1,0:T(8,128)(2,1)S(1)}, bf16[768,128]{1,0:T(8,128)(2,1)S(1)}, u32[]{:S(2)}, u32[]{:S(2)}) %collective-permute-start.48) | collective-permute-done | bytes 196640 | tf_op jit(solution)/shard_map/ppermute | solution.py:884
  355.1 1.6 collective-permute-start.50
  367.4 5.3 %collective-permute-done.64.refs_11_ = bf16[400,128]{1,0:T(8,128)(2,1)S(1)} collective-permute-done((bf16[400,128]{1,0:T(8,128)(2,1)S(1)}, bf16[400,128]{1,0:T(8,128)(2,1)S(1)}, u32[]{:S(2)}, u32[]{:S(2)}) %collective-permute-start.64) | collective-permute-done | bytes 102432 | tf_op jit(solution)/shard_map/ppermute | solution.py:884
  372.7 2.7 finish.1
  (191 shorter events, 57.1 us)
Async XLA Ops:
  4.6 32.0 %collective-permute-start.3 = (bf16[576,128]{1,0:T(8,128)(2,1)}, bf16[576,128]{1,0:T(8,128)(2,1)S(1)}, u32[]{:S(2)}, u32[]{:S(2)}) collective-permute-start(bf16[576,128]{1,0:T(8,128)(2,1)} %get-tuple-element.76), channel_id=1, source_target_pairs={{0,2},{1,3},{2,0},{3,1},{4,6},{5,7},{6,4},{7,5},{8,10},{9,11},{10,... | collective-permute-start | bytes 442376 | tf_op jit(solution)/shard_map/ppermute | solution.py:884
  7.7 30.2 %collective-permute-start.4 = (bf16[576,128]{1,0:T(8,128)(2,1)}, bf16[576,128]{1,0:T(8,128)(2,1)S(1)}, u32[]{:S(2)}, u32[]{:S(2)}) collective-permute-start(bf16[576,128]{1,0:T(8,128)(2,1)} %get-tuple-element.76), channel_id=1, source_target_pairs={{0,4},{1,5},{2,6},{3,7},{4,0},{5,1},{6,2},{7,3},{8,12},{9,13},{10,... | collective-permute-start | bytes 442376 | tf_op jit(solution)/shard_map/ppermute | solution.py:884
  10.2 27.6 %collective-permute-start.5 = (bf16[576,128]{1,0:T(8,128)(2,1)}, bf16[576,128]{1,0:T(8,128)(2,1)S(1)}, u32[]{:S(2)}, u32[]{:S(2)}) collective-permute-start(bf16[576,128]{1,0:T(8,128)(2,1)} %get-tuple-element.76), channel_id=1, source_target_pairs={{0,6},{1,7},{2,4},{3,5},{4,2},{5,3},{6,0},{7,1},{8,14},{9,15},{10,... | collective-permute-start | bytes 442376 | tf_op jit(solution)/shard_map/ppermute | solution.py:884
  19.1 21.9 %collective-permute-start.14 = (bf16[2,576,128]{2,1,0:T(8,128)(2,1)}, bf16[2,576,128]{2,1,0:T(8,128)(2,1)S(1)}, u32[]{:S(2)}, u32[]{:S(2)}) collective-permute-start(bf16[2,576,128]{2,1,0:T(8,128)(2,1)} %get-tuple-element.84), channel_id=1, source_target_pairs={{0,2},{1,3},{2,0},{3,1},{4,6},{5,7},{6,4},{7,5},{8,10},{9,11},{10,... | collective-permute-start | bytes 884744 | tf_op jit(solution)/shard_map/ppermute | solution.py:884
  34.0 22.4 %collective-permute-start.15 = (bf16[2,576,128]{2,1,0:T(8,128)(2,1)S(1)}, bf16[2,576,128]{2,1,0:T(8,128)(2,1)S(1)}, u32[]{:S(2)}, u32[]{:S(2)}) collective-permute-start(bf16[2,576,128]{2,1,0:T(8,128)(2,1)S(1)} %copy-done.17), channel_id=1, source_target_pairs={{0,4},{1,5},{2,6},{3,7},{4,0},{5,1},{6,2},{7,3},{8,12},{9,13},{10,... | collective-permute-start | bytes 884744 | tf_op jit(solution)/shard_map/ppermute | solution.py:884
  36.6 19.7 %collective-permute-start.16 = (bf16[2,576,128]{2,1,0:T(8,128)(2,1)S(1)}, bf16[2,576,128]{2,1,0:T(8,128)(2,1)S(1)}, u32[]{:S(2)}, u32[]{:S(2)}) collective-permute-start(bf16[2,576,128]{2,1,0:T(8,128)(2,1)S(1)} %copy-done.17), channel_id=1, source_target_pairs={{0,6},{1,7},{2,4},{3,5},{4,2},{5,3},{6,0},{7,1},{8,14},{9,15},{10,... | collective-permute-start | bytes 884744 | tf_op jit(solution)/shard_map/ppermute | solution.py:884
  37.9 19.0 %collective-permute-start.6 = (bf16[3,576,128]{2,1,0:T(8,128)(2,1)S(1)}, bf16[3,576,128]{2,1,0:T(8,128)(2,1)}, u32[]{:S(2)}, u32[]{:S(2)}) collective-permute-start(bf16[3,576,128]{2,1,0:T(8,128)(2,1)S(1)} %pad_maximum_fusion.1.p1), channel_id=1, source_target_pairs={{0,8},{1,9},{2,10},{3,11},{4,12},{5,13},{6,14},{7,15},{8,0},{9,1},... | collective-permute-start | bytes 1327112 | tf_op jit(solution)/shard_map/ppermute | solution.py:884
  39.5 19.8 %collective-permute-start.7 = (bf16[3,576,128]{2,1,0:T(8,128)(2,1)S(1)}, bf16[3,576,128]{2,1,0:T(8,128)(2,1)}, u32[]{:S(2)}, u32[]{:S(2)}) collective-permute-start(bf16[3,576,128]{2,1,0:T(8,128)(2,1)S(1)} %pad_maximum_fusion.1.p1), channel_id=1, source_target_pairs={{0,16},{1,17},{2,18},{3,19},{4,20},{5,21},{6,22},{7,23},{8,24},{9,... | collective-permute-start | bytes 1327112 | tf_op jit(solution)/shard_map/ppermute | solution.py:884
  41.0 18.3 %collective-permute-start.8 = (bf16[3,576,128]{2,1,0:T(8,128)(2,1)S(1)}, bf16[3,576,128]{2,1,0:T(8,128)(2,1)}, u32[]{:S(2)}, u32[]{:S(2)}) collective-permute-start(bf16[3,576,128]{2,1,0:T(8,128)(2,1)S(1)} %pad_maximum_fusion.1.p1), channel_id=1, source_target_pairs={{0,24},{1,25},{2,26},{3,27},{4,28},{5,29},{6,30},{7,31},{8,16},{9,... | collective-permute-start | bytes 1327112 | tf_op jit(solution)/shard_map/ppermute | solution.py:884
  56.3 13.7 %collective-permute-start.9 = (bf16[4,576,128]{2,1,0:T(8,128)(2,1)}, bf16[4,576,128]{2,1,0:T(8,128)(2,1)}, u32[]{:S(2)}, u32[]{:S(2)}) collective-permute-start(bf16[4,576,128]{2,1,0:T(8,128)(2,1)} %get-tuple-element.75.p0), channel_id=1, source_target_pairs={{0,1},{1,0},{2,3},{3,2},{4,5},{5,4},{6,7},{7,6},{8,9},{9,8},{10,11... | collective-permute-start | bytes 1769480 | tf_op jit(solution)/shard_map/ppermute | solution.py:884
  56.3 13.1 %collective-permute-start.10 = (bf16[3,576,128]{2,1,0:T(8,128)(2,1)S(1)}, bf16[3,576,128]{2,1,0:T(8,128)(2,1)}, u32[]{:S(2)}, u32[]{:S(2)}) collective-permute-start(bf16[3,576,128]{2,1,0:T(8,128)(2,1)S(1)} %pad_maximum_fusion.1.p1), channel_id=1, source_target_pairs={{0,1},{1,0},{2,3},{3,2},{4,5},{5,4},{6,7},{7,6},{8,9},{9,8},{10,11... | collective-permute-start | bytes 1327112 | tf_op jit(solution)/shard_map/ppermute | solution.py:884
  56.9 14.4 %collective-permute-start.11 = (bf16[3,576,128]{2,1,0:T(8,128)(2,1)}, bf16[3,576,128]{2,1,0:T(8,128)(2,1)}, u32[]{:S(2)}, u32[]{:S(2)}) collective-permute-start(bf16[3,576,128]{2,1,0:T(8,128)(2,1)} %collective-permute-done.6.p2), channel_id=1, source_target_pairs={{0,1},{1,0},{2,3},{3,2},{4,5},{5,4},{6,7},{7,6},{8,9},{9,8},{10,11... | collective-permute-start | bytes 1327112 | tf_op jit(solution)/shard_map/ppermute | solution.py:884
  59.2 12.8 %collective-permute-start.12 = (bf16[3,576,128]{2,1,0:T(8,128)(2,1)}, bf16[3,576,128]{2,1,0:T(8,128)(2,1)}, u32[]{:S(2)}, u32[]{:S(2)}) collective-permute-start(bf16[3,576,128]{2,1,0:T(8,128)(2,1)} %collective-permute-done.7.p3), channel_id=1, source_target_pairs={{0,1},{1,0},{2,3},{3,2},{4,5},{5,4},{6,7},{7,6},{8,9},{9,8},{10,11... | collective-permute-start | bytes 1327112 | tf_op jit(solution)/shard_map/ppermute | solution.py:884
  59.3 14.3 %collective-permute-start.13 = (bf16[3,576,128]{2,1,0:T(8,128)(2,1)}, bf16[3,576,128]{2,1,0:T(8,128)(2,1)}, u32[]{:S(2)}, u32[]{:S(2)}) collective-permute-start(bf16[3,576,128]{2,1,0:T(8,128)(2,1)} %collective-permute-done.8.p4), channel_id=1, source_target_pairs={{0,1},{1,0},{2,3},{3,2},{4,5},{5,4},{6,7},{7,6},{8,9},{9,8},{10,11... | collective-permute-start | bytes 1327112 | tf_op jit(solution)/shard_map/ppermute | solution.py:884
  70.0 81.5 %collective-permute-start.20 = (bf16[4,2,576,128]{3,2,1,0:T(8,128)(2,1)S(1)}, bf16[4,2,576,128]{3,2,1,0:T(8,128)(2,1)S(1)}, u32[]{:S(2)}, u32[]{:S(2)}) collective-permute-start(bf16[4,2,576,128]{3,2,1,0:T(8,128)(2,1)S(1)} %copy-done.15), channel_id=1, source_target_pairs={{0,1},{1,0},{2,3},{3,2},{4,5},{5,4},{6,7},{7,6},{8,9},{9,8},{10,11... | collective-permute-start | bytes 3538952 | tf_op jit(solution)/shard_map/ppermute | solution.py:884
  70.0 57.2 %collective-permute-start.17 = (bf16[3,2,576,128]{3,2,1,0:T(8,128)(2,1)S(1)}, bf16[3,2,576,128]{3,2,1,0:T(8,128)(2,1)}, u32[]{:S(2)}, u32[]{:S(2)}) collective-permute-start(bf16[3,2,576,128]{3,2,1,0:T(8,128)(2,1)S(1)} %pad_maximum_fusion.refs_18_.e1), channel_id=1, source_target_pairs={{0,8},{1,9},{2,10},{3,11},{4,12},{5,13},{6,14},{7,15},{8,0},{9,1},... | collective-permute-start | bytes 2654216 | tf_op jit(solution)/shard_map/ppermute | solution.py:884
  71.3 56.5 %collective-permute-start.18 = (bf16[3,2,576,128]{3,2,1,0:T(8,128)(2,1)S(1)}, bf16[3,2,576,128]{3,2,1,0:T(8,128)(2,1)}, u32[]{:S(2)}, u32[]{:S(2)}) collective-permute-start(bf16[3,2,576,128]{3,2,1,0:T(8,128)(2,1)S(1)} %pad_maximum_fusion.refs_18_.e1), channel_id=1, source_target_pairs={{0,16},{1,17},{2,18},{3,19},{4,20},{5,21},{6,22},{7,23},{8,24},{9,... | collective-permute-start | bytes 2654216 | tf_op jit(solution)/shard_map/ppermute | solution.py:884
  72.1 55.8 %collective-permute-start.19 = (bf16[3,2,576,128]{3,2,1,0:T(8,128)(2,1)S(1)}, bf16[3,2,576,128]{3,2,1,0:T(8,128)(2,1)}, u32[]{:S(2)}, u32[]{:S(2)}) collective-permute-start(bf16[3,2,576,128]{3,2,1,0:T(8,128)(2,1)S(1)} %pad_maximum_fusion.refs_18_.e1), channel_id=1, source_target_pairs={{0,24},{1,25},{2,26},{3,27},{4,28},{5,29},{6,30},{7,31},{8,16},{9,... | collective-permute-start | bytes 2654216 | tf_op jit(solution)/shard_map/ppermute | solution.py:884
  73.5 76.3 %collective-permute-start.21 = (bf16[3,2,576,128]{3,2,1,0:T(8,128)(2,1)S(1)}, bf16[3,2,576,128]{3,2,1,0:T(8,128)(2,1)}, u32[]{:S(2)}, u32[]{:S(2)}) collective-permute-start(bf16[3,2,576,128]{3,2,1,0:T(8,128)(2,1)S(1)} %pad_maximum_fusion.refs_18_.e1), channel_id=1, source_target_pairs={{0,1},{1,0},{2,3},{3,2},{4,5},{5,4},{6,7},{7,6},{8,9},{9,8},{10,11... | collective-permute-start | bytes 2654216 | tf_op jit(solution)/shard_map/ppermute | solution.py:884
  127.2 24.8 %collective-permute-start.22 = (bf16[3,2,576,128]{3,2,1,0:T(8,128)(2,1)}, bf16[3,2,576,128]{3,2,1,0:T(8,128)(2,1)}, u32[]{:S(2)}, u32[]{:S(2)}) collective-permute-start(bf16[3,2,576,128]{3,2,1,0:T(8,128)(2,1)} %collective-permute-done.17.refs_19_.e2), channel_id=1, source_target_pairs={{0,1},{1,0},{2,3},{3,2},{4,5},{5,4},{6,7},{7,6},{8,9},{9,8},{10,11... | collective-permute-start | bytes 2654216 | tf_op jit(solution)/shard_map/ppermute | solution.py:884
  127.8 24.2 %collective-permute-start.23 = (bf16[3,2,576,128]{3,2,1,0:T(8,128)(2,1)}, bf16[3,2,576,128]{3,2,1,0:T(8,128)(2,1)}, u32[]{:S(2)}, u32[]{:S(2)}) collective-permute-start(bf16[3,2,576,128]{3,2,1,0:T(8,128)(2,1)} %collective-permute-done.18.refs_20_.e3), channel_id=1, source_target_pairs={{0,1},{1,0},{2,3},{3,2},{4,5},{5,4},{6,7},{7,6},{8,9},{9,8},{10,11... | collective-permute-start | bytes 2654216 | tf_op jit(solution)/shard_map/ppermute | solution.py:884
  127.9 24.2 %collective-permute-start.24 = (bf16[3,2,576,128]{3,2,1,0:T(8,128)(2,1)}, bf16[3,2,576,128]{3,2,1,0:T(8,128)(2,1)}, u32[]{:S(2)}, u32[]{:S(2)}) collective-permute-start(bf16[3,2,576,128]{3,2,1,0:T(8,128)(2,1)} %collective-permute-done.19.refs_21_.e4), channel_id=1, source_target_pairs={{0,1},{1,0},{2,3},{3,2},{4,5},{5,4},{6,7},{7,6},{8,9},{9,8},{10,11... | collective-permute-start | bytes 2654216 | tf_op jit(solution)/shard_map/ppermute | solution.py:884
  149.9 113.8 %collective-permute-start.34 = (bf16[2,4,576,128]{3,2,1,0:T(8,128)(2,1)}, bf16[2,4,576,128]{3,2,1,0:T(8,128)(2,1)}, u32[]{:S(2)}, u32[]{:S(2)}) collective-permute-start(bf16[2,4,576,128]{3,2,1,0:T(8,128)(2,1)} %bitcast.97), channel_id=1, source_target_pairs={{0,16},{1,9},{2,18},{3,11},{4,20},{5,13},{6,22},{7,15},{8,24},{9,1... | collective-permute-start | bytes 3538952 | tf_op jit(solution)/shard_map/ppermute | solution.py:884
  151.5 112.6 %collective-permute-start.32 = (bf16[2,4,576,128]{3,2,1,0:T(8,128)(2,1)}, bf16[2,4,576,128]{3,2,1,0:T(8,128)(2,1)S(1)}, u32[]{:S(2)}, u32[]{:S(2)}) collective-permute-start(bf16[2,4,576,128]{3,2,1,0:T(8,128)(2,1)} %bitcast.96), channel_id=1, source_target_pairs={{0,8},{1,17},{2,10},{3,19},{4,12},{5,21},{6,14},{7,23},{8,0},{9,25... | collective-permute-start | bytes 3538952 | tf_op jit(solution)/shard_map/ppermute | solution.py:884
  224.7 42.8 %collective-permute-start.44 = (bf16[2,4,768,128]{3,2,1,0:T(8,128)(2,1)}, bf16[2,4,768,128]{3,2,1,0:T(8,128)(2,1)}, u32[]{:S(2)}, u32[]{:S(2)}) collective-permute-start(bf16[2,4,768,128]{3,2,1,0:T(8,128)(2,1)} %get-tuple-element.102), channel_id=1, source_target_pairs={{0,16},{1,9},{2,18},{3,11},{4,20},{5,13},{6,22},{7,15},{8,24},{9,1... | collective-permute-start | bytes 4718600 | tf_op jit(solution)/shard_map/ppermute | solution.py:884
  227.5 38.4 %collective-permute-start.33 = (bf16[2,4,576,128]{3,2,1,0:T(8,128)(2,1)}, bf16[2,4,576,128]{3,2,1,0:T(8,128)(2,1)}, u32[]{:S(2)}, u32[]{:S(2)}) collective-permute-start(bf16[2,4,576,128]{3,2,1,0:T(8,128)(2,1)} %bitcast.41), channel_id=1, source_target_pairs={{0,1},{1,0},{2,3},{3,2},{4,5},{5,4},{6,7},{7,6},{8,9},{9,8},{10,11... | collective-permute-start | bytes 3538952 | tf_op jit(solution)/shard_map/ppermute | solution.py:884
  262.7 29.1 %collective-permute-start.42 = (bf16[2,4,768,128]{3,2,1,0:T(8,128)(2,1)}, bf16[2,4,768,128]{3,2,1,0:T(8,128)(2,1)S(1)}, u32[]{:S(2)}, u32[]{:S(2)}) collective-permute-start(bf16[2,4,768,128]{3,2,1,0:T(8,128)(2,1)} %get-tuple-element.100), channel_id=1, source_target_pairs={{0,8},{1,17},{2,10},{3,19},{4,12},{5,21},{6,14},{7,23},{8,0},{9,25... | collective-permute-start | bytes 4718600 | tf_op jit(solution)/shard_map/ppermute | solution.py:884
  263.7 24.1 %collective-permute-start.35 = (bf16[2,4,576,128]{3,2,1,0:T(8,128)(2,1)}, bf16[2,4,576,128]{3,2,1,0:T(8,128)(2,1)}, u32[]{:S(2)}, u32[]{:S(2)}) collective-permute-start(bf16[2,4,576,128]{3,2,1,0:T(8,128)(2,1)} %collective-permute-done.34), channel_id=1, source_target_pairs={{0,1},{1,0},{2,3},{3,2},{4,5},{5,4},{6,7},{7,6},{8,9},{9,8},{10,11... | collective-permute-start | bytes 3538952 | tf_op jit(solution)/shard_map/ppermute | solution.py:884
  265.2 32.4 %collective-permute-start.43 = (bf16[2,4,768,128]{3,2,1,0:T(8,128)(2,1)}, bf16[2,4,768,128]{3,2,1,0:T(8,128)(2,1)S(1)}, u32[]{:S(2)}, u32[]{:S(2)}) collective-permute-start(bf16[2,4,768,128]{3,2,1,0:T(8,128)(2,1)} %get-tuple-element.101), channel_id=1, source_target_pairs={{0,1},{1,0},{2,3},{3,2},{4,5},{5,4},{6,7},{7,6},{8,9},{9,8},{10,11... | collective-permute-start | bytes 4718600 | tf_op jit(solution)/shard_map/ppermute | solution.py:884
  265.9 20.8 %collective-permute-start.54 = (bf16[2,4,384,128]{3,2,1,0:T(8,128)(2,1)}, bf16[2,4,384,128]{3,2,1,0:T(8,128)(2,1)}, u32[]{:S(2)}, u32[]{:S(2)}) collective-permute-start(bf16[2,4,384,128]{3,2,1,0:T(8,128)(2,1)} %get-tuple-element.106), channel_id=1, source_target_pairs={{0,16},{1,9},{2,18},{3,11},{4,20},{5,13},{6,22},{7,15},{8,24},{9,1... | collective-permute-start | bytes 2359304 | tf_op jit(solution)/shard_map/ppermute | solution.py:884
  267.4 31.7 %collective-permute-start.45 = (bf16[2,4,768,128]{3,2,1,0:T(8,128)(2,1)}, bf16[2,4,768,128]{3,2,1,0:T(8,128)(2,1)}, u32[]{:S(2)}, u32[]{:S(2)}) collective-permute-start(bf16[2,4,768,128]{3,2,1,0:T(8,128)(2,1)} %collective-permute-done.44), channel_id=1, source_target_pairs={{0,1},{1,0},{2,3},{3,2},{4,5},{5,4},{6,7},{7,6},{8,9},{9,8},{10,11... | collective-permute-start | bytes 4718600 | tf_op jit(solution)/shard_map/ppermute | solution.py:884
  286.7 22.6 %collective-permute-start.52 = (bf16[2,4,384,128]{3,2,1,0:T(8,128)(2,1)}, bf16[2,4,384,128]{3,2,1,0:T(8,128)(2,1)S(1)}, u32[]{:S(2)}, u32[]{:S(2)}) collective-permute-start(bf16[2,4,384,128]{3,2,1,0:T(8,128)(2,1)} %get-tuple-element.104), channel_id=1, source_target_pairs={{0,8},{1,17},{2,10},{3,19},{4,12},{5,21},{6,14},{7,23},{8,0},{9,25... | collective-permute-start | bytes 2359304 | tf_op jit(solution)/shard_map/ppermute | solution.py:884
  287.8 21.5 %collective-permute-start.53 = (bf16[2,4,384,128]{3,2,1,0:T(8,128)(2,1)}, bf16[2,4,384,128]{3,2,1,0:T(8,128)(2,1)S(1)}, u32[]{:S(2)}, u32[]{:S(2)}) collective-permute-start(bf16[2,4,384,128]{3,2,1,0:T(8,128)(2,1)} %get-tuple-element.105), channel_id=1, source_target_pairs={{0,1},{1,0},{2,3},{3,2},{4,5},{5,4},{6,7},{7,6},{8,9},{9,8},{10,11... | collective-permute-start | bytes 2359304 | tf_op jit(solution)/shard_map/ppermute | solution.py:884
  291.8 17.4 %collective-permute-start.55 = (bf16[2,4,384,128]{3,2,1,0:T(8,128)(2,1)}, bf16[2,4,384,128]{3,2,1,0:T(8,128)(2,1)S(1)}, u32[]{:S(2)}, u32[]{:S(2)}) collective-permute-start(bf16[2,4,384,128]{3,2,1,0:T(8,128)(2,1)} %collective-permute-done.54), channel_id=1, source_target_pairs={{0,1},{1,0},{2,3},{3,2},{4,5},{5,4},{6,7},{7,6},{8,9},{9,8},{10,11... | collective-permute-start | bytes 2359304 | tf_op jit(solution)/shard_map/ppermute | solution.py:884
  297.5 17.3 %collective-permute-start.36 = (bf16[4,576,128]{2,1,0:T(8,128)(2,1)S(1)}, bf16[4,576,128]{2,1,0:T(8,128)(2,1)S(1)}, u32[]{:S(2)}, u32[]{:S(2)}) collective-permute-start(bf16[4,576,128]{2,1,0:T(8,128)(2,1)S(1)} %combine.7), channel_id=1, source_target_pairs={{0,16},{1,9},{2,18},{3,11},{4,20},{5,13},{6,22},{7,15},{8,24},{9,1... | collective-permute-start | bytes 1769480 | tf_op jit(solution)/shard_map/ppermute | solution.py:884
  299.1 8.6 %collective-permute-start.58 = (f32[8,16,128]{2,1,0:T(8,128)S(1)}, f32[8,16,128]{2,1,0:T(8,128)S(1)}, u32[]{:S(2)}, u32[]{:S(2)}) collective-permute-start(f32[8,16,128]{2,1,0:T(8,128)S(1)} %copy-done.7), channel_id=1, source_target_pairs={{0,17},{1,8},{2,19},{3,10},{4,21},{5,12},{6,23},{7,14},{8,25},{9,0... | collective-permute-start | bytes 196616 | tf_op jit(solution)/shard_map/ppermute | solution.py:884
  307.7 19.4 %collective-permute-start.46 = (bf16[4,768,128]{2,1,0:T(8,128)(2,1)S(1)}, bf16[4,768,128]{2,1,0:T(8,128)(2,1)S(1)}, u32[]{:S(2)}, u32[]{:S(2)}) collective-permute-start(bf16[4,768,128]{2,1,0:T(8,128)(2,1)S(1)} %combine.9), channel_id=1, source_target_pairs={{0,16},{1,9},{2,18},{3,11},{4,20},{5,13},{6,22},{7,15},{8,24},{9,1... | collective-permute-start | bytes 2359304 | tf_op jit(solution)/shard_map/ppermute | solution.py:884
  310.2 13.9 %collective-permute-start.59 = (bf16[4,400,128]{2,1,0:T(8,128)(2,1)S(1)}, bf16[4,400,128]{2,1,0:T(8,128)(2,1)S(1)}, u32[]{:S(2)}, u32[]{:S(2)}) collective-permute-start(bf16[4,400,128]{2,1,0:T(8,128)(2,1)S(1)} %combine.11), channel_id=1, source_target_pairs={{0,16},{1,9},{2,18},{3,11},{4,20},{5,13},{6,22},{7,15},{8,24},{9,1... | collective-permute-start | bytes 1228808 | tf_op jit(solution)/shard_map/ppermute | solution.py:884
  314.9 17.6 %collective-permute-start.37 = (bf16[2,576,128]{2,1,0:T(8,128)(2,1)S(1)}, bf16[2,576,128]{2,1,0:T(8,128)(2,1)S(1)}, u32[]{:S(2)}, u32[]{:S(2)}) collective-permute-start(bf16[2,576,128]{2,1,0:T(8,128)(2,1)S(1)} %add_convert_fusion.1), channel_id=1, source_target_pairs={{0,2},{1,3},{2,0},{3,1},{4,6},{5,7},{6,4},{7,5},{8,10},{9,11},{10,... | collective-permute-start | bytes 884744 | tf_op jit(solution)/shard_map/ppermute | solution.py:884
  327.3 17.1 %collective-permute-start.47 = (bf16[2,768,128]{2,1,0:T(8,128)(2,1)S(1)}, bf16[2,768,128]{2,1,0:T(8,128)(2,1)S(1)}, u32[]{:S(2)}, u32[]{:S(2)}) collective-permute-start(bf16[2,768,128]{2,1,0:T(8,128)(2,1)S(1)} %add_convert_fusion), channel_id=1, source_target_pairs={{0,2},{1,3},{2,0},{3,1},{4,6},{5,7},{6,4},{7,5},{8,10},{9,11},{10,... | collective-permute-start | bytes 1179656 | tf_op jit(solution)/shard_map/ppermute | solution.py:884
  331.9 24.7 %collective-permute-start.61 = (bf16[400,128]{1,0:T(8,128)(2,1)S(1)}, bf16[400,128]{1,0:T(8,128)(2,1)S(1)}, u32[]{:S(2)}, u32[]{:S(2)}) collective-permute-start(bf16[400,128]{1,0:T(8,128)(2,1)S(1)} %fusion.10), channel_id=1, source_target_pairs={{0,4},{1,5},{2,6},{3,7},{4,0},{5,1},{6,2},{7,3},{8,12},{9,13},{10,... | collective-permute-start | bytes 307208 | tf_op jit(solution)/shard_map/ppermute | solution.py:884
  332.5 12.4 %collective-permute-start.38 = (bf16[576,128]{1,0:T(8,128)(2,1)S(1)}, bf16[576,128]{1,0:T(8,128)(2,1)S(1)}, u32[]{:S(2)}, u32[]{:S(2)}) collective-permute-start(bf16[576,128]{1,0:T(8,128)(2,1)S(1)} %fusion.9), channel_id=1, source_target_pairs={{0,4},{1,5},{2,6},{3,7},{4,0},{5,1},{6,2},{7,3},{8,12},{9,13},{10,... | collective-permute-start | bytes 442376 | tf_op jit(solution)/shard_map/ppermute | solution.py:884
  344.5 10.5 %collective-permute-start.48 = (bf16[768,128]{1,0:T(8,128)(2,1)S(1)}, bf16[768,128]{1,0:T(8,128)(2,1)S(1)}, u32[]{:S(2)}, u32[]{:S(2)}) collective-permute-start(bf16[768,128]{1,0:T(8,128)(2,1)S(1)} %fusion.8), channel_id=1, source_target_pairs={{0,4},{1,5},{2,6},{3,7},{4,0},{5,1},{6,2},{7,3},{8,12},{9,13},{10,... | collective-permute-start | bytes 589832 | tf_op jit(solution)/shard_map/ppermute | solution.py:884
  345.0 14.7 %collective-permute-start.39 = (bf16[576,128]{1,0:T(8,128)(2,1)S(1)}, bf16[576,128]{1,0:T(8,128)(2,1)S(1)}, u32[]{:S(2)}, u32[]{:S(2)}) collective-permute-start(bf16[576,128]{1,0:T(8,128)(2,1)S(1)} %fusion.6.refs_0_), channel_id=1, source_target_pairs={{0,8},{1,9},{2,10},{3,11},{4,12},{5,13},{6,14},{7,15},{8,0},{9,1},... | collective-permute-start | bytes 442376 | tf_op jit(solution)/shard_map/ppermute | solution.py:884
  358.2 14.5 %collective-permute-start.40 = (bf16[576,128]{1,0:T(8,128)(2,1)S(1)}, bf16[576,128]{1,0:T(8,128)(2,1)S(1)}, u32[]{:S(2)}, u32[]{:S(2)}) collective-permute-start(bf16[576,128]{1,0:T(8,128)(2,1)S(1)} %fusion.6.refs_0_), channel_id=1, source_target_pairs={{0,16},{1,17},{2,18},{3,19},{4,20},{5,21},{6,22},{7,23},{8,24},{9,... | collective-permute-start | bytes 442376 | tf_op jit(solution)/shard_map/ppermute | solution.py:884
  359.8 12.9 %collective-permute-start.41 = (bf16[576,128]{1,0:T(8,128)(2,1)S(1)}, bf16[576,128]{1,0:T(8,128)(2,1)S(1)}, u32[]{:S(2)}, u32[]{:S(2)}) collective-permute-start(bf16[576,128]{1,0:T(8,128)(2,1)S(1)} %collective-permute-done.39.refs_1_), channel_id=1, source_target_pairs={{0,16},{1,17},{2,18},{3,19},{4,20},{5,21},{6,22},{7,23},{8,24},{9,... | collective-permute-start | bytes 442376 | tf_op jit(solution)/shard_map/ppermute | solution.py:884
  361.5 11.2 %collective-permute-start.49 = (bf16[768,128]{1,0:T(8,128)(2,1)S(1)}, bf16[768,128]{1,0:T(8,128)(2,1)S(1)}, u32[]{:S(2)}, u32[]{:S(2)}) collective-permute-start(bf16[768,128]{1,0:T(8,128)(2,1)S(1)} %fusion.5.refs_4_), channel_id=1, source_target_pairs={{0,8},{1,9},{2,10},{3,11},{4,12},{5,13},{6,14},{7,15},{8,0},{9,1},... | collective-permute-start | bytes 589832 | tf_op jit(solution)/shard_map/ppermute | solution.py:884
  362.9 9.8 %collective-permute-start.51 = (bf16[768,128]{1,0:T(8,128)(2,1)S(1)}, bf16[768,128]{1,0:T(8,128)(2,1)S(1)}, u32[]{:S(2)}, u32[]{:S(2)}) collective-permute-start(bf16[768,128]{1,0:T(8,128)(2,1)S(1)} %collective-permute-done.50.refs_6_), channel_id=1, source_target_pairs={{0,8},{1,9},{2,10},{3,11},{4,12},{5,13},{6,14},{7,15},{8,0},{9,1},... | collective-permute-start | bytes 589832 | tf_op jit(solution)/shard_map/ppermute | solution.py:884
  (35 other events, 312.8 us)
